TPU v7x, 512 devices: a whole 4x8x8 slice. The times are simulated.
512 devices in a mesh: field: 32 (over x, y_lo, core), slab: 16 (over y_hi, z).
Axes of the slice: x: 4, y: 8 (y_hi: 2, y_lo: 4; y = y_hi * 4 + y_lo), z: 8, core: 2. Of those that a mesh axis runs over, the one named last changes fastest.
Arguments:
- fields: float32 [32, 16, 64, 16, 128], P('field', None, 'slab'), may hold values from -6 to 6
- velocity: float32 [3, 64, 16, 128], P(None, 'slab'), may hold values from -0.15 to 0.15
- diffusivity: float32 [64, 16, 128], P('slab'), may hold values from 0.06 to 0.14
- noise: float32 [32, 4, 3], P('field'), may hold values from -0.8 to 0.8
- mix_rate: float32 [64, 16, 128], P('slab'), may hold values from 0.2 to 1
- evaporation: float32 [64, 16, 128], P('slab'), may hold values from 0.05 to 0.5
- rate_matrix: float32 [32, 16], replicated, may hold values from -1.5 to 1.5
- stoich: float32 [16, 32], replicated, may hold values from -1 to 1
- prefactor: float32 [32], replicated, may hold values from 0.05 to 0.5
Outputs:
- updated: float32 [32, 16, 64, 16, 128], P('field', None, 'slab')
All inputs are finite; a program needn't handle non-finite values.
Results may differ from a plain program's by a relative error of at most 0.000073.
Values sent between devices are 32-bit elements; how exact they have to be, the bound alone decides.
No kernel may reach another device: no remote copies, remote signals or barrier semaphores. Data moves between devices by JAX's collectives and lax.ppermute only.
A program may use at most 64 MiB of HBM per device.

v0:
```python
import jax
import jax.numpy as jnp
from jax import lax
from jax.sharding import Mesh
from jax.sharding import PartitionSpec as P

F = 32
SUBSTEPS = 4
FIELD = ("field_0", "field_1", "field_2")


def with_halo(cells, sides, width):
    for axis, dim in sides:
        count = lax.axis_size(axis)
        ends = count - 1
        head = lax.slice_in_dim(cells, 0, width, axis=dim)
        tail = lax.slice_in_dim(cells, cells.shape[dim] - width, cells.shape[dim], axis=dim)
        cells = jnp.concatenate(
            [
                lax.ppermute(tail, axis, [(i, (i + 1) % count) for i in range(ends)]),
                cells,
                lax.ppermute(head, axis, [((i + 1) % count, i) for i in range(ends)]),
            ],
            axis=dim,
        )
    return cells


def cut_along(array, dim, devices):
    shape = array.shape
    blocks = array.reshape(*shape[:dim], devices, shape[dim] // devices, *shape[dim + 1 :])
    return jnp.moveaxis(blocks, dim, 0)


def in_order(blocks, dim):
    blocks = jnp.moveaxis(blocks, 0, dim)
    shape = blocks.shape
    return blocks.reshape(*shape[:dim], shape[dim] * shape[dim + 1], *shape[dim + 2 :])


def moved_by_axis(blocks, axes, turns):
    shape = [lax.axis_size(a) for a in axes]
    blocks = blocks.reshape(*shape, *blocks.shape[1:])
    for k in turns:
        blocks = lax.all_to_all(blocks, axes[k], split_axis=k, concat_axis=k, tiled=True)
    return blocks.reshape(-1, *blocks.shape[len(axes) :])


def two_step_exchange(array, groups, turns, split_dim, concat_dim):
    devices = lax.axis_size(groups[0]) * lax.axis_size(groups[1])
    blocks = cut_along(array, split_dim, devices)
    return in_order(moved_by_axis(blocks, groups, turns), concat_dim)


def advance(padded, velocity, diffusivity, drifts):
    center = padded[:, :, 1:-1]
    x_ahead = padded[:, :, 2:]
    x_behind = padded[:, :, :-2]
    y_ahead = jnp.roll(center, -1, axis=4)
    y_behind = jnp.roll(center, 1, axis=4)
    z_ahead = jnp.roll(center, -1, axis=3)
    z_behind = jnp.roll(center, 1, axis=3)
    spread = x_ahead + x_behind + y_ahead + y_behind + z_ahead + z_behind - 6.0 * center
    stir_scale = jnp.sqrt(2.0 * diffusivity)
    drift_x = velocity[0] - stir_scale * drifts[:, 0][:, None, None, None, None]
    drift_y = velocity[1] - stir_scale * drifts[:, 1][:, None, None, None, None]
    drift_z = velocity[2] - stir_scale * drifts[:, 2][:, None, None, None, None]
    carried = (
        drift_x * (x_ahead - x_behind) * 0.5
        + drift_y * (y_ahead - y_behind) * 0.5
        + drift_z * (z_ahead - z_behind) * 0.5
    )
    return center + diffusivity * spread - carried


def react(states, average, rates, vapour, rate_matrix, stoich, prefactor):
    species = states.shape[1]
    fuel = (jnp.arange(species) == 0).astype(jnp.float32)
    mixed = states - 0.5 * rates * (states - average) + vapour * fuel[:, None]
    drive = jnp.einsum("rs,ksc->krc", rate_matrix, mixed, precision=lax.Precision.HIGHEST)
    speed = prefactor[None, :, None] * jnp.exp(2.0 * jnp.tanh(drive))
    return mixed + jnp.einsum("sr,krc->ksc", stoich, speed, precision=lax.Precision.HIGHEST)


def per_device(
    fields, velocity, diffusivity, noise, mix_rate, evaporation, rate_matrix, stoich, prefactor
):
    state = with_halo(fields, (("slab", 2),), SUBSTEPS)
    coefficients = jnp.concatenate([velocity, diffusivity[None]], 0)
    coeff_ext = with_halo(coefficients, (("slab", 1),), SUBSTEPS - 1)
    slab_cells = fields.shape[2]
    domain_cells = slab_cells * lax.axis_size("slab")
    first_cell = lax.axis_index("slab") * slab_cells
    for substep in range(SUBSTEPS):
        reach = SUBSTEPS - substep - 1
        extent = slab_cells + 2 * reach
        coeff_window = coeff_ext[:, substep : substep + extent]
        state = advance(state, coeff_window[:3], coeff_window[3], noise[:, substep])
        positions = first_cell - reach + jnp.arange(extent, dtype=jnp.int32)
        inside = ((positions >= 0) & (positions < domain_cells)).astype(jnp.float32)
        state = state * inside[:, None, None]
    count_fields = state.shape[0]
    species = state.shape[1]
    flattened = state.reshape(count_fields, species, -1)
    gathered = two_step_exchange(flattened, (("field_0", "field_1"), "field_2"), (1, 0), 2, 0)
    block_cells = gathered.shape[2]
    first_slot = lax.axis_index(FIELD) * block_cells
    local_rates = lax.dynamic_slice_in_dim(mix_rate.reshape(-1), first_slot, block_cells)
    local_vapour = lax.dynamic_slice_in_dim(evaporation.reshape(-1), first_slot, block_cells)
    average = jnp.sum(gathered, axis=0) / F
    reacted = react(gathered, average, local_rates, local_vapour, rate_matrix, stoich, prefactor)
    returned = lax.all_to_all(reacted, FIELD, split_axis=0, concat_axis=2, tiled=True)
    return returned.reshape(state.shape)


def solution(mesh):
    split = Mesh(
        mesh.devices.reshape(4, 4, 2, mesh.shape["slab"]), ("field_0", "field_1", "field_2", "slab")
    )
    return jax.shard_map(
        per_device,
        mesh=split,
        in_specs=(
            P(FIELD, None, "slab", None, None),
            P(None, "slab", None, None),
            P("slab", None, None),
            P(FIELD, None, None),
            P("slab", None, None),
            P("slab", None, None),
            P(),
            P(),
            P(),
        ),
        out_specs=P(FIELD, None, "slab", None, None),
        check_vma=False,
    )
```

profile of v0, /device:TPU:57, one launch (start us, length us, event | category | flops | bytes accessed | tf_op | source)
XLA Modules:
  0.0 108.7 jit_solution(16660476904028493765)
XLA Ops:
  0.0 0.0 copy-start
  0.0 4.1 %collective-permute-start = (f32[1,16,4,16,128]{4,3,2,1,0:T(8,128)}, f32[1,16,4,16,128]{4,3,2,1,0:T(8,128)S(1)}, u32[]{:S(2)}, u32[]{:S(2)}) collective-permute-start(f32[1,16,4,16,128]{4,3,2,1,0:T(8,128)} %param.9), channel_id=1, source_target_pairs={{0,1},{1,2},{2,3},{3,4},{4,5},{5,6},{6,7},{7,8},{8,9},{9,10},{10,1... | collective-permute-start | bytes 1572872 | tf_op jit(solution)/shard_map/ppermute | solution.py:20
  4.1 10.8 %collective-permute-start.1 = (f32[1,16,4,16,128]{4,3,2,1,0:T(8,128)}, f32[1,16,4,16,128]{4,3,2,1,0:T(8,128)S(1)}, u32[]{:S(2)}, u32[]{:S(2)}) collective-permute-start(f32[1,16,4,16,128]{4,3,2,1,0:T(8,128)} %param.9), channel_id=1, source_target_pairs={{1,0},{2,1},{3,2},{4,3},{5,4},{6,5},{7,6},{8,7},{9,8},{10,9},{11,1... | collective-permute-start | bytes 1572872 | tf_op jit(solution)/shard_map/ppermute | solution.py:22
  15.0 1.0 fusion.7
  16.0 1.9 %collective-permute-start.2 = (f32[4,3,16,128]{3,2,1,0:T(8,128)S(1)}, f32[4,3,16,128]{3,2,1,0:T(8,128)S(1)}, u32[]{:S(2)}, u32[]{:S(2)}) collective-permute-start(f32[4,3,16,128]{3,2,1,0:T(8,128)S(1)} %get-tuple-element.53), channel_id=1, source_target_pairs={{0,1},{1,2},{2,3},{3,4},{4,5},{5,6},{6,7},{7,8},{8,9},{9,10},{10,1... | collective-permute-start | bytes 294920 | tf_op jit(solution)/shard_map/ppermute | solution.py:20
  17.9 9.4 %collective-permute-start.3 = (f32[4,3,16,128]{3,2,1,0:T(8,128)S(1)}, f32[4,3,16,128]{3,2,1,0:T(8,128)S(1)}, u32[]{:S(2)}, u32[]{:S(2)}) collective-permute-start(f32[4,3,16,128]{3,2,1,0:T(8,128)S(1)} %get-tuple-element.54), channel_id=1, source_target_pairs={{1,0},{2,1},{3,2},{4,3},{5,4},{6,5},{7,6},{8,7},{9,8},{10,9},{11,1... | collective-permute-start | bytes 294920 | tf_op jit(solution)/shard_map/ppermute | solution.py:22
  27.3 1.0 slice_reduce_fusion
  28.3 0.7 fusion.38
  29.0 0.7 fusion.37
  29.6 0.7 fusion.36
  30.3 0.7 fusion.35
  31.0 2.7 %bitcast_subtract_fusion.4 = (f32[4,16,128]{2,1,0:T(8,128)S(1)}, f32[4,16,128]{2,1,0:T(8,128)S(1)}, f32[4,16,128]{2,1,0:T(8,128)S(1)}) fusion(f32[3,4,16,128]{3,2,1,0:T(8,128)} %param.10, f32[4,16,128]{2,1,0:T(8,128)} %param.11, f32[]{:T(128)} %bitcast.23, f32[]{:T(128)} %bitcast.27, f32[]{:T(128)} %bitcast.25), kind=kLoop, calls=%fused_computation.62 | loop fusion | flops 57344 | bytes 229388 | tf_op jit(solution)/shard_map/sub | solution.py:65
  33.7 0.0 collective-permute-done.2
  33.7 0.0 collective-permute-done.3
  33.7 0.9 pad_maximum_fusion.16
  34.6 0.0 copy-start.2
  34.7 2.0 %fusion.13 = (f32[8,16,128]{2,1,0:T(8,128)S(1)}, f32[8,16,128]{2,1,0:T(8,128)S(1)}, f32[8,16,128]{2,1,0:T(8,128)S(1)}) fusion(f32[4,10,16,128]{3,2,1,0:T(8,128)S(1)} %pad_maximum_fusion.16, f32[]{:T(128)} %bitcast.10, f32[]{:T(128)} %bitcast.14, f32[]{:T(128)} %bitcast.12), kind=kLoop, calls=%fused_computation.49 | loop fusion | flops 114688 | bytes 458764 | tf_op jit(solution)/shard_map/sub | solution.py:65
  36.6 2.0 %fusion.16 = (f32[6,16,128]{2,1,0:T(8,128)S(1)}, f32[6,16,128]{2,1,0:T(8,128)S(1)}, f32[6,16,128]{2,1,0:T(8,128)S(1)}) fusion(f32[4,10,16,128]{3,2,1,0:T(8,128)S(1)} %pad_maximum_fusion.16, f32[]{:T(128)} %bitcast.17, f32[]{:T(128)} %bitcast.21, f32[]{:T(128)} %bitcast.19), kind=kLoop, calls=%fused_computation.57 | loop fusion | flops 86016 | bytes 344076 | tf_op jit(solution)/shard_map/sub | solution.py:65
  38.7 1.9 %fusion.10 = (f32[10,16,128]{2,1,0:T(8,128)S(1)}, f32[10,16,128]{2,1,0:T(8,128)S(1)}, f32[10,16,128]{2,1,0:T(8,128)S(1)}) fusion(f32[4,10,16,128]{3,2,1,0:T(8,128)S(1)} %pad_maximum_fusion.16, f32[]{:T(128)} %bitcast.3, f32[]{:T(128)} %bitcast.7, f32[]{:T(128)} %bitcast.5), kind=kLoop, calls=%fused_computation.41 | loop fusion | flops 143360 | bytes 573452 | tf_op jit(solution)/shard_map/sub | solution.py:65
  40.6 0.0 collective-permute-done
  40.7 0.0 copy-done.2
  40.7 0.0 collective-permute-done.1
  40.8 0.4 fusion.19
  41.2 0.4 fusion.20
  41.7 0.3 fusion.21
  42.0 0.1 fusion.22
  42.1 1.9 %subtract_multiply_fusion = f32[1,16,10,16,128]{4,3,2,1,0:T(8,128)S(1)} fusion(f32[1,16,12,16,128]{4,3,2,1,0:T(8,128)S(1)} %constant_dynamic-update-slice_fusion, f32[1,16,10,15,128]{4,3,2,1,0:T(8,128)S(1)} %get-tuple-element.14, f32[1,16,10,1,128]{4,3,2,1,0:T(1,128)S(1)} %get-tuple-element.16, f32[1,16,10,1,128]{4,3,2,1,0:T(1,128)S(1)} %get-tuple-element.15, ...), kind=kLoop, calls=%fused_computation.9 | loop fusion | flops 7864320 | bytes 10813480 | tf_op jit(solution)/shard_map/mul | solution.py:101
  44.0 0.4 fusion.23
  44.4 0.4 fusion.24
  44.7 0.2 fusion.25
  45.0 0.1 fusion.26
  45.1 1.3 %subtract_multiply_fusion.1 = f32[1,16,8,16,128]{4,3,2,1,0:T(8,128)S(1)} fusion(f32[1,16,10,16,128]{4,3,2,1,0:T(8,128)S(1)} %subtract_multiply_fusion, f32[1,16,8,15,128]{4,3,2,1,0:T(8,128)S(1)} %get-tuple-element.22, f32[1,16,8,1,128]{4,3,2,1,0:T(1,128)S(1)} %get-tuple-element.24, f32[1,16,8,1,128]{4,3,2,1,0:T(1,128)S(1)} %get-tuple-element.23, ...), kind=kLoop, calls=%fused_computation.16 | loop fusion | flops 6291456 | bytes 8650784 | tf_op jit(solution)/shard_map/mul | solution.py:101
  46.4 0.3 fusion.27
  46.7 0.3 fusion.28
  47.0 0.2 fusion.29
  47.2 0.1 fusion.30
  47.2 1.1 %subtract_multiply_fusion.2 = f32[1,16,6,16,128]{4,3,2,1,0:T(8,128)S(1)} fusion(f32[1,16,8,16,128]{4,3,2,1,0:T(8,128)S(1)} %subtract_multiply_fusion.1, f32[1,16,6,15,128]{4,3,2,1,0:T(8,128)S(1)} %get-tuple-element.30, f32[1,16,6,1,128]{4,3,2,1,0:T(1,128)S(1)} %get-tuple-element.32, f32[1,16,6,1,128]{4,3,2,1,0:T(1,128)S(1)} %get-tuple-element.31, ...), kind=kLoop, calls=%fused_computation.21 | loop fusion | flops 4718592 | bytes 6488088 | tf_op jit(solution)/shard_map/mul | solution.py:101
  48.3 0.2 fusion.31
  48.5 0.2 fusion.32
  48.7 0.0 copy-start.1
  48.8 0.1 fusion.33
  48.9 0.6 copy-done.1
  49.5 0.7 subtract_multiply_fusion.3
  50.3 0.1 reshape_reshape.6
  50.4 0.3 copy.18
  50.8 5.3 %all_to_all.25 = f32[16,2,1,16,256]{4,3,0,2,1:T(8,128)S(1)} all-to-all(f32[16,2,1,16,256]{4,3,0,2,1:T(8,128)S(1)} %copy.19), channel_id=1, replica_groups=mesh['field_0'=4,'field_1'=4,'field_2'=2,'slab'=16] {'field_2'}, dimensions={1} | all-to-all | bytes 1048576 | tf_op jit(solution)/shard_map/all_to_all | solution.py:45
  56.1 0.8 copy.20
  56.9 0.0 copy-start.4
  56.9 13.4 %all-to-all-start.1 = ((f32[16,2,1,16,256]{4,3,1,2,0:T(8,128)}), f32[16,2,1,16,256]{4,3,1,2,0:T(8,128)S(1)}, u32[]{:S(2)}, u32[]{:S(2)}) async-start(f32[16,2,1,16,256]{4,3,1,2,0:T(8,128)} %copy.20), calls=%async_computation.1 | async-start | bytes 1048576 | tf_op jit(solution)/shard_map/all_to_all | solution.py:45
  70.3 0.8 dynamic_slice.7
  71.1 0.8 dynamic-slice_multiply_fusion
  71.9 0.1 broadcast_multiply_fusion
  71.9 11.0 %all-to-all-done.1 = f32[16,2,1,16,256]{4,3,1,2,0:T(8,128)S(1)} async-done(((f32[16,2,1,16,256]{4,3,1,2,0:T(8,128)}), f32[16,2,1,16,256]{4,3,1,2,0:T(8,128)S(1)}, u32[]{:S(2)}, u32[]{:S(2)}) %all-to-all-start.1) | async-done | bytes 524320 | tf_op jit(solution)/shard_map/all_to_all | solution.py:45
  83.0 0.0 copy-start.3
  83.1 0.1 fusion.6
  83.2 0.0 copy-done
  83.2 0.0 copy-done.4
  83.2 1.2 %fusion.3 = f32[32,32,256]{2,1,0:T(8,128)S(1)} fusion(f32[32,16,256]{2,1,0:T(8,128)S(1)} %fusion.6, f32[32]{0:T(128)S(1)} %copy-done.4, f32[32,16]{0,1:T(8,128)S(1)} %copy-done), kind=kOutput, calls=%fused_computation.4 | convolution fusion | flops 50855936 | bytes 1575040 | tf_op jit(solution)/shard_map/rs,ksc->krc/dot_general | solution.py:80
  84.4 0.0 copy-done.3
  84.4 0.7 fusion.4
  85.0 22.5 %all_to_all.26 = f32[32,16,256]{2,1,0:T(8,128)S(1)} all-to-all(f32[32,16,256]{2,1,0:T(8,128)S(1)} %fusion.4), channel_id=1, replica_groups=mesh['field_0'=4,'field_1'=4,'field_2'=2,'slab'=16] {'field_0','field_1'..., dimensions={0} | all-to-all | bytes 1048576 | tf_op jit(solution)/shard_map/all_to_all | solution.py:112
  107.6 0.3 copy.21
  107.9 0.8 reshape.743
  (15 shorter events, 0.3 us)
Async XLA Ops:
  0.0 83.2 %copy-start = (f32[32,16]{0,1:T(8,128)S(1)}, f32[32,16]{0,1:T(8,128)}, u32[]{:S(2)}) copy-start(f32[32,16]{0,1:T(8,128)} %param.15) | copy-start | bytes 6148
  0.0 40.6 %collective-permute-start = (f32[1,16,4,16,128]{4,3,2,1,0:T(8,128)}, f32[1,16,4,16,128]{4,3,2,1,0:T(8,128)S(1)}, u32[]{:S(2)}, u32[]{:S(2)}) collective-permute-start(f32[1,16,4,16,128]{4,3,2,1,0:T(8,128)} %param.9), channel_id=1, source_target_pairs={{0,1},{1,2},{2,3},{3,4},{4,5},{5,6},{6,7},{7,8},{8,9},{9,10},{10,1... | collective-permute-start | bytes 1572872 | tf_op jit(solution)/shard_map/ppermute | solution.py:20
  4.1 36.6 %collective-permute-start.1 = (f32[1,16,4,16,128]{4,3,2,1,0:T(8,128)}, f32[1,16,4,16,128]{4,3,2,1,0:T(8,128)S(1)}, u32[]{:S(2)}, u32[]{:S(2)}) collective-permute-start(f32[1,16,4,16,128]{4,3,2,1,0:T(8,128)} %param.9), channel_id=1, source_target_pairs={{1,0},{2,1},{3,2},{4,3},{5,4},{6,5},{7,6},{8,7},{9,8},{10,9},{11,1... | collective-permute-start | bytes 1572872 | tf_op jit(solution)/shard_map/ppermute | solution.py:22
  16.0 17.7 %collective-permute-start.2 = (f32[4,3,16,128]{3,2,1,0:T(8,128)S(1)}, f32[4,3,16,128]{3,2,1,0:T(8,128)S(1)}, u32[]{:S(2)}, u32[]{:S(2)}) collective-permute-start(f32[4,3,16,128]{3,2,1,0:T(8,128)S(1)} %get-tuple-element.53), channel_id=1, source_target_pairs={{0,1},{1,2},{2,3},{3,4},{4,5},{5,6},{6,7},{7,8},{8,9},{9,10},{10,1... | collective-permute-start | bytes 294920 | tf_op jit(solution)/shard_map/ppermute | solution.py:20
  17.9 15.8 %collective-permute-start.3 = (f32[4,3,16,128]{3,2,1,0:T(8,128)S(1)}, f32[4,3,16,128]{3,2,1,0:T(8,128)S(1)}, u32[]{:S(2)}, u32[]{:S(2)}) collective-permute-start(f32[4,3,16,128]{3,2,1,0:T(8,128)S(1)} %get-tuple-element.54), channel_id=1, source_target_pairs={{1,0},{2,1},{3,2},{4,3},{5,4},{6,5},{7,6},{8,7},{9,8},{10,9},{11,1... | collective-permute-start | bytes 294920 | tf_op jit(solution)/shard_map/ppermute | solution.py:22
  34.6 6.0 %copy-start.2 = (f32[1,16,4,16,128]{4,3,2,1,0:T(8,128)S(1)}, f32[1,16,4,16,128]{4,3,2,1,0:T(8,128)}, u32[]{:S(2)}) copy-start(f32[1,16,4,16,128]{4,3,2,1,0:T(8,128)} %param.9) | copy-start | bytes 1572868
  48.7 0.8 copy-start.1
  56.9 26.3 %copy-start.4 = (f32[32]{0:T(128)S(1)}, f32[32]{0:T(128)}, u32[]{:S(2)}) copy-start(f32[32]{0:T(128)} %param.17) | copy-start | bytes 388
  56.9 26.1 %all-to-all-start.1 = ((f32[16,2,1,16,256]{4,3,1,2,0:T(8,128)}), f32[16,2,1,16,256]{4,3,1,2,0:T(8,128)S(1)}, u32[]{:S(2)}, u32[]{:S(2)}) async-start(f32[16,2,1,16,256]{4,3,1,2,0:T(8,128)} %copy.20), calls=%async_computation.1 | async-start | bytes 1048576 | tf_op jit(solution)/shard_map/all_to_all | solution.py:45
  83.0 1.3 %copy-start.3 = (f32[16,32]{1,0:T(8,128)S(1)}, f32[16,32]{1,0:T(8,128)}, u32[]{:S(2)}) copy-start(f32[16,32]{1,0:T(8,128)} %param.16) | copy-start | bytes 6148
where the time goes:
time: 110 us; the launch traced here: 109 us
  starting transfers between devices  39.7 us (36%)
  blocking collectives  27.8 us (25%)
  other arithmetic  16.6 us (15%)
  local copies, waits for them, and re-layouts  11.3 us (10%)
  waiting for transfers between devices  11.1 us (10%)
  matrix products  1.84 us (2%)
    all_to_all x1, blocking collectives, per_device(): lax.all_to_all(reacted, FIELD, split_axis=0, concat_axis=2, tiled=True)  22.5 us
    ppermute x2, starting transfers between devices, with_halo(): lax.ppermute(head, axis, [((i + 1) % count, i) for i in range(ends)])  20.2 us
    all_to_all x1, starting transfers between devices, moved_by_axis(): lax.all_to_all(blocks, axes[k], split_axis=k, concat_axis=k, tiled=True)  13.4 us
    all_to_all x1, waiting for transfers between devices, moved_by_axis(): lax.all_to_all(blocks, axes[k], split_axis=k, concat_axis=k, tiled=True)  11 us
    sub x4, other arithmetic, advance(): drift_x = velocity[0] - stir_scale * drifts[:, 0][:, None, None, None, None]  8.62 us
    ppermute x2, starting transfers between devices, with_halo(): lax.ppermute(tail, axis, [(i, (i + 1) % count) for i in range(ends)])  6.04 us
    all_to_all x1, blocking collectives, moved_by_axis(): lax.all_to_all(blocks, axes[k], split_axis=k, concat_axis=k, tiled=True)  5.3 us
    mul x4, other arithmetic, per_device(): state = state * inside[:, None, None]  5.06 us
  transfers between devices with their start and end apart: 5, of which 1 were waited for; matrix products, arithmetic and copies ran while one was open for 15% of the time, Pallas kernels for 0%

commit v1 on v0

v1 whole, which is shorter than its diff:
```python
import functools

import jax
import jax.numpy as jnp
from jax import lax
from jax.experimental import pallas as pl
from jax.experimental.pallas import tpu as pltpu
from jax.sharding import Mesh
from jax.sharding import PartitionSpec as P

F = 32
S = 16
R = 32
SUBSTEPS = 4
X = 4
NZ = 16
NY = 128
HALF = S // 2
CHIPS = ("field_0", "field_1")
FIELD = ("field_0", "field_1", "field_2")


def transport_kernel(core_ref, noise_ref, own_ref, prev_ref, next_ref, moved_ref, keep_ref, send_ref, coef_ref):
    core = core_ref[0]

    def layer(channel, i):
        ref, j = (prev_ref, i) if i < X else (own_ref, i - X) if i < 2 * X else (next_ref, i - 2 * X)
        return ref[channel, j]

    slot = 0
    slots = {}
    for i in range(1, 3 * X - 1):
        diff = layer(S + 3, i)
        vx, vy, vz = layer(S, i), layer(S + 1, i), layer(S + 2, i)
        stir = jnp.sqrt(2.0 * diff)
        center = 1.0 - 6.0 * diff
        for k in range(SUBSTEPS):
            if not k < i < 3 * X - 1 - k:
                continue
            slots[k, i] = slot
            hx = 0.5 * (vx - stir * noise_ref[3 * k])
            hy = 0.5 * (vy - stir * noise_ref[3 * k + 1])
            hz = 0.5 * (vz - stir * noise_ref[3 * k + 2])
            for n, c in enumerate((center, diff - hx, diff + hx, diff - hy, diff + hy, diff - hz, diff + hz)):
                coef_ref[slot, n] = c
            slot += 1

    def one(s, carry):
        state = [layer(s, i) for i in range(3 * X)]
        for k in range(SUBSTEPS):
            new = [None] * (3 * X)
            for i in range(k + 1, 3 * X - 1 - k):
                c = coef_ref.at[slots[k, i]]
                mid = state[i]
                new[i] = (
                    c[0] * mid
                    + c[1] * state[i + 1]
                    + c[2] * state[i - 1]
                    + c[3] * pltpu.roll(mid, NY - 1, 1)
                    + c[4] * pltpu.roll(mid, 1, 1)
                    + c[5] * pltpu.roll(mid, NZ - 1, 0)
                    + c[6] * pltpu.roll(mid, 1, 0)
                )
            state = new
        out = jnp.stack(state[X : 2 * X])
        moved_ref[s] = out
        mine = s // HALF == core

        @pl.when(mine)
        def _():
            keep_ref[s % HALF] = out

        @pl.when(jnp.logical_not(mine))
        def _():
            send_ref[s % HALF] = out

        return carry

    lax.fori_loop(0, S, one, 0)


def transport(core, noise, own, prev, following):
    half = jax.ShapeDtypeStruct((HALF, X, NZ, NY), jnp.float32)
    vmem = pl.BlockSpec(memory_space=pltpu.VMEM)
    smem = pl.BlockSpec(memory_space=pltpu.SMEM)
    return pl.pallas_call(
        transport_kernel,
        out_shape=(jax.ShapeDtypeStruct((S, X, NZ, NY), jnp.float32), half, half),
        in_specs=[smem, smem, vmem, vmem, vmem],
        out_specs=(vmem, vmem, vmem),
        scratch_shapes=[pltpu.VMEM((28, 7, NZ, NY), jnp.float32)],
        compiler_params=pltpu.CompilerParams(vmem_limit_bytes=32 * 2**20),
        name="transport",
    )(core, noise, own, prev, following)


def halves(x):
    hi = x.astype(jnp.bfloat16)
    return hi, (x - hi.astype(jnp.float32)).astype(jnp.bfloat16)


def product(weights, values):
    whi, wlo = weights
    vhi, vlo = halves(values)
    return lax.dot_general(
        jnp.concatenate([whi, whi, wlo], 0),
        jnp.concatenate([vhi, vlo, vhi], 0),
        (((0,), (0,)), ((), ())),
        preferred_element_type=jnp.float32,
    )


ROWS = 2


def react_kernel(core_ref, moved_ref, mine_ref, other_ref, rate_ref, vapour_ref, rate_matrix_ref, stoich_ref, out_ref):
    cells = X * NZ
    drive_weights = halves(rate_matrix_ref[...])
    source_weights = halves(stoich_ref[...])
    first = core_ref[0] == 0
    fuel = lax.broadcasted_iota(jnp.int32, (S, NY), 0) == 0

    def one(step, carry):
        mixed = []
        for j in range(ROWS):
            r = step * ROWS + j
            moved = moved_ref[pl.ds(r, S, stride=cells), :]
            mine = mine_ref[pl.ds(r, HALF, stride=cells), :]
            other = other_ref[pl.ds(r, HALF, stride=cells), :]
            average = jnp.concatenate([jnp.where(first, mine, other), jnp.where(first, other, mine)], 0)
            rate = rate_ref[pl.ds(r, 1), :]
            vapour = vapour_ref[pl.ds(r, 1), :]
            mixed.append(moved - 0.5 * rate * (moved - average) + jnp.where(fuel, vapour, 0.0))
        mixed = jnp.concatenate(mixed, 1)
        drive = product(drive_weights, mixed)
        speed = jnp.exp(2.0 * jnp.tanh(drive))
        updated = mixed + product(source_weights, speed)
        for j in range(ROWS):
            out_ref[pl.ds(step * ROWS + j, S, stride=cells), :] = updated[:, j * NY : (j + 1) * NY]
        return carry

    lax.fori_loop(0, cells // ROWS, one, 0)


def react(core, moved, mine, other, rates, vapour, rate_matrix, stoich, prefactor):
    vmem = pl.BlockSpec(memory_space=pltpu.VMEM)
    smem = pl.BlockSpec(memory_space=pltpu.SMEM)
    rows = X * NZ
    return pl.pallas_call(
        react_kernel,
        out_shape=jax.ShapeDtypeStruct((S * rows, NY), jnp.float32),
        in_specs=[smem] + [vmem] * 7,
        out_specs=vmem,
        compiler_params=pltpu.CompilerParams(vmem_limit_bytes=32 * 2**20),
        name="react",
    )(
        core,
        moved.reshape(S * rows, NY),
        mine.reshape(HALF * rows, NY),
        other.reshape(HALF * rows, NY),
        rates.reshape(rows, NY),
        vapour.reshape(rows, NY),
        rate_matrix.T,
        (stoich * prefactor[None]).T,
    )


def per_device(fields, velocity, diffusivity, noise, mix_rate, evaporation, rate_matrix, stoich, prefactor):
    slabs = lax.axis_size("slab")
    core = lax.axis_index("field_2").astype(jnp.int32)[None]
    own = jnp.concatenate([fields[0], velocity, diffusivity[None]], 0)
    prev = lax.ppermute(own, "slab", [(i, i + 1) for i in range(slabs - 1)])
    following = lax.ppermute(own, "slab", [(i + 1, i) for i in range(slabs - 1)])
    moved, keep, send = transport(core, noise.reshape(-1), own, prev, following)
    swap = functools.partial(lax.ppermute, axis_name="field_2", perm=[(0, 1), (1, 0)])
    chips = lax.axis_size(CHIPS)
    pair = (keep + swap(send)).reshape(chips, -1, NZ, NY)
    parts = lax.all_to_all(pair, CHIPS, 0, 0, tiled=True)
    average = jnp.sum(parts, 0) / F
    spread = jnp.broadcast_to(average[None], pair.shape)
    mine = lax.all_to_all(spread, CHIPS, 0, 0, tiled=True)
    updated = react(core, moved, mine, swap(mine), mix_rate, evaporation, rate_matrix, stoich, prefactor)
    return updated.reshape(fields.shape)


def solution(mesh):
    split = Mesh(mesh.devices.reshape(4, 4, 2, mesh.shape["slab"]), (*FIELD, "slab"))
    return jax.shard_map(
        per_device,
        mesh=split,
        in_specs=(
            P(FIELD, None, "slab", None, None),
            P(None, "slab", None, None),
            P("slab", None, None),
            P(FIELD, None, None),
            P("slab", None, None),
            P("slab", None, None),
            P(),
            P(),
            P(),
        ),
        out_specs=P(FIELD, None, "slab", None, None),
        check_vma=False,
    )
```

time: 110 us -> 97.6 us (0.89)
  Pallas kernels: 0 us -> 17.2 us
  starting transfers between devices: 39.7 us -> 22.8 us
  other arithmetic: 16.6 us -> 1.3 us
  blocking collectives: 27.8 us -> 39.5 us
  local copies, waits for them, and re-layouts: 11.3 us -> 0.97 us
  waiting for transfers between devices: 11.1 us -> 14.6 us
  matrix products: 1.84 us -> 0 us
    pallas_call x0 -> x2, Pallas kernels: none -> 17.2 us  [the longest x1 11.1 us: react(): pl.pallas_call(react_kernel, out_shape=jax.ShapeDtypeStruct((S * rows, NY...]
    ppermute x4, waiting for transfers between devices: 0.01 us -> 14.6 us  [the longest x1 11.6 us: per_device(): prev = lax.ppermute(own, 'slab', [(i, i + 1) for i in range(slabs - 1)])]
    all_to_all x1 -> x0, starting transfers between devices: 13.4 us -> none  [moved_by_axis(): lax.all_to_all(blocks, axes[k], split_axis=k, concat_axis=k, tiled=True)]
    all_to_all x2, blocking collectives: 27.8 us -> 39.5 us  [the longest x1 26.3 us: per_device(): parts = lax.all_to_all(pair, CHIPS, 0, 0, tiled=True)]
    all_to_all x1 -> x0, waiting for transfers between devices: 11 us -> none  [moved_by_axis(): lax.all_to_all(blocks, axes[k], split_axis=k, concat_axis=k, tiled=True)]
    sub x4 -> x0, other arithmetic: 8.62 us -> none  [advance(): drift_x = velocity[0] - stir_scale * drifts[:, 0][:, None, None, None, None]]
    slice x21 -> x0, local copies, waits for them, and re-layouts: 7.32 us -> none  [the longest x4 2.64 us: advance(): drift_x = velocity[0] - stir_scale * drifts[:, 0][:, None, None, None, None]]
    mul x6 -> x0, other arithmetic: 5.89 us -> none  [the longest x4 5.06 us: per_device(): state = state * inside[:, None, None]]
  transfers between devices with their start and end apart: 5 -> 4, of which waited for: 1 -> 4; matrix products, arithmetic and copies ran while one was open for 15% -> 0% of each run, Pallas kernels for 0% -> 0%
where the time goes in v1:
time: 97.6 us; the launch traced here: 96.6 us
  blocking collectives  39.5 us (40%)
  starting transfers between devices  22.8 us (23%)
  Pallas kernels  17.2 us (18%)
  waiting for transfers between devices  14.6 us (15%)
  other arithmetic  1.3 us (1%)
    all_to_all x1, blocking collectives, per_device(): parts = lax.all_to_all(pair, CHIPS, 0, 0, tiled=True)  26.3 us
    all_to_all x1, blocking collectives, per_device(): mine = lax.all_to_all(spread, CHIPS, 0, 0, tiled=True)  13.2 us
    ppermute x1, waiting for transfers between devices, per_device(): prev = lax.ppermute(own, 'slab', [(i, i + 1) for i in range(slabs - 1)])  11.6 us
    pallas_call x1, Pallas kernels, react(): pl.pallas_call(react_kernel, out_shape=jax.ShapeDtypeStruct((S * rows, NY...  11.1 us
    ppermute x1, starting transfers between devices, per_device(): lax.ppermute(own, 'slab', [(i + 1, i) for i in range(slabs - 1)])  10.8 us
    pallas_call x1, Pallas kernels, transport(): pl.pallas_call(transport_kernel, out_shape=(jax.ShapeDtypeStruct((S, X, N...  6.12 us
    ppermute x1, starting transfers between devices, per_device(): swap(mine)  4.53 us
    ppermute x1, starting transfers between devices, per_device(): prev = lax.ppermute(own, 'slab', [(i, i + 1) for i in range(slabs - 1)])  4 us
  transfers between devices with their start and end apart: 4, of which 4 were waited for; matrix products, arithmetic and copies ran while one was open for 0% of the time, Pallas kernels for 0%

profile of v1, /device:TPU:57, one launch (start us, length us, event | category | flops | bytes accessed | tf_op | source)
XLA Modules:
  0.0 96.6 jit_solution(5555824511414587287)
XLA Ops:
  0.0 1.2 %pad_maximum_fusion.own_ref = f32[20,4,16,128]{3,2,1,0:T(8,128)S(1)} fusion(f32[1,4,16,128]{3,2,1,0:T(8,128)} %bitcast.21, f32[3,4,16,128]{3,2,1,0:T(8,128)} %param.10, f32[16,4,16,128]{3,2,1,0:T(8,128)} %bitcast.20), kind=kLoop, calls=%fused_computation | loop fusion | flops 327680 | bytes 1310720 | tf_op jit(solution)/shard_map/concatenate | solution.py:171
  1.2 4.0 %collective-permute-start = (f32[20,4,16,128]{3,2,1,0:T(8,128)S(1)}, f32[20,4,16,128]{3,2,1,0:T(8,128)S(1)}, u32[]{:S(2)}, u32[]{:S(2)}) collective-permute-start(f32[20,4,16,128]{3,2,1,0:T(8,128)S(1)} %pad_maximum_fusion.own_ref), channel_id=1, source_target_pairs={{0,1},{1,2},{2,3},{3,4},{4,5},{5,6},{6,7},{7,8},{8,9},{9,10},{10,1... | collective-permute-start | bytes 1966088 | tf_op jit(solution)/shard_map/ppermute | solution.py:172
  5.2 10.8 %collective-permute-start.1 = (f32[20,4,16,128]{3,2,1,0:T(8,128)S(1)}, f32[20,4,16,128]{3,2,1,0:T(8,128)S(1)}, u32[]{:S(2)}, u32[]{:S(2)}) collective-permute-start(f32[20,4,16,128]{3,2,1,0:T(8,128)S(1)} %pad_maximum_fusion.own_ref), channel_id=1, source_target_pairs={{1,0},{2,1},{3,2},{4,3},{5,4},{6,5},{7,6},{8,7},{9,8},{10,9},{11,1... | collective-permute-start | bytes 1966088 | tf_op jit(solution)/shard_map/ppermute | solution.py:173
  16.0 0.0 copy-start.4
  16.0 0.7 copy-done.4
  16.7 0.1 copy.14
  16.8 0.1 reshape.28.noise_ref
  16.9 11.6 %collective-permute-done.prev_ref = f32[20,4,16,128]{3,2,1,0:T(8,128)S(1)} collective-permute-done((f32[20,4,16,128]{3,2,1,0:T(8,128)S(1)}, f32[20,4,16,128]{3,2,1,0:T(8,128)S(1)}, u32[]{:S(2)}, u32[]{:S(2)}) %collective-permute-start) | collective-permute-done | bytes 655392 | tf_op jit(solution)/shard_map/ppermute | solution.py:172
  28.5 0.9 collective-permute-done.1.next_ref
  29.4 6.1 %transport.1 = (f32[16,4,16,128]{3,2,1,0:T(8,128)S(1)}, f32[8,4,16,128]{3,2,1,0:T(8,128)S(1)}, f32[8,4,16,128]{3,2,1,0:T(8,128)S(1)}) custom-call(s32[1]{0:T(128)} %bitcast.core_ref, f32[12]{0:T(128)S(1)} %reshape.28.noise_ref, f32[20,4,16,128]{3,2,1,0:T(8,128)S(1)} %pad_maximum_fusion.own_ref, f32[20,4,16,128]{3,2,1,0:T(8,128)S(1)} %collective-permute-done.prev_ref, ...), custom_call_target="tpu_custom_call" | custom-call | tf_op jit(solution)/shard_map/transport/pallas_call | solution.py:86
  35.5 3.5 %collective-permute-start.2 = (f32[8,4,16,128]{3,2,1,0:T(8,128)S(1)}, f32[8,4,16,128]{3,2,1,0:T(8,128)S(1)}, u32[]{:S(2)}, u32[]{:S(2)}) collective-permute-start(f32[8,4,16,128]{3,2,1,0:T(8,128)S(1)} %get-tuple-element.10), channel_id=1, source_target_pairs={{0,16},{16,0},{1,17},{17,1},{2,18},{18,2},{3,19},{19,3},{4,20},{20... | collective-permute-start | bytes 786440 | tf_op jit(solution)/shard_map/ppermute | solution.py:177
  39.0 1.1 %collective-permute-done.2 = f32[8,4,16,128]{3,2,1,0:T(8,128)S(1)} collective-permute-done((f32[8,4,16,128]{3,2,1,0:T(8,128)S(1)}, f32[8,4,16,128]{3,2,1,0:T(8,128)S(1)}, u32[]{:S(2)}, u32[]{:S(2)}) %collective-permute-start.2) | collective-permute-done | bytes 262176 | tf_op jit(solution)/shard_map/ppermute | solution.py:177
  40.2 26.3 %all_to_all.10 = f32[16,2,16,128]{3,2,1,0:T(8,128)S(1)} all-to-all(f32[16,2,16,128]{3,2,1,0:T(8,128)S(1)} %bitcast.19), channel_id=1, replica_groups=mesh['field_0'=4,'field_1'=4,'field_2'=2,'slab'=16] {'field_0','field_1'}, dimensions={0} | all-to-all | bytes 524288 | tf_op jit(solution)/shard_map/all_to_all | solution.py:178
  66.6 0.0 copy-start.3
  66.6 0.0 copy-start.5
  66.6 0.0 copy-start.2
  66.6 13.2 %all_to_all.11 = f32[16,2,16,128]{3,2,1,0:T(8,128)S(1)} all-to-all(f32[16,2,16,128]{3,2,1,0:T(8,128)S(1)} %broadcast_in_dim.15), channel_id=1, replica_groups=mesh['field_0'=4,'field_1'=4,'field_2'=2,'slab'=16] {'field_0','field_1'}, dimensions={0} | all-to-all | bytes 524288 | tf_op jit(solution)/shard_map/all_to_all | solution.py:181
  79.8 0.0 copy-start
  79.8 0.0 copy-start.1
  79.8 4.5 %collective-permute-start.3 = (f32[16,2,16,128]{3,2,1,0:T(8,128)S(1)}, f32[16,2,16,128]{3,2,1,0:T(8,128)S(1)}, u32[]{:S(2)}, u32[]{:S(2)}) collective-permute-start(f32[16,2,16,128]{3,2,1,0:T(8,128)S(1)} %all_to_all.11), channel_id=1, source_target_pairs={{0,16},{16,0},{1,17},{17,1},{2,18},{18,2},{3,19},{19,3},{4,20},{20... | collective-permute-start | bytes 786440 | tf_op jit(solution)/shard_map/ppermute | solution.py:182
  84.3 0.0 copy-done.3
  84.3 0.1 copy.15
  84.4 0.0 copy-done.5
  84.4 0.1 multiply_bitcast_fusion.stoich_ref
  84.5 1.0 %collective-permute-done.3 = f32[16,2,16,128]{3,2,1,0:T(8,128)S(1)} collective-permute-done((f32[16,2,16,128]{3,2,1,0:T(8,128)S(1)}, f32[16,2,16,128]{3,2,1,0:T(8,128)S(1)}, u32[]{:S(2)}, u32[]{:S(2)}) %collective-permute-start.3) | collective-permute-done | bytes 262176 | tf_op jit(solution)/shard_map/ppermute | solution.py:182
  85.5 0.0 copy-done.2
  85.5 0.0 copy-done
  85.5 0.0 copy-done.1
  85.5 11.1 %react.1 = f32[1024,128]{1,0:T(8,128)} custom-call(s32[1]{0:T(128)} %bitcast.core_ref, f32[1024,128]{1,0:T(8,128)S(1)} %bitcast.14, f32[512,128]{1,0:T(8,128)S(1)} %bitcast.13, f32[512,128]{1,0:T(8,128)S(1)} %bitcast.15, f32[64,128]{1,0:T(8,128)S(1)} %bitcast.16, f32[64,128]{1,0:T(8,128)S(1)} %bitcast.17, f32[16,32]{1,0:T(8,128)S(1)} %bitcast.18, ...), custom_call_target="tpu_custom_call" | custom-call | tf_op jit(solution)/shard_map/react/pallas_call | solution.py:149
  (4 shorter events, 0.1 us)
Async XLA Ops:
  1.2 27.4 %collective-permute-start = (f32[20,4,16,128]{3,2,1,0:T(8,128)S(1)}, f32[20,4,16,128]{3,2,1,0:T(8,128)S(1)}, u32[]{:S(2)}, u32[]{:S(2)}) collective-permute-start(f32[20,4,16,128]{3,2,1,0:T(8,128)S(1)} %pad_maximum_fusion.own_ref), channel_id=1, source_target_pairs={{0,1},{1,2},{2,3},{3,4},{4,5},{5,6},{6,7},{7,8},{8,9},{9,10},{10,1... | collective-permute-start | bytes 1966088 | tf_op jit(solution)/shard_map/ppermute | solution.py:172
  5.2 24.2 %collective-permute-start.1 = (f32[20,4,16,128]{3,2,1,0:T(8,128)S(1)}, f32[20,4,16,128]{3,2,1,0:T(8,128)S(1)}, u32[]{:S(2)}, u32[]{:S(2)}) collective-permute-start(f32[20,4,16,128]{3,2,1,0:T(8,128)S(1)} %pad_maximum_fusion.own_ref), channel_id=1, source_target_pairs={{1,0},{2,1},{3,2},{4,3},{5,4},{6,5},{7,6},{8,7},{9,8},{10,9},{11,1... | collective-permute-start | bytes 1966088 | tf_op jit(solution)/shard_map/ppermute | solution.py:173
  16.0 0.7 copy-start.4
  35.5 4.6 %collective-permute-start.2 = (f32[8,4,16,128]{3,2,1,0:T(8,128)S(1)}, f32[8,4,16,128]{3,2,1,0:T(8,128)S(1)}, u32[]{:S(2)}, u32[]{:S(2)}) collective-permute-start(f32[8,4,16,128]{3,2,1,0:T(8,128)S(1)} %get-tuple-element.10), channel_id=1, source_target_pairs={{0,16},{16,0},{1,17},{17,1},{2,18},{18,2},{3,19},{19,3},{4,20},{20... | collective-permute-start | bytes 786440 | tf_op jit(solution)/shard_map/ppermute | solution.py:177
  66.6 17.7 %copy-start.3 = (f32[16,32]{1,0:T(8,128)S(1)}, f32[16,32]{1,0:T(8,128)}, u32[]{:S(2)}) copy-start(f32[16,32]{1,0:T(8,128)} %param.16) | copy-start | bytes 6148
  66.6 17.8 %copy-start.5 = (f32[32]{0:T(128)S(1)}, f32[32]{0:T(128)}, u32[]{:S(2)}) copy-start(f32[32]{0:T(128)} %param.17) | copy-start | bytes 388
  66.6 18.9 %copy-start.2 = (f32[32,16]{0,1:T(8,128)S(1)}, f32[32,16]{0,1:T(8,128)}, u32[]{:S(2)}) copy-start(f32[32,16]{0,1:T(8,128)} %param.15) | copy-start | bytes 6148
  79.8 5.7 %copy-start = (f32[4,16,128]{2,1,0:T(8,128)S(1)}, f32[4,16,128]{2,1,0:T(8,128)}, u32[]{:S(2)}) copy-start(f32[4,16,128]{2,1,0:T(8,128)} %param.13) | copy-start | bytes 98308
  79.8 5.7 %copy-start.1 = (f32[4,16,128]{2,1,0:T(8,128)S(1)}, f32[4,16,128]{2,1,0:T(8,128)}, u32[]{:S(2)}) copy-start(f32[4,16,128]{2,1,0:T(8,128)} %param.14) | copy-start | bytes 98308
  79.8 5.7 %collective-permute-start.3 = (f32[16,2,16,128]{3,2,1,0:T(8,128)S(1)}, f32[16,2,16,128]{3,2,1,0:T(8,128)S(1)}, u32[]{:S(2)}, u32[]{:S(2)}) collective-permute-start(f32[16,2,16,128]{3,2,1,0:T(8,128)S(1)} %all_to_all.11), channel_id=1, source_target_pairs={{0,16},{16,0},{1,17},{17,1},{2,18},{18,2},{3,19},{19,3},{4,20},{20... | collective-permute-start | bytes 786440 | tf_op jit(solution)/shard_map/ppermute | solution.py:182

commit v2 on v1

v2 whole, which is shorter than its diff:
```python
import functools

import jax
import jax.numpy as jnp
from jax import lax
from jax.experimental import pallas as pl
from jax.experimental.pallas import tpu as pltpu
from jax.sharding import Mesh
from jax.sharding import PartitionSpec as P

F = 32
S = 16
R = 32
SUBSTEPS = 4
X = 4
NZ = 16
NY = 128
HALF = S // 2
SEAM = 7
CHIPS = ("field_0", "field_1")
FIELD = ("field_0", "field_1", "field_2")


SLOT = {}
for _i in range(1, 3 * X - 1):
    for _k in range(SUBSTEPS):
        if _k < _i < 3 * X - 1 - _k:
            SLOT[_k, _i] = len(SLOT)
TOGETHER = 4
VMEM = pl.BlockSpec(memory_space=pltpu.VMEM)
SMEM = pl.BlockSpec(memory_space=pltpu.SMEM)
LIMIT = pltpu.CompilerParams(vmem_limit_bytes=48 * 2**20)


def pack_kernel(where_ref, fields_ref, velocity_ref, diffusivity_ref, sent_ref, kept_ref, sems):
    core = where_ref[0]
    copies = [
        pltpu.make_async_copy(fields_ref.at[0, pl.ds((1 - core) * HALF, HALF)], sent_ref.at[pl.ds(0, HALF)], sems.at[0]),
        pltpu.make_async_copy(velocity_ref, sent_ref.at[pl.ds(HALF, 3)], sems.at[1]),
        pltpu.make_async_copy(diffusivity_ref, sent_ref.at[HALF + 3], sems.at[2]),
        pltpu.make_async_copy(fields_ref.at[0, pl.ds(core * HALF, HALF)], kept_ref, sems.at[3]),
    ]
    for c in copies:
        c.start()
    for c in copies:
        c.wait()


def pack(where, fields, velocity, diffusivity):
    return pl.pallas_call(
        pack_kernel,
        out_shape=(
            jax.ShapeDtypeStruct((HALF + 4, X, NZ, NY), jnp.float32),
            jax.ShapeDtypeStruct((HALF, X, NZ, NY), jnp.float32),
        ),
        in_specs=[SMEM] + [pl.BlockSpec(memory_space=pltpu.HBM)] * 3,
        out_specs=(VMEM, VMEM),
        scratch_shapes=[pltpu.SemaphoreType.DMA((4,))],
        compiler_params=LIMIT,
        name="pack",
    )(where, fields, velocity, diffusivity)


def coefficients(noise_ref, layer, coef_ref):
    for i in range(1, 3 * X - 1):
        diff = layer(HALF + 3, i)
        vx, vy, vz = layer(HALF, i), layer(HALF + 1, i), layer(HALF + 2, i)
        stir = jnp.sqrt(2.0 * diff)
        center = 1.0 - 6.0 * diff
        for k in range(SUBSTEPS):
            if (k, i) not in SLOT:
                continue
            hx = 0.5 * (vx - stir * noise_ref[k, 0])
            hy = 0.5 * (vy - stir * noise_ref[k, 1])
            hz = 0.5 * (vz - stir * noise_ref[k, 2])
            for n, c in enumerate((center, diff - hx, diff + hx, diff - hy, diff + hy, diff - hz, diff + hz)):
                coef_ref[SLOT[k, i], n] = c


def substeps(layer, coef_ref, out_ref):
    def some(g, carry):
        scalars = pl.ds(g * TOGETHER, TOGETHER)
        state = [layer(scalars, i) for i in range(3 * X)]
        for k in range(SUBSTEPS):
            new = [None] * (3 * X)
            for i in range(k + 1, 3 * X - 1 - k):
                c = coef_ref.at[SLOT[k, i]]
                mid = state[i]
                new[i] = (
                    (c[0][None] * mid + c[1][None] * state[i + 1] + c[2][None] * state[i - 1])
                    + (c[3][None] * pltpu.roll(mid, NY - 1, 2) + c[4][None] * pltpu.roll(mid, 1, 2))
                    + (c[5][None] * pltpu.roll(mid, NZ - 1, 1) + c[6][None] * pltpu.roll(mid, 1, 1))
                )
            state = new
        for j in range(X):
            out_ref[scalars, j] = state[X + j]
        return carry

    lax.fori_loop(0, HALF // TOGETHER, some, 0)


def sent_kernel(noise_ref, own_ref, prev_ref, next_ref, out_ref, coef_ref):
    def layer(channel, i):
        ref, j = (prev_ref, i) if i < X else (own_ref, i - X) if i < 2 * X else (next_ref, i - 2 * X)
        return ref[channel, j]

    coefficients(noise_ref, layer, coef_ref)
    substeps(layer, coef_ref, out_ref)


def transport_sent(noise, own, prev, following):
    return pl.pallas_call(
        sent_kernel,
        out_shape=(
            jax.ShapeDtypeStruct((HALF, X, NZ, NY), jnp.float32),
            jax.ShapeDtypeStruct((len(SLOT), 7, NZ, NY), jnp.float32),
        ),
        in_specs=[SMEM, VMEM, VMEM, VMEM],
        out_specs=(VMEM, VMEM),
        compiler_params=LIMIT,
        name="transport_sent",
    )(noise, own, prev, following)


def kept_kernel(where_ref, own_ref, prev_ref, next_ref, crossed_ref, coef_ref, out_ref):
    low = where_ref[1] == SEAM
    high = where_ref[1] == SEAM + 1

    def layer(channel, i):
        if i < X:
            return jnp.where(high, crossed_ref[channel, i], prev_ref[channel, i])
        if i < 2 * X:
            return own_ref[channel, i - X]
        return jnp.where(low, crossed_ref[channel, i - 2 * X], next_ref[channel, i - 2 * X])

    substeps(layer, coef_ref, out_ref)


def transport_kept(where, own, prev, following, crossed, coef):
    return pl.pallas_call(
        kept_kernel,
        out_shape=jax.ShapeDtypeStruct((HALF, X, NZ, NY), jnp.float32),
        in_specs=[SMEM] + [VMEM] * 5,
        out_specs=VMEM,
        compiler_params=LIMIT,
        name="transport_kept",
    )(where, own, prev, following, crossed, coef)


def halves(x):
    hi = x.astype(jnp.bfloat16)
    return hi, (x - hi.astype(jnp.float32)).astype(jnp.bfloat16)


def product(weights, values):
    whi, wlo = weights
    vhi, vlo = halves(values)
    return lax.dot_general(
        jnp.concatenate([whi, whi, wlo], 0),
        jnp.concatenate([vhi, vlo, vhi], 0),
        (((0,), (0,)), ((), ())),
        preferred_element_type=jnp.float32,
    )


ROWS = 16


def react_kernel(
    where_ref, sent_ref, kept_ref, mine_ref, other_ref, rate_ref, vapour_ref, rate_matrix_ref, stoich_ref, out_ref
):
    cells = X * NZ
    drive_weights = halves(rate_matrix_ref[...])
    source_weights = halves(stoich_ref[...])
    first = where_ref[0] == 0
    fuel = lax.broadcasted_iota(jnp.int32, (S, NY), 0) == 0

    def some(step, carry):
        mixed = []
        for j in range(ROWS):
            r = step * ROWS + j
            sent, kept, mine, other = (
                ref[pl.ds(r, HALF, stride=cells), :] for ref in (sent_ref, kept_ref, mine_ref, other_ref)
            )
            rate = 0.5 * rate_ref[pl.ds(r, 1), :]
            vapour = vapour_ref[pl.ds(r, 1), :]
            kept = kept - rate * (kept - mine)
            sent = sent - rate * (sent - other)
            both = jnp.concatenate([jnp.where(first, kept, sent), jnp.where(first, sent, kept)], 0)
            mixed.append(both + jnp.where(fuel, vapour, 0.0))
        mixed = jnp.concatenate(mixed, 1)
        speed = jnp.exp(2.0 * jnp.tanh(product(drive_weights, mixed)))
        updated = mixed + product(source_weights, speed)
        for j in range(ROWS):
            out_ref[pl.ds(step * ROWS + j, S, stride=cells), :] = updated[:, j * NY : (j + 1) * NY]
        return carry

    lax.fori_loop(0, cells // ROWS, some, 0, unroll=2)


def react(where, sent, kept, mine, other, rates, vapour, rate_matrix, stoich, prefactor):
    rows = X * NZ
    return pl.pallas_call(
        react_kernel,
        out_shape=jax.ShapeDtypeStruct((S * rows, NY), jnp.float32),
        in_specs=[SMEM] + [VMEM] * 8,
        out_specs=VMEM,
        compiler_params=LIMIT,
        name="react",
    )(
        where,
        *(x.reshape(HALF * rows, NY) for x in (sent, kept, mine, other)),
        rates.reshape(rows, NY),
        vapour.reshape(rows, NY),
        rate_matrix.T,
        (stoich * prefactor[None]).T,
    )


def per_device(fields, velocity, diffusivity, noise, mix_rate, evaporation, rate_matrix, stoich, prefactor):
    slabs = lax.axis_size("slab")
    where = jnp.stack([lax.axis_index("field_2"), lax.axis_index("slab")]).astype(jnp.int32)
    up = [(i, i + 1) for i in range(slabs - 1)]
    down = [(i + 1, i) for i in range(slabs - 1)]
    send, keep = pack(where, fields, velocity, diffusivity)
    send_prev = lax.ppermute(send, "slab", up)
    send_next = lax.ppermute(send, "slab", down)
    halfway = lax.ppermute(keep, "slab", [(SEAM, slabs - 1), (SEAM + 1, 0)])
    crossed = lax.ppermute(halfway, "slab", [(slabs - 1, SEAM + 1), (0, SEAM)])
    keep_prev = lax.ppermute(keep, "slab", [p for p in up if p[0] != SEAM])
    keep_next = lax.ppermute(keep, "slab", [p for p in down if p[1] != SEAM])
    swap = functools.partial(lax.ppermute, axis_name="field_2", perm=[(0, 1), (1, 0)])
    sent, coef = transport_sent(noise[0], send, send_prev, send_next)
    other = swap(sent)
    kept = transport_kept(where, keep, keep_prev, keep_next, crossed, coef)
    chips = lax.axis_size(CHIPS)
    pair = (kept + other).reshape(chips, -1, NZ, NY)
    parts = lax.all_to_all(pair, CHIPS, 0, 0, tiled=True)
    average = jnp.sum(parts, 0) / F
    spread = jnp.broadcast_to(average[None], pair.shape)
    mine = lax.all_to_all(spread, CHIPS, 0, 0, tiled=True)
    updated = react(where, sent, kept, mine, swap(mine), mix_rate, evaporation, rate_matrix, stoich, prefactor)
    return updated.reshape(fields.shape)


def solution(mesh):
    split = Mesh(mesh.devices.reshape(4, 4, 2, mesh.shape["slab"]), (*FIELD, "slab"))
    return jax.shard_map(
        per_device,
        mesh=split,
        in_specs=(
            P(FIELD, None, "slab", None, None),
            P(None, "slab", None, None),
            P("slab", None, None),
            P(FIELD, None, None),
            P("slab", None, None),
            P("slab", None, None),
            P(),
            P(),
            P(),
        ),
        out_specs=P(FIELD, None, "slab", None, None),
        check_vma=False,
    )
```

time: 97.6 us -> 97.5 us (level)
  the two profiles are of different devices: /device:TPU:57 before, /device:TPU:1 now
where the time goes in v2:
time: 97.5 us; the launch traced here: 96.9 us
  blocking collectives  43.6 us (45%)
  starting transfers between devices  21.7 us (22%)
  waiting for transfers between devices  20.1 us (21%)
  Pallas kernels  7.49 us (8%)
  local copies, waits for them, and re-layouts  3.58 us (4%)
    all_to_all x1, blocking collectives, per_device(): parts = lax.all_to_all(pair, CHIPS, 0, 0, tiled=True)  30.3 us
    ppermute x1, waiting for transfers between devices, per_device(): halfway = lax.ppermute(keep, 'slab', [(SEAM, slabs - 1), (SEAM + 1, 0)])  19.1 us
    all_to_all x1, blocking collectives, per_device(): mine = lax.all_to_all(spread, CHIPS, 0, 0, tiled=True)  13.3 us
    ppermute x1, starting transfers between devices, per_device(): send_prev = lax.ppermute(send, 'slab', up)  4.85 us
    ppermute x1, starting transfers between devices, per_device(): swap(mine)  4.15 us
    ppermute x1, starting transfers between devices, per_device(): keep_prev = lax.ppermute(keep, 'slab', [p for p in up if p[0] != SEAM])  4.01 us
    unnamed x18, local copies, waits for them, and re-layouts  3.57 us
    ppermute x1, starting transfers between devices, per_device(): other = swap(sent)  3.55 us
  transfers between devices with their start and end apart: 8, of which 2 were waited for; matrix products, arithmetic and copies ran while one was open for 1% of the time, Pallas kernels for 4%

profile of v2, /device:TPU:1, one launch (start us, length us, event | category | flops | bytes accessed | tf_op | source)
XLA Modules:
  0.0 96.9 jit_solution(3394318513045634378)
XLA Ops:
  0.0 0.1 pad_add_fusion.where_ref
  0.1 0.0 copy-start
  0.1 1.0 %copy-done = f32[1,16,4,16,128]{4,3,2,1,0:T(8,128)S(1)} copy-done((f32[1,16,4,16,128]{4,3,2,1,0:T(8,128)S(1)}, f32[1,16,4,16,128]{4,3,2,1,0:T(8,128)}, u32[]{:S(2)}) %copy-start) | copy-done | bytes 524312
  1.1 0.0 copy-start.1
  1.1 0.9 copy-done.1
  2.0 0.0 copy-start.2
  2.0 0.8 copy-done.2
  2.8 0.8 pack.1
  3.6 4.8 %collective-permute-start = (f32[12,4,16,128]{3,2,1,0:T(8,128)S(1)}, f32[12,4,16,128]{3,2,1,0:T(8,128)S(1)}, u32[]{:S(2)}, u32[]{:S(2)}) collective-permute-start(f32[12,4,16,128]{3,2,1,0:T(8,128)S(1)} %get-tuple-element.9.own_ref), channel_id=1, source_target_pairs={{0,1},{1,2},{2,3},{3,4},{4,5},{5,6},{6,7},{7,8},{8,9},{9,10},{10,1... | collective-permute-start | bytes 1179656 | tf_op jit(solution)/shard_map/ppermute | solution.py:226
  8.4 1.3 %collective-permute-start.1 = (f32[12,4,16,128]{3,2,1,0:T(8,128)S(1)}, f32[12,4,16,128]{3,2,1,0:T(8,128)S(1)}, u32[]{:S(2)}, u32[]{:S(2)}) collective-permute-start(f32[12,4,16,128]{3,2,1,0:T(8,128)S(1)} %get-tuple-element.9.own_ref), channel_id=1, source_target_pairs={{1,0},{2,1},{3,2},{4,3},{5,4},{6,5},{7,6},{8,7},{9,8},{10,9},{11,1... | collective-permute-start | bytes 1179656 | tf_op jit(solution)/shard_map/ppermute | solution.py:227
  9.7 1.3 %collective-permute-start.4 = (f32[8,4,16,128]{3,2,1,0:T(8,128)S(1)}, f32[8,4,16,128]{3,2,1,0:T(8,128)S(1)}, u32[]{:S(2)}, u32[]{:S(2)}) collective-permute-start(f32[8,4,16,128]{3,2,1,0:T(8,128)S(1)} %get-tuple-element.11.own_ref), channel_id=1, source_target_pairs={{7,15},{8,0},{23,31},{24,16},{39,47},{40,32},{55,63},{56,48},{71,7... | collective-permute-start | bytes 786440 | tf_op jit(solution)/shard_map/ppermute | solution.py:228
  11.0 4.0 %collective-permute-start.2 = (f32[8,4,16,128]{3,2,1,0:T(8,128)S(1)}, f32[8,4,16,128]{3,2,1,0:T(8,128)S(1)}, u32[]{:S(2)}, u32[]{:S(2)}) collective-permute-start(f32[8,4,16,128]{3,2,1,0:T(8,128)S(1)} %get-tuple-element.11.own_ref), channel_id=1, source_target_pairs={{0,1},{1,2},{2,3},{3,4},{4,5},{5,6},{6,7},{8,9},{9,10},{10,11},{11... | collective-permute-start | bytes 786440 | tf_op jit(solution)/shard_map/ppermute | solution.py:230
  15.0 1.3 %collective-permute-start.3 = (f32[8,4,16,128]{3,2,1,0:T(8,128)S(1)}, f32[8,4,16,128]{3,2,1,0:T(8,128)S(1)}, u32[]{:S(2)}, u32[]{:S(2)}) collective-permute-start(f32[8,4,16,128]{3,2,1,0:T(8,128)S(1)} %get-tuple-element.11.own_ref), channel_id=1, source_target_pairs={{1,0},{2,1},{3,2},{4,3},{5,4},{6,5},{7,6},{9,8},{10,9},{11,10},{12... | collective-permute-start | bytes 786440 | tf_op jit(solution)/shard_map/ppermute | solution.py:231
  16.3 0.8 copy.12
  17.1 19.1 %collective-permute-done.4 = f32[8,4,16,128]{3,2,1,0:T(8,128)S(1)} collective-permute-done((f32[8,4,16,128]{3,2,1,0:T(8,128)S(1)}, f32[8,4,16,128]{3,2,1,0:T(8,128)S(1)}, u32[]{:S(2)}, u32[]{:S(2)}) %collective-permute-start.4) | collective-permute-done | bytes 262176 | tf_op jit(solution)/shard_map/ppermute | solution.py:228
  36.2 1.3 %collective-permute-start.5 = (f32[8,4,16,128]{3,2,1,0:T(8,128)S(1)}, f32[8,4,16,128]{3,2,1,0:T(8,128)S(1)}, u32[]{:S(2)}, u32[]{:S(2)}) collective-permute-start(f32[8,4,16,128]{3,2,1,0:T(8,128)S(1)} %collective-permute-done.4), channel_id=1, source_target_pairs={{15,8},{0,7},{31,24},{16,23},{47,40},{32,39},{63,56},{48,55},{79,7... | collective-permute-start | bytes 786440 | tf_op jit(solution)/shard_map/ppermute | solution.py:229
  37.5 0.0 collective-permute-done.prev_ref
  37.5 0.0 collective-permute-done.1.next_ref
  37.5 2.0 %transport_sent.1 = (f32[8,4,16,128]{3,2,1,0:T(8,128)S(1)}, f32[28,7,16,128]{3,2,1,0:T(8,128)S(1)}) custom-call(f32[4,3]{1,0:T(4,128)S(1)} %bitcast.21, f32[12,4,16,128]{3,2,1,0:T(8,128)S(1)} %get-tuple-element.9.own_ref, f32[12,4,16,128]{3,2,1,0:T(8,128)S(1)} %collective-permute-done.prev_ref, f32[12,4,16,128]{3,2,1,0:T(8,128)S(1)} %collective-permute-done.1.next_ref), custom_call_target="tpu_custom_call" | custom-call | tf_op jit(solution)/shard_map/transport_sent/pallas_call | solution.py:112
  39.5 3.6 %collective-permute-start.6 = (f32[8,4,16,128]{3,2,1,0:T(8,128)S(1)}, f32[8,4,16,128]{3,2,1,0:T(8,128)S(1)}, u32[]{:S(2)}, u32[]{:S(2)}) collective-permute-start(f32[8,4,16,128]{3,2,1,0:T(8,128)S(1)} %get-tuple-element.10), channel_id=1, source_target_pairs={{0,16},{16,0},{1,17},{17,1},{2,18},{18,2},{3,19},{19,3},{4,20},{20... | collective-permute-start | bytes 786440 | tf_op jit(solution)/shard_map/ppermute | solution.py:234
  43.1 0.0 collective-permute-done.2.prev_ref
  43.1 0.0 collective-permute-done.3.next_ref
  43.1 0.0 collective-permute-done.5.crossed_ref
  43.1 1.8 %transport_kept.1 = f32[8,4,16,128]{3,2,1,0:T(8,128)S(1)} custom-call(s32[2]{0:T(128)S(1)} %pad_add_fusion.where_ref, f32[8,4,16,128]{3,2,1,0:T(8,128)S(1)} %get-tuple-element.11.own_ref, f32[8,4,16,128]{3,2,1,0:T(8,128)S(1)} %collective-permute-done.2.prev_ref, f32[8,4,16,128]{3,2,1,0:T(8,128)S(1)} %collective-permute-done.3.next_ref, ...), custom_call_target="tpu_custom_call" | custom-call | tf_op jit(solution)/shard_map/transport_kept/pallas_call | solution.py:140
  44.9 0.0 copy-start.6
  44.9 0.0 copy-start.7
  44.9 0.0 copy-start.3
  44.9 0.0 copy-start.4
  44.9 0.0 copy-start.5
  44.9 0.0 collective-permute-done.6
  45.0 30.3 %all_to_all.10 = f32[16,2,16,128]{3,2,1,0:T(8,128)S(1)} all-to-all(f32[16,2,16,128]{3,2,1,0:T(8,128)S(1)} %bitcast.22), channel_id=1, replica_groups=mesh['field_0'=4,'field_1'=4,'field_2'=2,'slab'=16] {'field_0','field_1'}, dimensions={0} | all-to-all | bytes 524288 | tf_op jit(solution)/shard_map/all_to_all | solution.py:238
  75.4 13.3 %all_to_all.11 = f32[16,2,16,128]{3,2,1,0:T(8,128)S(1)} all-to-all(f32[16,2,16,128]{3,2,1,0:T(8,128)S(1)} %broadcast_in_dim.2), channel_id=1, replica_groups=mesh['field_0'=4,'field_1'=4,'field_2'=2,'slab'=16] {'field_0','field_1'}, dimensions={0} | all-to-all | bytes 524288 | tf_op jit(solution)/shard_map/all_to_all | solution.py:241
  88.7 4.1 %collective-permute-start.7 = (f32[16,2,16,128]{3,2,1,0:T(8,128)S(1)}, f32[16,2,16,128]{3,2,1,0:T(8,128)S(1)}, u32[]{:S(2)}, u32[]{:S(2)}) collective-permute-start(f32[16,2,16,128]{3,2,1,0:T(8,128)S(1)} %all_to_all.11), channel_id=1, source_target_pairs={{0,16},{16,0},{1,17},{17,1},{2,18},{18,2},{3,19},{19,3},{4,20},{20... | collective-permute-start | bytes 786440 | tf_op jit(solution)/shard_map/ppermute | solution.py:242
  92.8 0.0 copy-done.6
  92.8 0.1 copy.13
  92.9 0.0 copy-done.7
  92.9 0.1 multiply_bitcast_fusion.stoich_ref
  93.0 1.0 %collective-permute-done.7 = f32[16,2,16,128]{3,2,1,0:T(8,128)S(1)} collective-permute-done((f32[16,2,16,128]{3,2,1,0:T(8,128)S(1)}, f32[16,2,16,128]{3,2,1,0:T(8,128)S(1)}, u32[]{:S(2)}, u32[]{:S(2)}) %collective-permute-start.7) | collective-permute-done | bytes 262176 | tf_op jit(solution)/shard_map/ppermute | solution.py:242
  94.0 0.0 copy-done.3
  94.0 0.0 copy-done.4
  94.0 0.0 copy-done.5
  94.0 3.0 %react.1 = f32[1024,128]{1,0:T(8,128)} custom-call(s32[2]{0:T(128)S(1)} %pad_add_fusion.where_ref, f32[512,128]{1,0:T(8,128)S(1)} %bitcast.16, f32[512,128]{1,0:T(8,128)S(1)} %bitcast.14, f32[512,128]{1,0:T(8,128)S(1)} %bitcast.15, f32[512,128]{1,0:T(8,128)S(1)} %bitcast.17, f32[64,128]{1,0:T(8,128)S(1)} %bitcast.18, f32[64,128]{1,0:T(8,128)S(1)} %bitcast.19, ...), custom_call_target="tpu_custom_call" | custom-call | tf_op jit(solution)/shard_map/react/pallas_call | solution.py:203
  (4 shorter events, 0.1 us)
Async XLA Ops:
  0.1 1.0 %copy-start = (f32[1,16,4,16,128]{4,3,2,1,0:T(8,128)S(1)}, f32[1,16,4,16,128]{4,3,2,1,0:T(8,128)}, u32[]{:S(2)}) copy-start(f32[1,16,4,16,128]{4,3,2,1,0:T(8,128)} %fields_ref.1) | copy-start | bytes 1572868
  1.1 0.9 copy-start.1
  2.0 0.8 copy-start.2
  3.6 33.9 %collective-permute-start = (f32[12,4,16,128]{3,2,1,0:T(8,128)S(1)}, f32[12,4,16,128]{3,2,1,0:T(8,128)S(1)}, u32[]{:S(2)}, u32[]{:S(2)}) collective-permute-start(f32[12,4,16,128]{3,2,1,0:T(8,128)S(1)} %get-tuple-element.9.own_ref), channel_id=1, source_target_pairs={{0,1},{1,2},{2,3},{3,4},{4,5},{5,6},{6,7},{7,8},{8,9},{9,10},{10,1... | collective-permute-start | bytes 1179656 | tf_op jit(solution)/shard_map/ppermute | solution.py:226
  8.4 29.1 %collective-permute-start.1 = (f32[12,4,16,128]{3,2,1,0:T(8,128)S(1)}, f32[12,4,16,128]{3,2,1,0:T(8,128)S(1)}, u32[]{:S(2)}, u32[]{:S(2)}) collective-permute-start(f32[12,4,16,128]{3,2,1,0:T(8,128)S(1)} %get-tuple-element.9.own_ref), channel_id=1, source_target_pairs={{1,0},{2,1},{3,2},{4,3},{5,4},{6,5},{7,6},{8,7},{9,8},{10,9},{11,1... | collective-permute-start | bytes 1179656 | tf_op jit(solution)/shard_map/ppermute | solution.py:227
  9.7 26.5 %collective-permute-start.4 = (f32[8,4,16,128]{3,2,1,0:T(8,128)S(1)}, f32[8,4,16,128]{3,2,1,0:T(8,128)S(1)}, u32[]{:S(2)}, u32[]{:S(2)}) collective-permute-start(f32[8,4,16,128]{3,2,1,0:T(8,128)S(1)} %get-tuple-element.11.own_ref), channel_id=1, source_target_pairs={{7,15},{8,0},{23,31},{24,16},{39,47},{40,32},{55,63},{56,48},{71,7... | collective-permute-start | bytes 786440 | tf_op jit(solution)/shard_map/ppermute | solution.py:228
  11.0 32.1 %collective-permute-start.2 = (f32[8,4,16,128]{3,2,1,0:T(8,128)S(1)}, f32[8,4,16,128]{3,2,1,0:T(8,128)S(1)}, u32[]{:S(2)}, u32[]{:S(2)}) collective-permute-start(f32[8,4,16,128]{3,2,1,0:T(8,128)S(1)} %get-tuple-element.11.own_ref), channel_id=1, source_target_pairs={{0,1},{1,2},{2,3},{3,4},{4,5},{5,6},{6,7},{8,9},{9,10},{10,11},{11... | collective-permute-start | bytes 786440 | tf_op jit(solution)/shard_map/ppermute | solution.py:230
  15.0 28.0 %collective-permute-start.3 = (f32[8,4,16,128]{3,2,1,0:T(8,128)S(1)}, f32[8,4,16,128]{3,2,1,0:T(8,128)S(1)}, u32[]{:S(2)}, u32[]{:S(2)}) collective-permute-start(f32[8,4,16,128]{3,2,1,0:T(8,128)S(1)} %get-tuple-element.11.own_ref), channel_id=1, source_target_pairs={{1,0},{2,1},{3,2},{4,3},{5,4},{6,5},{7,6},{9,8},{10,9},{11,10},{12... | collective-permute-start | bytes 786440 | tf_op jit(solution)/shard_map/ppermute | solution.py:231
  36.2 6.9 %collective-permute-start.5 = (f32[8,4,16,128]{3,2,1,0:T(8,128)S(1)}, f32[8,4,16,128]{3,2,1,0:T(8,128)S(1)}, u32[]{:S(2)}, u32[]{:S(2)}) collective-permute-start(f32[8,4,16,128]{3,2,1,0:T(8,128)S(1)} %collective-permute-done.4), channel_id=1, source_target_pairs={{15,8},{0,7},{31,24},{16,23},{47,40},{32,39},{63,56},{48,55},{79,7... | collective-permute-start | bytes 786440 | tf_op jit(solution)/shard_map/ppermute | solution.py:229
  39.5 5.4 %collective-permute-start.6 = (f32[8,4,16,128]{3,2,1,0:T(8,128)S(1)}, f32[8,4,16,128]{3,2,1,0:T(8,128)S(1)}, u32[]{:S(2)}, u32[]{:S(2)}) collective-permute-start(f32[8,4,16,128]{3,2,1,0:T(8,128)S(1)} %get-tuple-element.10), channel_id=1, source_target_pairs={{0,16},{16,0},{1,17},{17,1},{2,18},{18,2},{3,19},{19,3},{4,20},{20... | collective-permute-start | bytes 786440 | tf_op jit(solution)/shard_map/ppermute | solution.py:234
  44.9 47.9 %copy-start.6 = (f32[16,32]{1,0:T(8,128)S(1)}, f32[16,32]{1,0:T(8,128)}, u32[]{:S(2)}) copy-start(f32[16,32]{1,0:T(8,128)} %param.16) | copy-start | bytes 6148
  44.9 48.0 %copy-start.7 = (f32[32]{0:T(128)S(1)}, f32[32]{0:T(128)}, u32[]{:S(2)}) copy-start(f32[32]{0:T(128)} %param.17) | copy-start | bytes 388
  44.9 49.1 %copy-start.3 = (f32[4,16,128]{2,1,0:T(8,128)S(1)}, f32[4,16,128]{2,1,0:T(8,128)}, u32[]{:S(2)}) copy-start(f32[4,16,128]{2,1,0:T(8,128)} %param.13) | copy-start | bytes 98308
  44.9 49.0 %copy-start.4 = (f32[4,16,128]{2,1,0:T(8,128)S(1)}, f32[4,16,128]{2,1,0:T(8,128)}, u32[]{:S(2)}) copy-start(f32[4,16,128]{2,1,0:T(8,128)} %param.14) | copy-start | bytes 98308
  44.9 49.0 %copy-start.5 = (f32[32,16]{0,1:T(8,128)S(1)}, f32[32,16]{0,1:T(8,128)}, u32[]{:S(2)}) copy-start(f32[32,16]{0,1:T(8,128)} %param.15) | copy-start | bytes 6148
  88.7 5.3 %collective-permute-start.7 = (f32[16,2,16,128]{3,2,1,0:T(8,128)S(1)}, f32[16,2,16,128]{3,2,1,0:T(8,128)S(1)}, u32[]{:S(2)}, u32[]{:S(2)}) collective-permute-start(f32[16,2,16,128]{3,2,1,0:T(8,128)S(1)} %all_to_all.11), channel_id=1, source_target_pairs={{0,16},{16,0},{1,17},{17,1},{2,18},{18,2},{3,19},{19,3},{4,20},{20... | collective-permute-start | bytes 786440 | tf_op jit(solution)/shard_map/ppermute | solution.py:242

commit v3 on v2

--- a/solution.py
+++ b/solution.py
@@ -16,7 +16,6 @@
 NZ = 16
 NY = 128
 HALF = S // 2
-SEAM = 7
 CHIPS = ("field_0", "field_1")
 FIELD = ("field_0", "field_1", "field_2")
 
@@ -58,7 +57,19 @@
         scratch_shapes=[pltpu.SemaphoreType.DMA((4,))],
         compiler_params=LIMIT,
         name="pack",
-    )(where, fields, velocity, diffusivity)
+    )(where, *(pltpu.with_memory_space_constraint(x, pltpu.HBM) for x in (fields, velocity, diffusivity)))
+
+
+def extended(where_ref, own_ref, inner_ref, outer_ref):
+    odd = where_ref[1] % 2 == 1
+
+    def layer(channel, i):
+        if X <= i < 2 * X:
+            return own_ref[channel, i - X]
+        inner, outer = inner_ref[channel, i % X], outer_ref[channel, i % X]
+        return jnp.where(odd, inner, outer) if i < X else jnp.where(odd, outer, inner)
+
+    return layer
 
 
 def coefficients(noise_ref, layer, coef_ref):
@@ -99,52 +110,39 @@
     lax.fori_loop(0, HALF // TOGETHER, some, 0)
 
 
-def sent_kernel(noise_ref, own_ref, prev_ref, next_ref, out_ref, coef_ref):
-    def layer(channel, i):
-        ref, j = (prev_ref, i) if i < X else (own_ref, i - X) if i < 2 * X else (next_ref, i - 2 * X)
-        return ref[channel, j]
-
+def sent_kernel(where_ref, noise_ref, own_ref, outer_ref, inner_ref, out_ref, coef_ref):
+    layer = extended(where_ref, own_ref, inner_ref, outer_ref)
     coefficients(noise_ref, layer, coef_ref)
     substeps(layer, coef_ref, out_ref)
 
 
-def transport_sent(noise, own, prev, following):
+def transport_sent(where, noise, own, outer, inner):
     return pl.pallas_call(
         sent_kernel,
         out_shape=(
             jax.ShapeDtypeStruct((HALF, X, NZ, NY), jnp.float32),
             jax.ShapeDtypeStruct((len(SLOT), 7, NZ, NY), jnp.float32),
         ),
-        in_specs=[SMEM, VMEM, VMEM, VMEM],
+        in_specs=[SMEM, SMEM, VMEM, VMEM, VMEM],
         out_specs=(VMEM, VMEM),
         compiler_params=LIMIT,
         name="transport_sent",
-    )(noise, own, prev, following)
-
-
-def kept_kernel(where_ref, own_ref, prev_ref, next_ref, crossed_ref, coef_ref, out_ref):
-    low = where_ref[1] == SEAM
-    high = where_ref[1] == SEAM + 1
-
-    def layer(channel, i):
-        if i < X:
-            return jnp.where(high, crossed_ref[channel, i], prev_ref[channel, i])
-        if i < 2 * X:
-            return own_ref[channel, i - X]
-        return jnp.where(low, crossed_ref[channel, i - 2 * X], next_ref[channel, i - 2 * X])
-
-    substeps(layer, coef_ref, out_ref)
-
-
-def transport_kept(where, own, prev, following, crossed, coef):
+    )(where, noise, own, outer, inner)
+
+
+def kept_kernel(where_ref, own_ref, inner_ref, outer_ref, coef_ref, out_ref):
+    substeps(extended(where_ref, own_ref, inner_ref, outer_ref), coef_ref, out_ref)
+
+
+def transport_kept(where, own, inner, outer, coef):
     return pl.pallas_call(
         kept_kernel,
         out_shape=jax.ShapeDtypeStruct((HALF, X, NZ, NY), jnp.float32),
-        in_specs=[SMEM] + [VMEM] * 5,
+        in_specs=[SMEM, VMEM, VMEM, VMEM, VMEM],
         out_specs=VMEM,
         compiler_params=LIMIT,
         name="transport_kept",
-    )(where, own, prev, following, crossed, coef)
+    )(where, own, inner, outer, coef)
 
 
 def halves(x):
@@ -195,7 +193,7 @@
             out_ref[pl.ds(step * ROWS + j, S, stride=cells), :] = updated[:, j * NY : (j + 1) * NY]
         return carry
 
-    lax.fori_loop(0, cells // ROWS, some, 0, unroll=2)
+    lax.fori_loop(0, cells // ROWS, some, 0, unroll=4)
 
 
 def react(where, sent, kept, mine, other, rates, vapour, rate_matrix, stoich, prefactor):
@@ -220,19 +218,17 @@
 def per_device(fields, velocity, diffusivity, noise, mix_rate, evaporation, rate_matrix, stoich, prefactor):
     slabs = lax.axis_size("slab")
     where = jnp.stack([lax.axis_index("field_2"), lax.axis_index("slab")]).astype(jnp.int32)
-    up = [(i, i + 1) for i in range(slabs - 1)]
-    down = [(i + 1, i) for i in range(slabs - 1)]
+    inner = [(i, i ^ 1) for i in range(slabs)]
+    outer = [(i, i + 1 if i % 2 else i - 1) for i in range(1, slabs - 1)]
     send, keep = pack(where, fields, velocity, diffusivity)
-    send_prev = lax.ppermute(send, "slab", up)
-    send_next = lax.ppermute(send, "slab", down)
-    halfway = lax.ppermute(keep, "slab", [(SEAM, slabs - 1), (SEAM + 1, 0)])
-    crossed = lax.ppermute(halfway, "slab", [(slabs - 1, SEAM + 1), (0, SEAM)])
-    keep_prev = lax.ppermute(keep, "slab", [p for p in up if p[0] != SEAM])
-    keep_next = lax.ppermute(keep, "slab", [p for p in down if p[1] != SEAM])
+    send_outer = lax.ppermute(send, "slab", outer)
+    send_inner = lax.ppermute(send, "slab", inner)
+    keep_inner = lax.ppermute(keep, "slab", inner)
+    keep_outer = lax.ppermute(keep, "slab", outer)
     swap = functools.partial(lax.ppermute, axis_name="field_2", perm=[(0, 1), (1, 0)])
-    sent, coef = transport_sent(noise[0], send, send_prev, send_next)
+    sent, coef = transport_sent(where, noise[0], send, send_outer, send_inner)
     other = swap(sent)
-    kept = transport_kept(where, keep, keep_prev, keep_next, crossed, coef)
+    kept = transport_kept(where, keep, keep_inner, keep_outer, coef)
     chips = lax.axis_size(CHIPS)
     pair = (kept + other).reshape(chips, -1, NZ, NY)
     parts = lax.all_to_all(pair, CHIPS, 0, 0, tiled=True)

time: 97.5 us -> 80.5 us (0.83)
  the two profiles are of different devices: /device:TPU:1 before, /device:TPU:57 now
where the time goes in v3:
time: 80.5 us; the launch traced here: 79.6 us
  blocking collectives  35.1 us (44%)
  starting transfers between devices  29.7 us (37%)
  Pallas kernels  8.24 us (10%)
  waiting for transfers between devices  5.25 us (7%)
  local copies, waits for them, and re-layouts  0.89 us (1%)
    all_to_all x1, blocking collectives, per_device(): parts = lax.all_to_all(pair, CHIPS, 0, 0, tiled=True)  21.8 us
    all_to_all x1, blocking collectives, per_device(): mine = lax.all_to_all(spread, CHIPS, 0, 0, tiled=True)  13.3 us
    ppermute x1, starting transfers between devices, per_device(): send_outer = lax.ppermute(send, 'slab', outer)  12.9 us
    ppermute x1, starting transfers between devices, per_device(): other = swap(sent)  5.24 us
    ppermute x1, starting transfers between devices, per_device(): swap(mine)  4.37 us
    ppermute x1, starting transfers between devices, per_device(): keep_inner = lax.ppermute(keep, 'slab', inner)  3.36 us
    pallas_call x1, Pallas kernels, react(): pl.pallas_call(react_kernel, out_shape=jax.ShapeDtypeStruct((S * rows, NY...  2.83 us
    ppermute x1, waiting for transfers between devices, per_device(): send_inner = lax.ppermute(send, 'slab', inner)  2.73 us
  transfers between devices with their start and end apart: 6, of which 4 were waited for; matrix products, arithmetic and copies ran while one was open for 1% of the time, Pallas kernels for 5%

profile of v3, /device:TPU:57, one launch (start us, length us, event | category | flops | bytes accessed | tf_op | source)
XLA Modules:
  0.0 79.6 jit_solution(11104285908738713787)
XLA Ops:
  0.0 0.1 pad_add_fusion.where_ref
  0.1 1.7 %pack.1 = (f32[12,4,16,128]{3,2,1,0:T(8,128)S(1)}, f32[8,4,16,128]{3,2,1,0:T(8,128)S(1)}) custom-call(s32[2]{0:T(128)S(1)} %pad_add_fusion.where_ref, f32[1,16,4,16,128]{4,3,2,1,0:T(8,128)} %fields_ref.1, f32[3,4,16,128]{3,2,1,0:T(8,128)} %velocity_ref.1, f32[4,16,128]{2,1,0:T(8,128)} %diffusivity_ref.1), custom_call_target="tpu_custom_call" | custom-call | tf_op jit(solution)/shard_map/pack/pallas_call | solution.py:49
  1.8 12.9 %collective-permute-start = (f32[12,4,16,128]{3,2,1,0:T(8,128)S(1)}, f32[12,4,16,128]{3,2,1,0:T(8,128)S(1)}, u32[]{:S(2)}, u32[]{:S(2)}) collective-permute-start(f32[12,4,16,128]{3,2,1,0:T(8,128)S(1)} %get-tuple-element.9.own_ref), channel_id=1, source_target_pairs={{1,2},{2,1},{3,4},{4,3},{5,6},{6,5},{7,8},{8,7},{9,10},{10,9},{11,... | collective-permute-start | bytes 1179656 | tf_op jit(solution)/shard_map/ppermute | solution.py:224
  14.7 1.9 %collective-permute-start.1 = (f32[12,4,16,128]{3,2,1,0:T(8,128)S(1)}, f32[12,4,16,128]{3,2,1,0:T(8,128)S(1)}, u32[]{:S(2)}, u32[]{:S(2)}) collective-permute-start(f32[12,4,16,128]{3,2,1,0:T(8,128)S(1)} %get-tuple-element.9.own_ref), channel_id=1, source_target_pairs={{0,1},{1,0},{2,3},{3,2},{4,5},{5,4},{6,7},{7,6},{8,9},{9,8},{10,11... | collective-permute-start | bytes 1179656 | tf_op jit(solution)/shard_map/ppermute | solution.py:225
  16.6 3.4 %collective-permute-start.2 = (f32[8,4,16,128]{3,2,1,0:T(8,128)S(1)}, f32[8,4,16,128]{3,2,1,0:T(8,128)S(1)}, u32[]{:S(2)}, u32[]{:S(2)}) collective-permute-start(f32[8,4,16,128]{3,2,1,0:T(8,128)S(1)} %get-tuple-element.11.own_ref), channel_id=1, source_target_pairs={{0,1},{1,0},{2,3},{3,2},{4,5},{5,4},{6,7},{7,6},{8,9},{9,8},{10,11... | collective-permute-start | bytes 786440 | tf_op jit(solution)/shard_map/ppermute | solution.py:226
  20.0 1.9 %collective-permute-start.3 = (f32[8,4,16,128]{3,2,1,0:T(8,128)S(1)}, f32[8,4,16,128]{3,2,1,0:T(8,128)S(1)}, u32[]{:S(2)}, u32[]{:S(2)}) collective-permute-start(f32[8,4,16,128]{3,2,1,0:T(8,128)S(1)} %get-tuple-element.11.own_ref), channel_id=1, source_target_pairs={{1,2},{2,1},{3,4},{4,3},{5,6},{6,5},{7,8},{8,7},{9,10},{10,9},{11,... | collective-permute-start | bytes 786440 | tf_op jit(solution)/shard_map/ppermute | solution.py:227
  21.9 0.8 copy.12
  22.7 0.8 %collective-permute-done.outer_ref = f32[12,4,16,128]{3,2,1,0:T(8,128)S(1)} collective-permute-done((f32[12,4,16,128]{3,2,1,0:T(8,128)S(1)}, f32[12,4,16,128]{3,2,1,0:T(8,128)S(1)}, u32[]{:S(2)}, u32[]{:S(2)}) %collective-permute-start) | collective-permute-done | bytes 393248 | tf_op jit(solution)/shard_map/ppermute | solution.py:224
  23.5 2.7 %collective-permute-done.1.inner_ref = f32[12,4,16,128]{3,2,1,0:T(8,128)S(1)} collective-permute-done((f32[12,4,16,128]{3,2,1,0:T(8,128)S(1)}, f32[12,4,16,128]{3,2,1,0:T(8,128)S(1)}, u32[]{:S(2)}, u32[]{:S(2)}) %collective-permute-start.1) | collective-permute-done | bytes 393248 | tf_op jit(solution)/shard_map/ppermute | solution.py:225
  26.2 2.0 %transport_sent.1 = (f32[8,4,16,128]{3,2,1,0:T(8,128)S(1)}, f32[28,7,16,128]{3,2,1,0:T(8,128)S(1)}) custom-call(s32[2]{0:T(128)S(1)} %pad_add_fusion.where_ref, f32[4,3]{1,0:T(4,128)S(1)} %bitcast.21, f32[12,4,16,128]{3,2,1,0:T(8,128)S(1)} %get-tuple-element.9.own_ref, f32[12,4,16,128]{3,2,1,0:T(8,128)S(1)} %collective-permute-done.outer_ref, ...), custom_call_target="tpu_custom_call" | custom-call | tf_op jit(solution)/shard_map/transport_sent/pallas_call | solution.py:120
  28.2 5.2 %collective-permute-start.4 = (f32[8,4,16,128]{3,2,1,0:T(8,128)S(1)}, f32[8,4,16,128]{3,2,1,0:T(8,128)S(1)}, u32[]{:S(2)}, u32[]{:S(2)}) collective-permute-start(f32[8,4,16,128]{3,2,1,0:T(8,128)S(1)} %get-tuple-element.10), channel_id=1, source_target_pairs={{0,16},{16,0},{1,17},{17,1},{2,18},{18,2},{3,19},{19,3},{4,20},{20... | collective-permute-start | bytes 786440 | tf_op jit(solution)/shard_map/ppermute | solution.py:230
  33.5 0.0 collective-permute-done.2.inner_ref
  33.5 0.7 collective-permute-done.3.outer_ref
  34.2 1.8 %transport_kept.1 = f32[8,4,16,128]{3,2,1,0:T(8,128)S(1)} custom-call(s32[2]{0:T(128)S(1)} %pad_add_fusion.where_ref, f32[8,4,16,128]{3,2,1,0:T(8,128)S(1)} %get-tuple-element.11.own_ref, f32[8,4,16,128]{3,2,1,0:T(8,128)S(1)} %collective-permute-done.2.inner_ref, f32[8,4,16,128]{3,2,1,0:T(8,128)S(1)} %collective-permute-done.3.outer_ref, ...), custom_call_target="tpu_custom_call" | custom-call | tf_op jit(solution)/shard_map/transport_kept/pallas_call | solution.py:138
  35.9 0.0 copy-start.3
  36.0 0.0 copy-start.4
  36.0 0.0 copy-start
  36.0 0.0 copy-start.1
  36.0 0.0 copy-start.2
  36.0 0.0 collective-permute-done.4
  36.1 21.8 %all_to_all.10 = f32[16,2,16,128]{3,2,1,0:T(8,128)S(1)} all-to-all(f32[16,2,16,128]{3,2,1,0:T(8,128)S(1)} %bitcast.22), channel_id=1, replica_groups=mesh['field_0'=4,'field_1'=4,'field_2'=2,'slab'=16] {'field_0','field_1'}, dimensions={0} | all-to-all | bytes 524288 | tf_op jit(solution)/shard_map/all_to_all | solution.py:234
  57.9 13.3 %all_to_all.11 = f32[16,2,16,128]{3,2,1,0:T(8,128)S(1)} all-to-all(f32[16,2,16,128]{3,2,1,0:T(8,128)S(1)} %broadcast_in_dim.2), channel_id=1, replica_groups=mesh['field_0'=4,'field_1'=4,'field_2'=2,'slab'=16] {'field_0','field_1'}, dimensions={0} | all-to-all | bytes 524288 | tf_op jit(solution)/shard_map/all_to_all | solution.py:237
  71.2 4.4 %collective-permute-start.5 = (f32[16,2,16,128]{3,2,1,0:T(8,128)S(1)}, f32[16,2,16,128]{3,2,1,0:T(8,128)S(1)}, u32[]{:S(2)}, u32[]{:S(2)}) collective-permute-start(f32[16,2,16,128]{3,2,1,0:T(8,128)S(1)} %all_to_all.11), channel_id=1, source_target_pairs={{0,16},{16,0},{1,17},{17,1},{2,18},{18,2},{3,19},{19,3},{4,20},{20... | collective-permute-start | bytes 786440 | tf_op jit(solution)/shard_map/ppermute | solution.py:238
  75.6 0.0 copy-done.3
  75.6 0.1 copy.13
  75.7 0.0 copy-done.4
  75.7 0.1 multiply_bitcast_fusion.stoich_ref
  75.8 1.0 %collective-permute-done.5 = f32[16,2,16,128]{3,2,1,0:T(8,128)S(1)} collective-permute-done((f32[16,2,16,128]{3,2,1,0:T(8,128)S(1)}, f32[16,2,16,128]{3,2,1,0:T(8,128)S(1)}, u32[]{:S(2)}, u32[]{:S(2)}) %collective-permute-start.5) | collective-permute-done | bytes 262176 | tf_op jit(solution)/shard_map/ppermute | solution.py:238
  76.8 0.0 copy-done
  76.8 0.0 copy-done.1
  76.8 0.0 copy-done.2
  76.8 2.8 %react.1 = f32[1024,128]{1,0:T(8,128)} custom-call(s32[2]{0:T(128)S(1)} %pad_add_fusion.where_ref, f32[512,128]{1,0:T(8,128)S(1)} %bitcast.16, f32[512,128]{1,0:T(8,128)S(1)} %bitcast.14, f32[512,128]{1,0:T(8,128)S(1)} %bitcast.15, f32[512,128]{1,0:T(8,128)S(1)} %bitcast.17, f32[64,128]{1,0:T(8,128)S(1)} %bitcast.18, f32[64,128]{1,0:T(8,128)S(1)} %bitcast.19, ...), custom_call_target="tpu_custom_call" | custom-call | tf_op jit(solution)/shard_map/react/pallas_call | solution.py:201
  (4 shorter events, 0.1 us)
Async XLA Ops:
  1.8 21.7 %collective-permute-start = (f32[12,4,16,128]{3,2,1,0:T(8,128)S(1)}, f32[12,4,16,128]{3,2,1,0:T(8,128)S(1)}, u32[]{:S(2)}, u32[]{:S(2)}) collective-permute-start(f32[12,4,16,128]{3,2,1,0:T(8,128)S(1)} %get-tuple-element.9.own_ref), channel_id=1, source_target_pairs={{1,2},{2,1},{3,4},{4,3},{5,6},{6,5},{7,8},{8,7},{9,10},{10,9},{11,... | collective-permute-start | bytes 1179656 | tf_op jit(solution)/shard_map/ppermute | solution.py:224
  14.7 11.6 %collective-permute-start.1 = (f32[12,4,16,128]{3,2,1,0:T(8,128)S(1)}, f32[12,4,16,128]{3,2,1,0:T(8,128)S(1)}, u32[]{:S(2)}, u32[]{:S(2)}) collective-permute-start(f32[12,4,16,128]{3,2,1,0:T(8,128)S(1)} %get-tuple-element.9.own_ref), channel_id=1, source_target_pairs={{0,1},{1,0},{2,3},{3,2},{4,5},{5,4},{6,7},{7,6},{8,9},{9,8},{10,11... | collective-permute-start | bytes 1179656 | tf_op jit(solution)/shard_map/ppermute | solution.py:225
  16.6 16.9 %collective-permute-start.2 = (f32[8,4,16,128]{3,2,1,0:T(8,128)S(1)}, f32[8,4,16,128]{3,2,1,0:T(8,128)S(1)}, u32[]{:S(2)}, u32[]{:S(2)}) collective-permute-start(f32[8,4,16,128]{3,2,1,0:T(8,128)S(1)} %get-tuple-element.11.own_ref), channel_id=1, source_target_pairs={{0,1},{1,0},{2,3},{3,2},{4,5},{5,4},{6,7},{7,6},{8,9},{9,8},{10,11... | collective-permute-start | bytes 786440 | tf_op jit(solution)/shard_map/ppermute | solution.py:226
  20.0 14.2 %collective-permute-start.3 = (f32[8,4,16,128]{3,2,1,0:T(8,128)S(1)}, f32[8,4,16,128]{3,2,1,0:T(8,128)S(1)}, u32[]{:S(2)}, u32[]{:S(2)}) collective-permute-start(f32[8,4,16,128]{3,2,1,0:T(8,128)S(1)} %get-tuple-element.11.own_ref), channel_id=1, source_target_pairs={{1,2},{2,1},{3,4},{4,3},{5,6},{6,5},{7,8},{8,7},{9,10},{10,9},{11,... | collective-permute-start | bytes 786440 | tf_op jit(solution)/shard_map/ppermute | solution.py:227
  28.2 7.8 %collective-permute-start.4 = (f32[8,4,16,128]{3,2,1,0:T(8,128)S(1)}, f32[8,4,16,128]{3,2,1,0:T(8,128)S(1)}, u32[]{:S(2)}, u32[]{:S(2)}) collective-permute-start(f32[8,4,16,128]{3,2,1,0:T(8,128)S(1)} %get-tuple-element.10), channel_id=1, source_target_pairs={{0,16},{16,0},{1,17},{17,1},{2,18},{18,2},{3,19},{19,3},{4,20},{20... | collective-permute-start | bytes 786440 | tf_op jit(solution)/shard_map/ppermute | solution.py:230
  35.9 39.7 %copy-start.3 = (f32[16,32]{1,0:T(8,128)S(1)}, f32[16,32]{1,0:T(8,128)}, u32[]{:S(2)}) copy-start(f32[16,32]{1,0:T(8,128)} %param.16) | copy-start | bytes 6148
  36.0 39.8 %copy-start.4 = (f32[32]{0:T(128)S(1)}, f32[32]{0:T(128)}, u32[]{:S(2)}) copy-start(f32[32]{0:T(128)} %param.17) | copy-start | bytes 388
  36.0 40.8 %copy-start = (f32[4,16,128]{2,1,0:T(8,128)S(1)}, f32[4,16,128]{2,1,0:T(8,128)}, u32[]{:S(2)}) copy-start(f32[4,16,128]{2,1,0:T(8,128)} %param.13) | copy-start | bytes 98308
  36.0 40.8 %copy-start.1 = (f32[4,16,128]{2,1,0:T(8,128)S(1)}, f32[4,16,128]{2,1,0:T(8,128)}, u32[]{:S(2)}) copy-start(f32[4,16,128]{2,1,0:T(8,128)} %param.14) | copy-start | bytes 98308
  36.0 40.8 %copy-start.2 = (f32[32,16]{0,1:T(8,128)S(1)}, f32[32,16]{0,1:T(8,128)}, u32[]{:S(2)}) copy-start(f32[32,16]{0,1:T(8,128)} %param.15) | copy-start | bytes 6148
  71.2 5.5 %collective-permute-start.5 = (f32[16,2,16,128]{3,2,1,0:T(8,128)S(1)}, f32[16,2,16,128]{3,2,1,0:T(8,128)S(1)}, u32[]{:S(2)}, u32[]{:S(2)}) collective-permute-start(f32[16,2,16,128]{3,2,1,0:T(8,128)S(1)} %all_to_all.11), channel_id=1, source_target_pairs={{0,16},{16,0},{1,17},{17,1},{2,18},{18,2},{3,19},{19,3},{4,20},{20... | collective-permute-start | bytes 786440 | tf_op jit(solution)/shard_map/ppermute | solution.py:238

commit v4 on v3

--- a/solution.py
+++ b/solution.py
@@ -16,6 +16,7 @@
 NZ = 16
 NY = 128
 HALF = S // 2
+SEAM = 7
 CHIPS = ("field_0", "field_1")
 FIELD = ("field_0", "field_1", "field_2")
 
@@ -31,13 +32,27 @@
 LIMIT = pltpu.CompilerParams(vmem_limit_bytes=48 * 2**20)
 
 
-def pack_kernel(where_ref, fields_ref, velocity_ref, diffusivity_ref, sent_ref, kept_ref, sems):
+def at_seam(where_ref):
+    return jnp.logical_or(where_ref[1] == SEAM, where_ref[1] == SEAM + 1)
+
+
+def pack_kernel(where_ref, fields_ref, velocity_ref, diffusivity_ref, sent_ref, kept_ref, first_ref, sems):
     core = where_ref[0]
+    sent, kept = (1 - core) * HALF, core * HALF
+    first = jnp.where(at_seam(where_ref), kept, sent)
     copies = [
-        pltpu.make_async_copy(fields_ref.at[0, pl.ds((1 - core) * HALF, HALF)], sent_ref.at[pl.ds(0, HALF)], sems.at[0]),
-        pltpu.make_async_copy(velocity_ref, sent_ref.at[pl.ds(HALF, 3)], sems.at[1]),
-        pltpu.make_async_copy(diffusivity_ref, sent_ref.at[HALF + 3], sems.at[2]),
-        pltpu.make_async_copy(fields_ref.at[0, pl.ds(core * HALF, HALF)], kept_ref, sems.at[3]),
+        pltpu.make_async_copy(source, target, sems.at[i])
+        for i, (source, target) in enumerate(
+            [
+                (fields_ref.at[0, pl.ds(first, HALF)], first_ref.at[pl.ds(0, HALF)]),
+                (velocity_ref, first_ref.at[pl.ds(HALF, 3)]),
+                (diffusivity_ref, first_ref.at[HALF + 3]),
+                (fields_ref.at[0, pl.ds(sent, HALF)], sent_ref.at[pl.ds(0, HALF)]),
+                (velocity_ref, sent_ref.at[pl.ds(HALF, 3)]),
+                (diffusivity_ref, sent_ref.at[HALF + 3]),
+                (fields_ref.at[0, pl.ds(kept, HALF)], kept_ref),
+            ]
+        )
     ]
     for c in copies:
         c.start()
@@ -45,19 +60,26 @@
         c.wait()
 
 
-def pack(where, fields, velocity, diffusivity):
+def pack(where, *arrays):
+    sent = jax.ShapeDtypeStruct((HALF + 4, X, NZ, NY), jnp.float32)
     return pl.pallas_call(
         pack_kernel,
-        out_shape=(
-            jax.ShapeDtypeStruct((HALF + 4, X, NZ, NY), jnp.float32),
-            jax.ShapeDtypeStruct((HALF, X, NZ, NY), jnp.float32),
-        ),
+        out_shape=(sent, jax.ShapeDtypeStruct((HALF, X, NZ, NY), jnp.float32), sent),
         in_specs=[SMEM] + [pl.BlockSpec(memory_space=pltpu.HBM)] * 3,
-        out_specs=(VMEM, VMEM),
-        scratch_shapes=[pltpu.SemaphoreType.DMA((4,))],
+        out_specs=(VMEM, VMEM, VMEM),
+        scratch_shapes=[pltpu.SemaphoreType.DMA((7,))],
         compiler_params=LIMIT,
         name="pack",
-    )(where, *(pltpu.with_memory_space_constraint(x, pltpu.HBM) for x in (fields, velocity, diffusivity)))
+    )(where, *(pltpu.with_memory_space_constraint(x, pltpu.HBM) for x in arrays))
+
+
+class Chosen:
+    def __init__(self, flag, other, ref):
+        self.flag, self.other, self.ref = flag, other, ref
+
+    def __getitem__(self, at):
+        other = 0.0 if self.other is None else self.other[at]
+        return jnp.where(self.flag, other, self.ref[at])
 
 
 def extended(where_ref, own_ref, inner_ref, outer_ref):
@@ -110,39 +132,43 @@
     lax.fori_loop(0, HALF // TOGETHER, some, 0)
 
 
-def sent_kernel(where_ref, noise_ref, own_ref, outer_ref, inner_ref, out_ref, coef_ref):
-    layer = extended(where_ref, own_ref, inner_ref, outer_ref)
+def sent_kernel(_, where_ref, noise_ref, own_ref, first_ref, far_ref, inner_ref, out_ref, coef_ref):
+    slab = where_ref[1]
+    ends = jnp.logical_or(slab == 0, slab == 2 * SEAM + 1)
+    outer = Chosen(at_seam(where_ref), far_ref, Chosen(ends, None, first_ref))
+    layer = extended(where_ref, own_ref, inner_ref, outer)
     coefficients(noise_ref, layer, coef_ref)
     substeps(layer, coef_ref, out_ref)
 
 
-def transport_sent(where, noise, own, outer, inner):
+def transport_sent(*args):
     return pl.pallas_call(
         sent_kernel,
         out_shape=(
             jax.ShapeDtypeStruct((HALF, X, NZ, NY), jnp.float32),
             jax.ShapeDtypeStruct((len(SLOT), 7, NZ, NY), jnp.float32),
         ),
-        in_specs=[SMEM, SMEM, VMEM, VMEM, VMEM],
+        in_specs=[pl.BlockSpec(memory_space=pl.ANY), SMEM, SMEM, VMEM, VMEM, VMEM, VMEM],
         out_specs=(VMEM, VMEM),
         compiler_params=LIMIT,
         name="transport_sent",
-    )(where, noise, own, outer, inner)
-
-
-def kept_kernel(where_ref, own_ref, inner_ref, outer_ref, coef_ref, out_ref):
-    substeps(extended(where_ref, own_ref, inner_ref, outer_ref), coef_ref, out_ref)
-
-
-def transport_kept(where, own, inner, outer, coef):
+    )(*args)
+
+
+def kept_kernel(where_ref, own_ref, crossed_ref, inner_ref, outer_ref, coef_ref, out_ref):
+    outer = Chosen(at_seam(where_ref), crossed_ref, outer_ref)
+    substeps(extended(where_ref, own_ref, inner_ref, outer), coef_ref, out_ref)
+
+
+def transport_kept(*args):
     return pl.pallas_call(
         kept_kernel,
         out_shape=jax.ShapeDtypeStruct((HALF, X, NZ, NY), jnp.float32),
-        in_specs=[SMEM, VMEM, VMEM, VMEM, VMEM],
+        in_specs=[SMEM, VMEM, VMEM, VMEM, VMEM, VMEM],
         out_specs=VMEM,
         compiler_params=LIMIT,
         name="transport_kept",
-    )(where, own, inner, outer, coef)
+    )(*args)
 
 
 def halves(x):
@@ -219,16 +245,19 @@
     slabs = lax.axis_size("slab")
     where = jnp.stack([lax.axis_index("field_2"), lax.axis_index("slab")]).astype(jnp.int32)
     inner = [(i, i ^ 1) for i in range(slabs)]
-    outer = [(i, i + 1 if i % 2 else i - 1) for i in range(1, slabs - 1)]
-    send, keep = pack(where, fields, velocity, diffusivity)
-    send_outer = lax.ppermute(send, "slab", outer)
+    outer = [(i, i + 1 if i % 2 else i - 1) for i in range(1, slabs - 1) if i not in (SEAM, SEAM + 1)]
+    send, keep, first = pack(where, fields, velocity, diffusivity)
+    send_outer = lax.ppermute(first, "slab", outer + [(SEAM, slabs - 1), (SEAM + 1, 0)])
+    send_far = lax.ppermute(send, "slab", [(SEAM, SEAM + 1), (SEAM + 1, SEAM)])
     send_inner = lax.ppermute(send, "slab", inner)
+    halfway = send_outer[:HALF]
+    crossed = lax.ppermute(halfway, "slab", [(slabs - 1, SEAM + 1), (0, SEAM)])
     keep_inner = lax.ppermute(keep, "slab", inner)
     keep_outer = lax.ppermute(keep, "slab", outer)
     swap = functools.partial(lax.ppermute, axis_name="field_2", perm=[(0, 1), (1, 0)])
-    sent, coef = transport_sent(where, noise[0], send, send_outer, send_inner)
+    sent, coef = transport_sent(halfway, where, noise[0], send, send_outer, send_far, send_inner)
     other = swap(sent)
-    kept = transport_kept(where, keep, keep_inner, keep_outer, coef)
+    kept = transport_kept(where, keep, crossed, keep_inner, keep_outer, coef)
     chips = lax.axis_size(CHIPS)
     pair = (kept + other).reshape(chips, -1, NZ, NY)
     parts = lax.all_to_all(pair, CHIPS, 0, 0, tiled=True)

time: 80.5 us -> 95.8 us (1.19)
  blocking collectives: 35.1 us -> 43.2 us
  waiting for transfers between devices: 5.25 us -> 8.99 us
  starting transfers between devices: 29.7 us -> 33 us
    all_to_all x1, blocking collectives: 21.8 us -> 30.2 us  [per_device(): parts = lax.all_to_all(pair, CHIPS, 0, 0, tiled=True)]
    ppermute x1 -> x3, waiting for transfers between devices: 0.83 us -> 8 us  [the longest x1 6.9 us: per_device(): send_far = lax.ppermute(send, 'slab', [(SEAM, SEAM + 1), (SEAM + 1, SEAM)])]
    ppermute x1 -> x3, starting transfers between devices: 12.9 us -> 19 us  [the longest x1 13.2 us: per_device(): send_far = lax.ppermute(send, 'slab', [(SEAM, SEAM + 1), (SEAM + 1, SEAM)])]
    ppermute x1, waiting for transfers between devices: 2.73 us -> 0.01 us  [per_device(): send_inner = lax.ppermute(send, 'slab', inner)]
    ppermute x1, starting transfers between devices: 5.24 us -> 3.66 us  [per_device(): other = swap(sent)]
    ppermute x1, starting transfers between devices: 1.92 us -> 0.68 us  [per_device(): keep_outer = lax.ppermute(keep, 'slab', outer)]
  transfers between devices with their start and end apart: 6 -> 8, of which waited for: 4 -> 3; matrix products, arithmetic and copies ran while one was open for 1% -> 1% of each run, Pallas kernels for 5% -> 4%
where the time goes in v4:
time: 95.8 us; the launch traced here: 94.9 us
  blocking collectives  43.2 us (45%)
  starting transfers between devices  33 us (34%)
  waiting for transfers between devices  8.99 us (9%)
  Pallas kernels  8.42 us (9%)
    all_to_all x1, blocking collectives, per_device(): parts = lax.all_to_all(pair, CHIPS, 0, 0, tiled=True)  30.2 us
    ppermute x1, starting transfers between devices, per_device(): send_far = lax.ppermute(send, 'slab', [(SEAM, SEAM + 1), (SEAM + 1, SEAM)])  13.2 us
    all_to_all x1, blocking collectives, per_device(): mine = lax.all_to_all(spread, CHIPS, 0, 0, tiled=True)  13 us
    ppermute x1, waiting for transfers between devices, per_device(): send_far = lax.ppermute(send, 'slab', [(SEAM, SEAM + 1), (SEAM + 1, SEAM)])  6.9 us
    ppermute x1, starting transfers between devices, per_device(): lax.ppermute(first, 'slab', outer + [(SEAM, slabs - 1), (SEAM + 1, 0)])  4.45 us
    ppermute x1, starting transfers between devices, per_device(): swap(mine)  4.4 us
    ppermute x1, starting transfers between devices, per_device(): other = swap(sent)  3.66 us
    ppermute x1, starting transfers between devices, per_device(): keep_inner = lax.ppermute(keep, 'slab', inner)  3.36 us
  transfers between devices with their start and end apart: 8, of which 3 were waited for; matrix products, arithmetic and copies ran while one was open for 1% of the time, Pallas kernels for 4%

profile of v4, /device:TPU:57, one launch (start us, length us, event | category | flops | bytes accessed | tf_op | source)
XLA Modules:
  0.0 94.9 jit_solution(15841074086244621006)
XLA Ops:
  0.0 0.1 pad_add_fusion.where_ref
  0.1 1.8 %pack.1 = (f32[12,4,16,128]{3,2,1,0:T(8,128)S(1)}, f32[8,4,16,128]{3,2,1,0:T(8,128)S(1)}, f32[12,4,16,128]{3,2,1,0:T(8,128)S(1)}) custom-call(s32[2]{0:T(128)S(1)} %pad_add_fusion.where_ref, f32[1,16,4,16,128]{4,3,2,1,0:T(8,128)} %fields_ref.1, f32[3,4,16,128]{3,2,1,0:T(8,128)} %velocity_ref.1, f32[4,16,128]{2,1,0:T(8,128)} %diffusivity_ref.1), custom_call_target="tpu_custom_call" | custom-call | tf_op jit(solution)/shard_map/pack/pallas_call | solution.py:65
  1.9 4.5 %collective-permute-start = (f32[12,4,16,128]{3,2,1,0:T(8,128)S(1)}, f32[12,4,16,128]{3,2,1,0:T(8,128)S(1)}, u32[]{:S(2)}, u32[]{:S(2)}) collective-permute-start(f32[12,4,16,128]{3,2,1,0:T(8,128)S(1)} %get-tuple-element.10), channel_id=1, source_target_pairs={{1,2},{2,1},{3,4},{4,3},{5,6},{6,5},{9,10},{10,9},{11,12},{12,11},... | collective-permute-start | bytes 1179656 | tf_op jit(solution)/shard_map/ppermute | solution.py:250
  6.4 13.2 %collective-permute-start.1 = (f32[12,4,16,128]{3,2,1,0:T(8,128)S(1)}, f32[12,4,16,128]{3,2,1,0:T(8,128)S(1)}, u32[]{:S(2)}, u32[]{:S(2)}) collective-permute-start(f32[12,4,16,128]{3,2,1,0:T(8,128)S(1)} %get-tuple-element.11.own_ref), channel_id=1, source_target_pairs={{7,8},{8,7},{23,24},{24,23},{39,40},{40,39},{55,56},{56,55},{71,72... | collective-permute-start | bytes 1179656 | tf_op jit(solution)/shard_map/ppermute | solution.py:251
  19.6 1.9 %collective-permute-start.2 = (f32[12,4,16,128]{3,2,1,0:T(8,128)S(1)}, f32[12,4,16,128]{3,2,1,0:T(8,128)S(1)}, u32[]{:S(2)}, u32[]{:S(2)}) collective-permute-start(f32[12,4,16,128]{3,2,1,0:T(8,128)S(1)} %get-tuple-element.11.own_ref), channel_id=1, source_target_pairs={{0,1},{1,0},{2,3},{3,2},{4,5},{5,4},{6,7},{7,6},{8,9},{9,8},{10,11... | collective-permute-start | bytes 1179656 | tf_op jit(solution)/shard_map/ppermute | solution.py:252
  21.5 3.4 %collective-permute-start.4 = (f32[8,4,16,128]{3,2,1,0:T(8,128)S(1)}, f32[8,4,16,128]{3,2,1,0:T(8,128)S(1)}, u32[]{:S(2)}, u32[]{:S(2)}) collective-permute-start(f32[8,4,16,128]{3,2,1,0:T(8,128)S(1)} %get-tuple-element.13.own_ref), channel_id=1, source_target_pairs={{0,1},{1,0},{2,3},{3,2},{4,5},{5,4},{6,7},{7,6},{8,9},{9,8},{10,11... | collective-permute-start | bytes 786440 | tf_op jit(solution)/shard_map/ppermute | solution.py:255
  24.9 0.7 collective-permute-start.5
  25.6 0.8 copy.12
  26.4 0.0 collective-permute-done.first_ref
  26.4 1.3 %collective-permute-start.3 = (f32[8,4,16,128]{3,2,1,0:T(8,128)S(1)}, f32[8,4,16,128]{3,2,1,0:T(8,128)S(1)}, u32[]{:S(2)}, u32[]{:S(2)}) collective-permute-start(f32[8,4,16,128]{3,2,1,0:T(8,128)S(1)} %slice.4._), channel_id=1, source_target_pairs={{15,8},{0,7},{31,24},{16,23},{47,40},{32,39},{63,56},{48,55},{79,7... | collective-permute-start | bytes 786440 | tf_op jit(solution)/shard_map/ppermute | solution.py:254
  27.7 6.9 %collective-permute-done.1.far_ref = f32[12,4,16,128]{3,2,1,0:T(8,128)S(1)} collective-permute-done((f32[12,4,16,128]{3,2,1,0:T(8,128)S(1)}, f32[12,4,16,128]{3,2,1,0:T(8,128)S(1)}, u32[]{:S(2)}, u32[]{:S(2)}) %collective-permute-start.1) | collective-permute-done | bytes 393248 | tf_op jit(solution)/shard_map/ppermute | solution.py:251
  34.6 0.0 collective-permute-done.2.inner_ref
  34.6 2.0 %transport_sent.1 = (f32[8,4,16,128]{3,2,1,0:T(8,128)S(1)}, f32[28,7,16,128]{3,2,1,0:T(8,128)S(1)}) custom-call(f32[8,4,16,128]{3,2,1,0:T(8,128)S(1)} %slice.4._, s32[2]{0:T(128)S(1)} %pad_add_fusion.where_ref, f32[4,3]{1,0:T(4,128)S(1)} %bitcast.21, f32[12,4,16,128]{3,2,1,0:T(8,128)S(1)} %get-tuple-element.11.own_ref, ...), custom_call_target="tpu_custom_call" | custom-call | tf_op jit(solution)/shard_map/transport_sent/pallas_call | solution.py:145
  36.6 3.7 %collective-permute-start.6 = (f32[8,4,16,128]{3,2,1,0:T(8,128)S(1)}, f32[8,4,16,128]{3,2,1,0:T(8,128)S(1)}, u32[]{:S(2)}, u32[]{:S(2)}) collective-permute-start(f32[8,4,16,128]{3,2,1,0:T(8,128)S(1)} %get-tuple-element.12), channel_id=1, source_target_pairs={{0,16},{16,0},{1,17},{17,1},{2,18},{18,2},{3,19},{19,3},{4,20},{20... | collective-permute-start | bytes 786440 | tf_op jit(solution)/shard_map/ppermute | solution.py:259
  40.3 0.0 collective-permute-done.4.inner_ref
  40.3 0.0 collective-permute-done.5.outer_ref
  40.3 1.1 %collective-permute-done.3.crossed_ref = f32[8,4,16,128]{3,2,1,0:T(8,128)S(1)} collective-permute-done((f32[8,4,16,128]{3,2,1,0:T(8,128)S(1)}, f32[8,4,16,128]{3,2,1,0:T(8,128)S(1)}, u32[]{:S(2)}, u32[]{:S(2)}) %collective-permute-start.3) | collective-permute-done | bytes 262176 | tf_op jit(solution)/shard_map/ppermute | solution.py:254
  41.4 1.8 %transport_kept.1 = f32[8,4,16,128]{3,2,1,0:T(8,128)S(1)} custom-call(s32[2]{0:T(128)S(1)} %pad_add_fusion.where_ref, f32[8,4,16,128]{3,2,1,0:T(8,128)S(1)} %get-tuple-element.13.own_ref, f32[8,4,16,128]{3,2,1,0:T(8,128)S(1)} %collective-permute-done.3.crossed_ref, f32[8,4,16,128]{3,2,1,0:T(8,128)S(1)} %collective-permute-done.4.inner_ref, ...), custom_call_target="tpu_custom_call" | custom-call | tf_op jit(solution)/shard_map/transport_kept/pallas_call | solution.py:164
  43.2 0.0 copy-start.3
  43.2 0.0 copy-start.4
  43.2 0.0 copy-start
  43.2 0.0 copy-start.1
  43.2 0.0 copy-start.2
  43.2 0.0 collective-permute-done.6
  43.3 30.2 %all_to_all.10 = f32[16,2,16,128]{3,2,1,0:T(8,128)S(1)} all-to-all(f32[16,2,16,128]{3,2,1,0:T(8,128)S(1)} %bitcast.22), channel_id=1, replica_groups=mesh['field_0'=4,'field_1'=4,'field_2'=2,'slab'=16] {'field_0','field_1'}, dimensions={0} | all-to-all | bytes 524288 | tf_op jit(solution)/shard_map/all_to_all | solution.py:263
  73.5 13.0 %all_to_all.11 = f32[16,2,16,128]{3,2,1,0:T(8,128)S(1)} all-to-all(f32[16,2,16,128]{3,2,1,0:T(8,128)S(1)} %broadcast_in_dim.2), channel_id=1, replica_groups=mesh['field_0'=4,'field_1'=4,'field_2'=2,'slab'=16] {'field_0','field_1'}, dimensions={0} | all-to-all | bytes 524288 | tf_op jit(solution)/shard_map/all_to_all | solution.py:266
  86.6 4.4 %collective-permute-start.7 = (f32[16,2,16,128]{3,2,1,0:T(8,128)S(1)}, f32[16,2,16,128]{3,2,1,0:T(8,128)S(1)}, u32[]{:S(2)}, u32[]{:S(2)}) collective-permute-start(f32[16,2,16,128]{3,2,1,0:T(8,128)S(1)} %all_to_all.11), channel_id=1, source_target_pairs={{0,16},{16,0},{1,17},{17,1},{2,18},{18,2},{3,19},{19,3},{4,20},{20... | collective-permute-start | bytes 786440 | tf_op jit(solution)/shard_map/ppermute | solution.py:267
  91.0 0.0 copy-done.3
  91.0 0.1 copy.13
  91.0 0.0 copy-done.4
  91.0 0.1 multiply_bitcast_fusion.stoich_ref
  91.1 1.0 %collective-permute-done.7 = f32[16,2,16,128]{3,2,1,0:T(8,128)S(1)} collective-permute-done((f32[16,2,16,128]{3,2,1,0:T(8,128)S(1)}, f32[16,2,16,128]{3,2,1,0:T(8,128)S(1)}, u32[]{:S(2)}, u32[]{:S(2)}) %collective-permute-start.7) | collective-permute-done | bytes 262176 | tf_op jit(solution)/shard_map/ppermute | solution.py:267
  92.1 0.0 copy-done
  92.1 0.0 copy-done.1
  92.1 0.0 copy-done.2
  92.1 2.8 %react.1 = f32[1024,128]{1,0:T(8,128)} custom-call(s32[2]{0:T(128)S(1)} %pad_add_fusion.where_ref, f32[512,128]{1,0:T(8,128)S(1)} %bitcast.16, f32[512,128]{1,0:T(8,128)S(1)} %bitcast.14, f32[512,128]{1,0:T(8,128)S(1)} %bitcast.15, f32[512,128]{1,0:T(8,128)S(1)} %bitcast.17, f32[64,128]{1,0:T(8,128)S(1)} %bitcast.18, f32[64,128]{1,0:T(8,128)S(1)} %bitcast.19, ...), custom_call_target="tpu_custom_call" | custom-call | tf_op jit(solution)/shard_map/react/pallas_call | solution.py:227
  (5 shorter events, 0.1 us)
Async XLA Ops:
  1.9 24.5 %collective-permute-start = (f32[12,4,16,128]{3,2,1,0:T(8,128)S(1)}, f32[12,4,16,128]{3,2,1,0:T(8,128)S(1)}, u32[]{:S(2)}, u32[]{:S(2)}) collective-permute-start(f32[12,4,16,128]{3,2,1,0:T(8,128)S(1)} %get-tuple-element.10), channel_id=1, source_target_pairs={{1,2},{2,1},{3,4},{4,3},{5,6},{6,5},{9,10},{10,9},{11,12},{12,11},... | collective-permute-start | bytes 1179656 | tf_op jit(solution)/shard_map/ppermute | solution.py:250
  6.4 28.2 %collective-permute-start.1 = (f32[12,4,16,128]{3,2,1,0:T(8,128)S(1)}, f32[12,4,16,128]{3,2,1,0:T(8,128)S(1)}, u32[]{:S(2)}, u32[]{:S(2)}) collective-permute-start(f32[12,4,16,128]{3,2,1,0:T(8,128)S(1)} %get-tuple-element.11.own_ref), channel_id=1, source_target_pairs={{7,8},{8,7},{23,24},{24,23},{39,40},{40,39},{55,56},{56,55},{71,72... | collective-permute-start | bytes 1179656 | tf_op jit(solution)/shard_map/ppermute | solution.py:251
  19.6 15.0 %collective-permute-start.2 = (f32[12,4,16,128]{3,2,1,0:T(8,128)S(1)}, f32[12,4,16,128]{3,2,1,0:T(8,128)S(1)}, u32[]{:S(2)}, u32[]{:S(2)}) collective-permute-start(f32[12,4,16,128]{3,2,1,0:T(8,128)S(1)} %get-tuple-element.11.own_ref), channel_id=1, source_target_pairs={{0,1},{1,0},{2,3},{3,2},{4,5},{5,4},{6,7},{7,6},{8,9},{9,8},{10,11... | collective-permute-start | bytes 1179656 | tf_op jit(solution)/shard_map/ppermute | solution.py:252
  21.5 18.7 %collective-permute-start.4 = (f32[8,4,16,128]{3,2,1,0:T(8,128)S(1)}, f32[8,4,16,128]{3,2,1,0:T(8,128)S(1)}, u32[]{:S(2)}, u32[]{:S(2)}) collective-permute-start(f32[8,4,16,128]{3,2,1,0:T(8,128)S(1)} %get-tuple-element.13.own_ref), channel_id=1, source_target_pairs={{0,1},{1,0},{2,3},{3,2},{4,5},{5,4},{6,7},{7,6},{8,9},{9,8},{10,11... | collective-permute-start | bytes 786440 | tf_op jit(solution)/shard_map/ppermute | solution.py:255
  24.9 15.4 %collective-permute-start.5 = (f32[8,4,16,128]{3,2,1,0:T(8,128)S(1)}, f32[8,4,16,128]{3,2,1,0:T(8,128)S(1)}, u32[]{:S(2)}, u32[]{:S(2)}) collective-permute-start(f32[8,4,16,128]{3,2,1,0:T(8,128)S(1)} %get-tuple-element.13.own_ref), channel_id=1, source_target_pairs={{1,2},{2,1},{3,4},{4,3},{5,6},{6,5},{9,10},{10,9},{11,12},{12,11},... | collective-permute-start | bytes 786440 | tf_op jit(solution)/shard_map/ppermute | solution.py:256
  26.4 15.0 %collective-permute-start.3 = (f32[8,4,16,128]{3,2,1,0:T(8,128)S(1)}, f32[8,4,16,128]{3,2,1,0:T(8,128)S(1)}, u32[]{:S(2)}, u32[]{:S(2)}) collective-permute-start(f32[8,4,16,128]{3,2,1,0:T(8,128)S(1)} %slice.4._), channel_id=1, source_target_pairs={{15,8},{0,7},{31,24},{16,23},{47,40},{32,39},{63,56},{48,55},{79,7... | collective-permute-start | bytes 786440 | tf_op jit(solution)/shard_map/ppermute | solution.py:254
  36.6 6.7 %collective-permute-start.6 = (f32[8,4,16,128]{3,2,1,0:T(8,128)S(1)}, f32[8,4,16,128]{3,2,1,0:T(8,128)S(1)}, u32[]{:S(2)}, u32[]{:S(2)}) collective-permute-start(f32[8,4,16,128]{3,2,1,0:T(8,128)S(1)} %get-tuple-element.12), channel_id=1, source_target_pairs={{0,16},{16,0},{1,17},{17,1},{2,18},{18,2},{3,19},{19,3},{4,20},{20... | collective-permute-start | bytes 786440 | tf_op jit(solution)/shard_map/ppermute | solution.py:259
  43.2 47.8 %copy-start.3 = (f32[16,32]{1,0:T(8,128)S(1)}, f32[16,32]{1,0:T(8,128)}, u32[]{:S(2)}) copy-start(f32[16,32]{1,0:T(8,128)} %param.16) | copy-start | bytes 6148
  43.2 47.9 %copy-start.4 = (f32[32]{0:T(128)S(1)}, f32[32]{0:T(128)}, u32[]{:S(2)}) copy-start(f32[32]{0:T(128)} %param.17) | copy-start | bytes 388
  43.2 48.9 %copy-start = (f32[4,16,128]{2,1,0:T(8,128)S(1)}, f32[4,16,128]{2,1,0:T(8,128)}, u32[]{:S(2)}) copy-start(f32[4,16,128]{2,1,0:T(8,128)} %param.13) | copy-start | bytes 98308
  43.2 48.9 %copy-start.1 = (f32[4,16,128]{2,1,0:T(8,128)S(1)}, f32[4,16,128]{2,1,0:T(8,128)}, u32[]{:S(2)}) copy-start(f32[4,16,128]{2,1,0:T(8,128)} %param.14) | copy-start | bytes 98308
  43.2 48.9 %copy-start.2 = (f32[32,16]{0,1:T(8,128)S(1)}, f32[32,16]{0,1:T(8,128)}, u32[]{:S(2)}) copy-start(f32[32,16]{0,1:T(8,128)} %param.15) | copy-start | bytes 6148
  86.6 5.5 %collective-permute-start.7 = (f32[16,2,16,128]{3,2,1,0:T(8,128)S(1)}, f32[16,2,16,128]{3,2,1,0:T(8,128)S(1)}, u32[]{:S(2)}, u32[]{:S(2)}) collective-permute-start(f32[16,2,16,128]{3,2,1,0:T(8,128)S(1)} %all_to_all.11), channel_id=1, source_target_pairs={{0,16},{16,0},{1,17},{17,1},{2,18},{18,2},{3,19},{19,3},{4,20},{20... | collective-permute-start | bytes 786440 | tf_op jit(solution)/shard_map/ppermute | solution.py:267

commit v5 on v4

--- a/solution.py
+++ b/solution.py
@@ -36,21 +36,20 @@
     return jnp.logical_or(where_ref[1] == SEAM, where_ref[1] == SEAM + 1)
 
 
-def pack_kernel(where_ref, fields_ref, velocity_ref, diffusivity_ref, sent_ref, kept_ref, first_ref, sems):
+def pack_kernel(where_ref, fields_ref, velocity_ref, diffusivity_ref, both_ref, sent_ref, flow_ref, kept_ref, sems):
     core = where_ref[0]
-    sent, kept = (1 - core) * HALF, core * HALF
-    first = jnp.where(at_seam(where_ref), kept, sent)
+    sent = fields_ref.at[0, pl.ds((1 - core) * HALF, HALF)]
     copies = [
         pltpu.make_async_copy(source, target, sems.at[i])
         for i, (source, target) in enumerate(
             [
-                (fields_ref.at[0, pl.ds(first, HALF)], first_ref.at[pl.ds(0, HALF)]),
-                (velocity_ref, first_ref.at[pl.ds(HALF, 3)]),
-                (diffusivity_ref, first_ref.at[HALF + 3]),
-                (fields_ref.at[0, pl.ds(sent, HALF)], sent_ref.at[pl.ds(0, HALF)]),
-                (velocity_ref, sent_ref.at[pl.ds(HALF, 3)]),
-                (diffusivity_ref, sent_ref.at[HALF + 3]),
-                (fields_ref.at[0, pl.ds(kept, HALF)], kept_ref),
+                (sent, sent_ref),
+                (velocity_ref, flow_ref.at[pl.ds(0, 3)]),
+                (diffusivity_ref, flow_ref.at[3]),
+                (sent, both_ref.at[pl.ds(0, HALF)]),
+                (velocity_ref, both_ref.at[pl.ds(HALF, 3)]),
+                (diffusivity_ref, both_ref.at[HALF + 3]),
+                (fields_ref.at[0, pl.ds(core * HALF, HALF)], kept_ref),
             ]
         )
     ]
@@ -61,12 +60,12 @@
 
 
 def pack(where, *arrays):
-    sent = jax.ShapeDtypeStruct((HALF + 4, X, NZ, NY), jnp.float32)
+    channels = (HALF + 4, HALF, 4, HALF)
     return pl.pallas_call(
         pack_kernel,
-        out_shape=(sent, jax.ShapeDtypeStruct((HALF, X, NZ, NY), jnp.float32), sent),
+        out_shape=tuple(jax.ShapeDtypeStruct((n, X, NZ, NY), jnp.float32) for n in channels),
         in_specs=[SMEM] + [pl.BlockSpec(memory_space=pltpu.HBM)] * 3,
-        out_specs=(VMEM, VMEM, VMEM),
+        out_specs=(VMEM,) * 4,
         scratch_shapes=[pltpu.SemaphoreType.DMA((7,))],
         compiler_params=LIMIT,
         name="pack",
@@ -96,8 +95,8 @@
 
 def coefficients(noise_ref, layer, coef_ref):
     for i in range(1, 3 * X - 1):
-        diff = layer(HALF + 3, i)
-        vx, vy, vz = layer(HALF, i), layer(HALF + 1, i), layer(HALF + 2, i)
+        diff = layer(3, i)
+        vx, vy, vz = layer(0, i), layer(1, i), layer(2, i)
         stir = jnp.sqrt(2.0 * diff)
         center = 1.0 - 6.0 * diff
         for k in range(SUBSTEPS):
@@ -132,13 +131,13 @@
     lax.fori_loop(0, HALF // TOGETHER, some, 0)
 
 
-def sent_kernel(_, where_ref, noise_ref, own_ref, first_ref, far_ref, inner_ref, out_ref, coef_ref):
+def sent_kernel(where_ref, noise_ref, own_ref, first_ref, flow_ref, inner_ref, crossed_ref, out_ref, coef_ref):
     slab = where_ref[1]
     ends = jnp.logical_or(slab == 0, slab == 2 * SEAM + 1)
-    outer = Chosen(at_seam(where_ref), far_ref, Chosen(ends, None, first_ref))
-    layer = extended(where_ref, own_ref, inner_ref, outer)
-    coefficients(noise_ref, layer, coef_ref)
-    substeps(layer, coef_ref, out_ref)
+    outer = Chosen(at_seam(where_ref), crossed_ref, Chosen(ends, None, first_ref))
+    flow = pl.ds(HALF, 4)
+    coefficients(noise_ref, extended(where_ref, own_ref.at[flow], inner_ref.at[flow], flow_ref), coef_ref)
+    substeps(extended(where_ref, own_ref, inner_ref, outer), coef_ref, out_ref)
 
 
 def transport_sent(*args):
@@ -148,23 +147,22 @@
             jax.ShapeDtypeStruct((HALF, X, NZ, NY), jnp.float32),
             jax.ShapeDtypeStruct((len(SLOT), 7, NZ, NY), jnp.float32),
         ),
-        in_specs=[pl.BlockSpec(memory_space=pl.ANY), SMEM, SMEM, VMEM, VMEM, VMEM, VMEM],
+        in_specs=[SMEM, SMEM] + [VMEM] * 5,
         out_specs=(VMEM, VMEM),
         compiler_params=LIMIT,
         name="transport_sent",
     )(*args)
 
 
-def kept_kernel(where_ref, own_ref, crossed_ref, inner_ref, outer_ref, coef_ref, out_ref):
-    outer = Chosen(at_seam(where_ref), crossed_ref, outer_ref)
-    substeps(extended(where_ref, own_ref, inner_ref, outer), coef_ref, out_ref)
+def kept_kernel(where_ref, coef_ref, own_ref, inner_ref, outer_ref, out_ref):
+    substeps(extended(where_ref, own_ref, inner_ref, outer_ref), coef_ref, out_ref)
 
 
 def transport_kept(*args):
     return pl.pallas_call(
         kept_kernel,
         out_shape=jax.ShapeDtypeStruct((HALF, X, NZ, NY), jnp.float32),
-        in_specs=[SMEM, VMEM, VMEM, VMEM, VMEM, VMEM],
+        in_specs=[SMEM] + [VMEM] * 4,
         out_specs=VMEM,
         compiler_params=LIMIT,
         name="transport_kept",
@@ -245,19 +243,20 @@
     slabs = lax.axis_size("slab")
     where = jnp.stack([lax.axis_index("field_2"), lax.axis_index("slab")]).astype(jnp.int32)
     inner = [(i, i ^ 1) for i in range(slabs)]
-    outer = [(i, i + 1 if i % 2 else i - 1) for i in range(1, slabs - 1) if i not in (SEAM, SEAM + 1)]
-    send, keep, first = pack(where, fields, velocity, diffusivity)
-    send_outer = lax.ppermute(first, "slab", outer + [(SEAM, slabs - 1), (SEAM + 1, 0)])
-    send_far = lax.ppermute(send, "slab", [(SEAM, SEAM + 1), (SEAM + 1, SEAM)])
-    send_inner = lax.ppermute(send, "slab", inner)
-    halfway = send_outer[:HALF]
-    crossed = lax.ppermute(halfway, "slab", [(slabs - 1, SEAM + 1), (0, SEAM)])
+    outer = [(i, i + 1 if i % 2 else i - 1) for i in range(1, slabs - 1)]
+    near = [p for p in outer if p[0] not in (SEAM, SEAM + 1)]
+    both, send, flow, keep = pack(where, fields, velocity, diffusivity)
+    send_outer = lax.ppermute(send, "slab", near + [(SEAM, 0), (SEAM + 1, slabs - 1)])
+    flow_outer = lax.ppermute(flow, "slab", outer)
+    both_inner = lax.ppermute(both, "slab", inner)
+    crossed = lax.ppermute(send_outer, "slab", [(0, SEAM + 1), (slabs - 1, SEAM)])
     keep_inner = lax.ppermute(keep, "slab", inner)
-    keep_outer = lax.ppermute(keep, "slab", outer)
+    after, _ = lax.optimization_barrier((keep, send_outer))
+    keep_outer = lax.ppermute(after, "slab", outer)
     swap = functools.partial(lax.ppermute, axis_name="field_2", perm=[(0, 1), (1, 0)])
-    sent, coef = transport_sent(halfway, where, noise[0], send, send_outer, send_far, send_inner)
+    sent, coef = transport_sent(where, noise[0], both, send_outer, flow_outer, both_inner, crossed)
     other = swap(sent)
-    kept = transport_kept(where, keep, crossed, keep_inner, keep_outer, coef)
+    kept = transport_kept(where, coef, keep, keep_inner, keep_outer)
     chips = lax.axis_size(CHIPS)
     pair = (kept + other).reshape(chips, -1, NZ, NY)
     parts = lax.all_to_all(pair, CHIPS, 0, 0, tiled=True)

time: 95.8 us -> 83.2 us (0.87)
  blocking collectives: 43.2 us -> 27.1 us
  starting transfers between devices: 33 us -> 35 us
  waiting for transfers between devices: 8.99 us -> 10.4 us
    all_to_all x1, blocking collectives: 30.2 us -> 13.8 us  [per_device(): parts = lax.all_to_all(pair, CHIPS, 0, 0, tiled=True)]
    ppermute x5, starting transfers between devices: 21.6 us -> 25.2 us  [the longest x1 10.7 us: per_device(): lax.ppermute(send, 'slab', near + [(SEAM, 0), (SEAM + 1, slabs - 1)])]
    ppermute x1, starting transfers between devices: 3.36 us -> 1.92 us  [per_device(): keep_inner = lax.ppermute(keep, 'slab', inner)]
    ppermute x5, waiting for transfers between devices: 8 us -> 9.41 us  [the longest x1 5.88 us: per_device(): keep_outer = lax.ppermute(after, 'slab', outer)]
  transfers between devices with their start and end apart: 8 -> 8, of which waited for: 3 -> 4; matrix products, arithmetic and copies ran while one was open for 1% -> 1% of each run, Pallas kernels for 4% -> 5%
where the time goes in v5:
time: 83.2 us; the launch traced here: 82.3 us
  starting transfers between devices  35 us (42%)
  blocking collectives  27.1 us (33%)
  waiting for transfers between devices  10.4 us (12%)
  Pallas kernels  8.42 us (10%)
  local copies, waits for them, and re-layouts  0.89 us (1%)
    all_to_all x1, blocking collectives, per_device(): parts = lax.all_to_all(pair, CHIPS, 0, 0, tiled=True)  13.8 us
    all_to_all x1, blocking collectives, per_device(): mine = lax.all_to_all(spread, CHIPS, 0, 0, tiled=True)  13.3 us
    ppermute x1, starting transfers between devices, per_device(): lax.ppermute(send, 'slab', near + [(SEAM, 0), (SEAM + 1, slabs - 1)])  10.7 us
    ppermute x1, starting transfers between devices, per_device(): keep_outer = lax.ppermute(after, 'slab', outer)  7.43 us
    ppermute x1, waiting for transfers between devices, per_device(): keep_outer = lax.ppermute(after, 'slab', outer)  5.88 us
    ppermute x1, starting transfers between devices, per_device(): swap(mine)  4.4 us
    ppermute x1, starting transfers between devices, per_device(): flow_outer = lax.ppermute(flow, 'slab', outer)  3.85 us
    ppermute x1, starting transfers between devices, per_device(): other = swap(sent)  3.54 us
  transfers between devices with their start and end apart: 8, of which 4 were waited for; matrix products, arithmetic and copies ran while one was open for 1% of the time, Pallas kernels for 5%

profile of v5, /device:TPU:57, one launch (start us, length us, event | category | flops | bytes accessed | tf_op | source)
XLA Modules:
  0.0 82.3 jit_solution(3269032523856227109)
XLA Ops:
  0.0 0.1 pad_add_fusion.where_ref
  0.1 1.8 %pack.1 = (f32[12,4,16,128]{3,2,1,0:T(8,128)S(1)}, f32[8,4,16,128]{3,2,1,0:T(8,128)S(1)}, f32[4,4,16,128]{3,2,1,0:T(8,128)S(1)}, f32[8,4,16,128]{3,2,1,0:T(8,128)S(1)}) custom-call(s32[2]{0:T(128)S(1)} %pad_add_fusion.where_ref, f32[1,16,4,16,128]{4,3,2,1,0:T(8,128)} %fields_ref.1, f32[3,4,16,128]{3,2,1,0:T(8,128)} %velocity_ref.1, f32[4,16,128]{2,1,0:T(8,128)} %diffusivity_ref.1), custom_call_target="tpu_custom_call" | custom-call | tf_op jit(solution)/shard_map/pack/pallas_call | solution.py:64
  1.9 10.7 %collective-permute-start = (f32[8,4,16,128]{3,2,1,0:T(8,128)S(1)}, f32[8,4,16,128]{3,2,1,0:T(8,128)S(1)}, u32[]{:S(2)}, u32[]{:S(2)}) collective-permute-start(f32[8,4,16,128]{3,2,1,0:T(8,128)S(1)} %get-tuple-element.13), channel_id=1, source_target_pairs={{1,2},{2,1},{3,4},{4,3},{5,6},{6,5},{9,10},{10,9},{11,12},{12,11},... | collective-permute-start | bytes 786440 | tf_op jit(solution)/shard_map/ppermute | solution.py:249
  12.6 1.9 %collective-permute-start.2 = (f32[12,4,16,128]{3,2,1,0:T(8,128)S(1)}, f32[12,4,16,128]{3,2,1,0:T(8,128)S(1)}, u32[]{:S(2)}, u32[]{:S(2)}) collective-permute-start(f32[12,4,16,128]{3,2,1,0:T(8,128)S(1)} %get-tuple-element.12.own_ref), channel_id=1, source_target_pairs={{0,1},{1,0},{2,3},{3,2},{4,5},{5,4},{6,7},{7,6},{8,9},{9,8},{10,11... | collective-permute-start | bytes 1179656 | tf_op jit(solution)/shard_map/ppermute | solution.py:251
  14.5 3.0 %collective-permute-done.first_ref = f32[8,4,16,128]{3,2,1,0:T(8,128)S(1)} collective-permute-done((f32[8,4,16,128]{3,2,1,0:T(8,128)S(1)}, f32[8,4,16,128]{3,2,1,0:T(8,128)S(1)}, u32[]{:S(2)}, u32[]{:S(2)}) %collective-permute-start) | collective-permute-done | bytes 262176 | tf_op jit(solution)/shard_map/ppermute | solution.py:249
  17.5 1.3 %collective-permute-start.3 = (f32[8,4,16,128]{3,2,1,0:T(8,128)S(1)}, f32[8,4,16,128]{3,2,1,0:T(8,128)S(1)}, u32[]{:S(2)}, u32[]{:S(2)}) collective-permute-start(f32[8,4,16,128]{3,2,1,0:T(8,128)S(1)} %collective-permute-done.first_ref), channel_id=1, source_target_pairs={{0,8},{15,7},{16,24},{31,23},{32,40},{47,39},{48,56},{63,55},{64,7... | collective-permute-start | bytes 786440 | tf_op jit(solution)/shard_map/ppermute | solution.py:252
  18.8 3.9 %collective-permute-start.1 = (f32[4,4,16,128]{3,2,1,0:T(8,128)S(1)}, f32[4,4,16,128]{3,2,1,0:T(8,128)S(1)}, u32[]{:S(2)}, u32[]{:S(2)}) collective-permute-start(f32[4,4,16,128]{3,2,1,0:T(8,128)S(1)} %get-tuple-element.14), channel_id=1, source_target_pairs={{1,2},{2,1},{3,4},{4,3},{5,6},{6,5},{7,8},{8,7},{9,10},{10,9},{11,... | collective-permute-start | bytes 393224 | tf_op jit(solution)/shard_map/ppermute | solution.py:250
  22.7 1.9 %collective-permute-start.4 = (f32[8,4,16,128]{3,2,1,0:T(8,128)S(1)}, f32[8,4,16,128]{3,2,1,0:T(8,128)S(1)}, u32[]{:S(2)}, u32[]{:S(2)}) collective-permute-start(f32[8,4,16,128]{3,2,1,0:T(8,128)S(1)} %get-tuple-element.18.own_ref), channel_id=1, source_target_pairs={{0,1},{1,0},{2,3},{3,2},{4,5},{5,4},{6,7},{7,6},{8,9},{9,8},{10,11... | collective-permute-start | bytes 786440 | tf_op jit(solution)/shard_map/ppermute | solution.py:253
  24.6 0.8 copy.12
  25.4 7.4 %collective-permute-start.5 = (f32[8,4,16,128]{3,2,1,0:T(8,128)S(1)}, f32[8,4,16,128]{3,2,1,0:T(8,128)S(1)}, u32[]{:S(2)}, u32[]{:S(2)}) collective-permute-start(f32[8,4,16,128]{3,2,1,0:T(8,128)S(1)} %get-tuple-element.18.own_ref), channel_id=1, source_target_pairs={{1,2},{2,1},{3,4},{4,3},{5,6},{6,5},{7,8},{8,7},{9,10},{10,9},{11,... | collective-permute-start | bytes 786440 | tf_op jit(solution)/shard_map/ppermute | solution.py:255
  32.8 0.0 collective-permute-done.1.flow_ref
  32.8 0.0 collective-permute-done.2.inner_ref
  32.8 0.5 collective-permute-done.3.crossed_ref
  33.4 2.0 %transport_sent.1 = (f32[8,4,16,128]{3,2,1,0:T(8,128)S(1)}, f32[28,7,16,128]{3,2,1,0:T(8,128)S(1)}) custom-call(s32[2]{0:T(128)S(1)} %pad_add_fusion.where_ref, f32[4,3]{1,0:T(4,128)S(1)} %bitcast.21, f32[12,4,16,128]{3,2,1,0:T(8,128)S(1)} %get-tuple-element.12.own_ref, f32[8,4,16,128]{3,2,1,0:T(8,128)S(1)} %collective-permute-done.first_ref, ...), custom_call_target="tpu_custom_call" | custom-call | tf_op jit(solution)/shard_map/transport_sent/pallas_call | solution.py:144
  35.3 3.5 %collective-permute-start.6 = (f32[8,4,16,128]{3,2,1,0:T(8,128)S(1)}, f32[8,4,16,128]{3,2,1,0:T(8,128)S(1)}, u32[]{:S(2)}, u32[]{:S(2)}) collective-permute-start(f32[8,4,16,128]{3,2,1,0:T(8,128)S(1)} %get-tuple-element.15), channel_id=1, source_target_pairs={{0,16},{16,0},{1,17},{17,1},{2,18},{18,2},{3,19},{19,3},{4,20},{20... | collective-permute-start | bytes 786440 | tf_op jit(solution)/shard_map/ppermute | solution.py:258
  38.9 0.0 collective-permute-done.4.inner_ref
  38.9 5.9 %collective-permute-done.5.outer_ref = f32[8,4,16,128]{3,2,1,0:T(8,128)S(1)} collective-permute-done((f32[8,4,16,128]{3,2,1,0:T(8,128)S(1)}, f32[8,4,16,128]{3,2,1,0:T(8,128)S(1)}, u32[]{:S(2)}, u32[]{:S(2)}) %collective-permute-start.5) | collective-permute-done | bytes 262176 | tf_op jit(solution)/shard_map/ppermute | solution.py:255
  44.8 1.8 %transport_kept.1 = f32[8,4,16,128]{3,2,1,0:T(8,128)S(1)} custom-call(s32[2]{0:T(128)S(1)} %pad_add_fusion.where_ref, f32[28,7,16,128]{3,2,1,0:T(8,128)S(1)} %get-tuple-element.16.coef_ref, f32[8,4,16,128]{3,2,1,0:T(8,128)S(1)} %get-tuple-element.18.own_ref, f32[8,4,16,128]{3,2,1,0:T(8,128)S(1)} %collective-permute-done.4.inner_ref, ...), custom_call_target="tpu_custom_call" | custom-call | tf_op jit(solution)/shard_map/transport_kept/pallas_call | solution.py:162
  46.6 0.0 copy-start.3
  46.6 0.0 copy-start.4
  46.6 0.0 copy-start
  46.6 0.0 copy-start.1
  46.6 0.0 copy-start.2
  46.6 0.0 collective-permute-done.6
  46.7 13.8 %all_to_all.10 = f32[16,2,16,128]{3,2,1,0:T(8,128)S(1)} all-to-all(f32[16,2,16,128]{3,2,1,0:T(8,128)S(1)} %bitcast.22), channel_id=1, replica_groups=mesh['field_0'=4,'field_1'=4,'field_2'=2,'slab'=16] {'field_0','field_1'}, dimensions={0} | all-to-all | bytes 524288 | tf_op jit(solution)/shard_map/all_to_all | solution.py:262
  60.6 13.3 %all_to_all.11 = f32[16,2,16,128]{3,2,1,0:T(8,128)S(1)} all-to-all(f32[16,2,16,128]{3,2,1,0:T(8,128)S(1)} %broadcast_in_dim.2), channel_id=1, replica_groups=mesh['field_0'=4,'field_1'=4,'field_2'=2,'slab'=16] {'field_0','field_1'}, dimensions={0} | all-to-all | bytes 524288 | tf_op jit(solution)/shard_map/all_to_all | solution.py:265
  73.9 4.4 %collective-permute-start.7 = (f32[16,2,16,128]{3,2,1,0:T(8,128)S(1)}, f32[16,2,16,128]{3,2,1,0:T(8,128)S(1)}, u32[]{:S(2)}, u32[]{:S(2)}) collective-permute-start(f32[16,2,16,128]{3,2,1,0:T(8,128)S(1)} %all_to_all.11), channel_id=1, source_target_pairs={{0,16},{16,0},{1,17},{17,1},{2,18},{18,2},{3,19},{19,3},{4,20},{20... | collective-permute-start | bytes 786440 | tf_op jit(solution)/shard_map/ppermute | solution.py:266
  78.3 0.0 copy-done.3
  78.3 0.1 copy.13
  78.4 0.0 copy-done.4
  78.4 0.1 multiply_bitcast_fusion.stoich_ref
  78.5 1.0 %collective-permute-done.7 = f32[16,2,16,128]{3,2,1,0:T(8,128)S(1)} collective-permute-done((f32[16,2,16,128]{3,2,1,0:T(8,128)S(1)}, f32[16,2,16,128]{3,2,1,0:T(8,128)S(1)}, u32[]{:S(2)}, u32[]{:S(2)}) %collective-permute-start.7) | collective-permute-done | bytes 262176 | tf_op jit(solution)/shard_map/ppermute | solution.py:266
  79.5 0.0 copy-done
  79.5 0.0 copy-done.1
  79.5 0.0 copy-done.2
  79.5 2.8 %react.1 = f32[1024,128]{1,0:T(8,128)} custom-call(s32[2]{0:T(128)S(1)} %pad_add_fusion.where_ref, f32[512,128]{1,0:T(8,128)S(1)} %bitcast.16, f32[512,128]{1,0:T(8,128)S(1)} %bitcast.14, f32[512,128]{1,0:T(8,128)S(1)} %bitcast.15, f32[512,128]{1,0:T(8,128)S(1)} %bitcast.17, f32[64,128]{1,0:T(8,128)S(1)} %bitcast.18, f32[64,128]{1,0:T(8,128)S(1)} %bitcast.19, ...), custom_call_target="tpu_custom_call" | custom-call | tf_op jit(solution)/shard_map/react/pallas_call | solution.py:225
  (4 shorter events, 0.1 us)
Async XLA Ops:
  1.9 15.6 %collective-permute-start = (f32[8,4,16,128]{3,2,1,0:T(8,128)S(1)}, f32[8,4,16,128]{3,2,1,0:T(8,128)S(1)}, u32[]{:S(2)}, u32[]{:S(2)}) collective-permute-start(f32[8,4,16,128]{3,2,1,0:T(8,128)S(1)} %get-tuple-element.13), channel_id=1, source_target_pairs={{1,2},{2,1},{3,4},{4,3},{5,6},{6,5},{9,10},{10,9},{11,12},{12,11},... | collective-permute-start | bytes 786440 | tf_op jit(solution)/shard_map/ppermute | solution.py:249
  12.6 20.2 %collective-permute-start.2 = (f32[12,4,16,128]{3,2,1,0:T(8,128)S(1)}, f32[12,4,16,128]{3,2,1,0:T(8,128)S(1)}, u32[]{:S(2)}, u32[]{:S(2)}) collective-permute-start(f32[12,4,16,128]{3,2,1,0:T(8,128)S(1)} %get-tuple-element.12.own_ref), channel_id=1, source_target_pairs={{0,1},{1,0},{2,3},{3,2},{4,5},{5,4},{6,7},{7,6},{8,9},{9,8},{10,11... | collective-permute-start | bytes 1179656 | tf_op jit(solution)/shard_map/ppermute | solution.py:251
  17.5 15.8 %collective-permute-start.3 = (f32[8,4,16,128]{3,2,1,0:T(8,128)S(1)}, f32[8,4,16,128]{3,2,1,0:T(8,128)S(1)}, u32[]{:S(2)}, u32[]{:S(2)}) collective-permute-start(f32[8,4,16,128]{3,2,1,0:T(8,128)S(1)} %collective-permute-done.first_ref), channel_id=1, source_target_pairs={{0,8},{15,7},{16,24},{31,23},{32,40},{47,39},{48,56},{63,55},{64,7... | collective-permute-start | bytes 786440 | tf_op jit(solution)/shard_map/ppermute | solution.py:252
  18.8 14.0 %collective-permute-start.1 = (f32[4,4,16,128]{3,2,1,0:T(8,128)S(1)}, f32[4,4,16,128]{3,2,1,0:T(8,128)S(1)}, u32[]{:S(2)}, u32[]{:S(2)}) collective-permute-start(f32[4,4,16,128]{3,2,1,0:T(8,128)S(1)} %get-tuple-element.14), channel_id=1, source_target_pairs={{1,2},{2,1},{3,4},{4,3},{5,6},{6,5},{7,8},{8,7},{9,10},{10,9},{11,... | collective-permute-start | bytes 393224 | tf_op jit(solution)/shard_map/ppermute | solution.py:250
  22.7 16.2 %collective-permute-start.4 = (f32[8,4,16,128]{3,2,1,0:T(8,128)S(1)}, f32[8,4,16,128]{3,2,1,0:T(8,128)S(1)}, u32[]{:S(2)}, u32[]{:S(2)}) collective-permute-start(f32[8,4,16,128]{3,2,1,0:T(8,128)S(1)} %get-tuple-element.18.own_ref), channel_id=1, source_target_pairs={{0,1},{1,0},{2,3},{3,2},{4,5},{5,4},{6,7},{7,6},{8,9},{9,8},{10,11... | collective-permute-start | bytes 786440 | tf_op jit(solution)/shard_map/ppermute | solution.py:253
  25.4 19.4 %collective-permute-start.5 = (f32[8,4,16,128]{3,2,1,0:T(8,128)S(1)}, f32[8,4,16,128]{3,2,1,0:T(8,128)S(1)}, u32[]{:S(2)}, u32[]{:S(2)}) collective-permute-start(f32[8,4,16,128]{3,2,1,0:T(8,128)S(1)} %get-tuple-element.18.own_ref), channel_id=1, source_target_pairs={{1,2},{2,1},{3,4},{4,3},{5,6},{6,5},{7,8},{8,7},{9,10},{10,9},{11,... | collective-permute-start | bytes 786440 | tf_op jit(solution)/shard_map/ppermute | solution.py:255
  35.3 11.3 %collective-permute-start.6 = (f32[8,4,16,128]{3,2,1,0:T(8,128)S(1)}, f32[8,4,16,128]{3,2,1,0:T(8,128)S(1)}, u32[]{:S(2)}, u32[]{:S(2)}) collective-permute-start(f32[8,4,16,128]{3,2,1,0:T(8,128)S(1)} %get-tuple-element.15), channel_id=1, source_target_pairs={{0,16},{16,0},{1,17},{17,1},{2,18},{18,2},{3,19},{19,3},{4,20},{20... | collective-permute-start | bytes 786440 | tf_op jit(solution)/shard_map/ppermute | solution.py:258
  46.6 31.7 %copy-start.3 = (f32[16,32]{1,0:T(8,128)S(1)}, f32[16,32]{1,0:T(8,128)}, u32[]{:S(2)}) copy-start(f32[16,32]{1,0:T(8,128)} %param.16) | copy-start | bytes 6148
  46.6 31.8 %copy-start.4 = (f32[32]{0:T(128)S(1)}, f32[32]{0:T(128)}, u32[]{:S(2)}) copy-start(f32[32]{0:T(128)} %param.17) | copy-start | bytes 388
  46.6 32.8 %copy-start = (f32[4,16,128]{2,1,0:T(8,128)S(1)}, f32[4,16,128]{2,1,0:T(8,128)}, u32[]{:S(2)}) copy-start(f32[4,16,128]{2,1,0:T(8,128)} %param.13) | copy-start | bytes 98308
  46.6 32.8 %copy-start.1 = (f32[4,16,128]{2,1,0:T(8,128)S(1)}, f32[4,16,128]{2,1,0:T(8,128)}, u32[]{:S(2)}) copy-start(f32[4,16,128]{2,1,0:T(8,128)} %param.14) | copy-start | bytes 98308
  46.6 32.8 %copy-start.2 = (f32[32,16]{0,1:T(8,128)S(1)}, f32[32,16]{0,1:T(8,128)}, u32[]{:S(2)}) copy-start(f32[32,16]{0,1:T(8,128)} %param.15) | copy-start | bytes 6148
  73.9 5.5 %collective-permute-start.7 = (f32[16,2,16,128]{3,2,1,0:T(8,128)S(1)}, f32[16,2,16,128]{3,2,1,0:T(8,128)S(1)}, u32[]{:S(2)}, u32[]{:S(2)}) collective-permute-start(f32[16,2,16,128]{3,2,1,0:T(8,128)S(1)} %all_to_all.11), channel_id=1, source_target_pairs={{0,16},{16,0},{1,17},{17,1},{2,18},{18,2},{3,19},{19,3},{4,20},{20... | collective-permute-start | bytes 786440 | tf_op jit(solution)/shard_map/ppermute | solution.py:266

commit v6 on v5

--- a/solution.py
+++ b/solution.py
@@ -36,19 +36,15 @@
     return jnp.logical_or(where_ref[1] == SEAM, where_ref[1] == SEAM + 1)
 
 
-def pack_kernel(where_ref, fields_ref, velocity_ref, diffusivity_ref, both_ref, sent_ref, flow_ref, kept_ref, sems):
+def pack_kernel(where_ref, fields_ref, velocity_ref, diffusivity_ref, sent_ref, kept_ref, sems):
     core = where_ref[0]
-    sent = fields_ref.at[0, pl.ds((1 - core) * HALF, HALF)]
     copies = [
         pltpu.make_async_copy(source, target, sems.at[i])
         for i, (source, target) in enumerate(
             [
-                (sent, sent_ref),
-                (velocity_ref, flow_ref.at[pl.ds(0, 3)]),
-                (diffusivity_ref, flow_ref.at[3]),
-                (sent, both_ref.at[pl.ds(0, HALF)]),
-                (velocity_ref, both_ref.at[pl.ds(HALF, 3)]),
-                (diffusivity_ref, both_ref.at[HALF + 3]),
+                (fields_ref.at[0, pl.ds((1 - core) * HALF, HALF)], sent_ref.at[pl.ds(0, HALF)]),
+                (velocity_ref, sent_ref.at[pl.ds(HALF, 3)]),
+                (diffusivity_ref, sent_ref.at[HALF + 3]),
                 (fields_ref.at[0, pl.ds(core * HALF, HALF)], kept_ref),
             ]
         )
@@ -60,13 +56,12 @@
 
 
 def pack(where, *arrays):
-    channels = (HALF + 4, HALF, 4, HALF)
     return pl.pallas_call(
         pack_kernel,
-        out_shape=tuple(jax.ShapeDtypeStruct((n, X, NZ, NY), jnp.float32) for n in channels),
+        out_shape=tuple(jax.ShapeDtypeStruct((n, X, NZ, NY), jnp.float32) for n in (HALF + 4, HALF)),
         in_specs=[SMEM] + [pl.BlockSpec(memory_space=pltpu.HBM)] * 3,
-        out_specs=(VMEM,) * 4,
-        scratch_shapes=[pltpu.SemaphoreType.DMA((7,))],
+        out_specs=(VMEM, VMEM),
+        scratch_shapes=[pltpu.SemaphoreType.DMA((4,))],
         compiler_params=LIMIT,
         name="pack",
     )(where, *(pltpu.with_memory_space_constraint(x, pltpu.HBM) for x in arrays))
@@ -95,8 +90,8 @@
 
 def coefficients(noise_ref, layer, coef_ref):
     for i in range(1, 3 * X - 1):
-        diff = layer(3, i)
-        vx, vy, vz = layer(0, i), layer(1, i), layer(2, i)
+        diff = layer(HALF + 3, i)
+        vx, vy, vz = layer(HALF, i), layer(HALF + 1, i), layer(HALF + 2, i)
         stir = jnp.sqrt(2.0 * diff)
         center = 1.0 - 6.0 * diff
         for k in range(SUBSTEPS):
@@ -131,13 +126,13 @@
     lax.fori_loop(0, HALF // TOGETHER, some, 0)
 
 
-def sent_kernel(where_ref, noise_ref, own_ref, first_ref, flow_ref, inner_ref, crossed_ref, out_ref, coef_ref):
+def sent_kernel(where_ref, noise_ref, own_ref, first_ref, inner_ref, crossed_ref, out_ref, coef_ref):
     slab = where_ref[1]
     ends = jnp.logical_or(slab == 0, slab == 2 * SEAM + 1)
     outer = Chosen(at_seam(where_ref), crossed_ref, Chosen(ends, None, first_ref))
-    flow = pl.ds(HALF, 4)
-    coefficients(noise_ref, extended(where_ref, own_ref.at[flow], inner_ref.at[flow], flow_ref), coef_ref)
-    substeps(extended(where_ref, own_ref, inner_ref, outer), coef_ref, out_ref)
+    layer = extended(where_ref, own_ref, inner_ref, outer)
+    coefficients(noise_ref, layer, coef_ref)
+    substeps(layer, coef_ref, out_ref)
 
 
 def transport_sent(*args):
@@ -147,14 +142,14 @@
             jax.ShapeDtypeStruct((HALF, X, NZ, NY), jnp.float32),
             jax.ShapeDtypeStruct((len(SLOT), 7, NZ, NY), jnp.float32),
         ),
-        in_specs=[SMEM, SMEM] + [VMEM] * 5,
+        in_specs=[SMEM, SMEM] + [VMEM] * 4,
         out_specs=(VMEM, VMEM),
         compiler_params=LIMIT,
         name="transport_sent",
     )(*args)
 
 
-def kept_kernel(where_ref, coef_ref, own_ref, inner_ref, outer_ref, out_ref):
+def kept_kernel(where_ref, coef_ref, own_ref, outer_ref, inner_ref, out_ref):
     substeps(extended(where_ref, own_ref, inner_ref, outer_ref), coef_ref, out_ref)
 
 
@@ -245,18 +240,17 @@
     inner = [(i, i ^ 1) for i in range(slabs)]
     outer = [(i, i + 1 if i % 2 else i - 1) for i in range(1, slabs - 1)]
     near = [p for p in outer if p[0] not in (SEAM, SEAM + 1)]
-    both, send, flow, keep = pack(where, fields, velocity, diffusivity)
+    send, keep = pack(where, fields, velocity, diffusivity)
     send_outer = lax.ppermute(send, "slab", near + [(SEAM, 0), (SEAM + 1, slabs - 1)])
-    flow_outer = lax.ppermute(flow, "slab", outer)
-    both_inner = lax.ppermute(both, "slab", inner)
+    send_inner = lax.ppermute(send, "slab", inner)
     crossed = lax.ppermute(send_outer, "slab", [(0, SEAM + 1), (slabs - 1, SEAM)])
-    keep_inner = lax.ppermute(keep, "slab", inner)
     after, _ = lax.optimization_barrier((keep, send_outer))
     keep_outer = lax.ppermute(after, "slab", outer)
+    keep_inner = lax.ppermute(keep, "slab", inner)
     swap = functools.partial(lax.ppermute, axis_name="field_2", perm=[(0, 1), (1, 0)])
-    sent, coef = transport_sent(where, noise[0], both, send_outer, flow_outer, both_inner, crossed)
+    sent, coef = transport_sent(where, noise[0], send, send_outer, send_inner, crossed)
     other = swap(sent)
-    kept = transport_kept(where, coef, keep, keep_inner, keep_outer)
+    kept = transport_kept(where, coef, keep, keep_outer, keep_inner)
     chips = lax.axis_size(CHIPS)
     pair = (kept + other).reshape(chips, -1, NZ, NY)
     parts = lax.all_to_all(pair, CHIPS, 0, 0, tiled=True)

time: 83.2 us -> 88 us (1.058)
  blocking collectives: 27.1 us -> 33 us
  starting transfers between devices: 35 us -> 30.1 us
  waiting for transfers between devices: 10.4 us -> 13.8 us
    ppermute x1, waiting for transfers between devices: 0.51 us -> 6.98 us  [per_device(): lax.ppermute(send_outer, 'slab', [(0, SEAM + 1), (slabs - 1, SEAM)])]
    all_to_all x1, blocking collectives: 13.8 us -> 19.8 us  [per_device(): parts = lax.all_to_all(pair, CHIPS, 0, 0, tiled=True)]
    ppermute x1, waiting for transfers between devices: 5.88 us -> 0.01 us  [per_device(): keep_outer = lax.ppermute(after, 'slab', outer)]
    ppermute x2 -> x1, starting transfers between devices: 5.78 us -> 1.92 us  [per_device(): send_inner = lax.ppermute(send, 'slab', inner)]
    ppermute x1, waiting for transfers between devices: 3.01 us -> 5.81 us  [per_device(): lax.ppermute(send, 'slab', near + [(SEAM, 0), (SEAM + 1, slabs - 1)])]
    ppermute x1, starting transfers between devices: 7.43 us -> 5.99 us  [per_device(): keep_outer = lax.ppermute(after, 'slab', outer)]
    ppermute x1, starting transfers between devices: 3.54 us -> 4.52 us  [per_device(): other = swap(sent)]
  transfers between devices with their start and end apart: 8 -> 7, of which waited for: 4 -> 3; matrix products, arithmetic and copies ran while one was open for 1% -> 1% of each run, Pallas kernels for 5% -> 4%
where the time goes in v6:
time: 88 us; the launch traced here: 86.4 us
  blocking collectives  33 us (38%)
  starting transfers between devices  30.1 us (34%)
  waiting for transfers between devices  13.8 us (16%)
  Pallas kernels  8.26 us (9%)
  local copies, waits for them, and re-layouts  0.89 us (1%)
    all_to_all x1, blocking collectives, per_device(): parts = lax.all_to_all(pair, CHIPS, 0, 0, tiled=True)  19.8 us
    all_to_all x1, blocking collectives, per_device(): mine = lax.all_to_all(spread, CHIPS, 0, 0, tiled=True)  13.1 us
    ppermute x1, starting transfers between devices, per_device(): lax.ppermute(send, 'slab', near + [(SEAM, 0), (SEAM + 1, slabs - 1)])  10.7 us
    ppermute x1, waiting for transfers between devices, per_device(): lax.ppermute(send_outer, 'slab', [(0, SEAM + 1), (slabs - 1, SEAM)])  6.98 us
    ppermute x1, starting transfers between devices, per_device(): keep_outer = lax.ppermute(after, 'slab', outer)  5.99 us
    ppermute x1, waiting for transfers between devices, per_device(): lax.ppermute(send, 'slab', near + [(SEAM, 0), (SEAM + 1, slabs - 1)])  5.81 us
    ppermute x1, starting transfers between devices, per_device(): other = swap(sent)  4.52 us
    ppermute x1, starting transfers between devices, per_device(): swap(mine)  3.79 us
  transfers between devices with their start and end apart: 7, of which 3 were waited for; matrix products, arithmetic and copies ran while one was open for 1% of the time, Pallas kernels for 4%

profile of v6, /device:TPU:57, one launch (start us, length us, event | category | flops | bytes accessed | tf_op | source)
XLA Modules:
  0.0 86.4 jit_solution(13133404541486474601)
XLA Ops:
  0.0 0.1 pad_add_fusion.where_ref
  0.1 1.7 %pack.1 = (f32[12,4,16,128]{3,2,1,0:T(8,128)S(1)}, f32[8,4,16,128]{3,2,1,0:T(8,128)S(1)}) custom-call(s32[2]{0:T(128)S(1)} %pad_add_fusion.where_ref, f32[1,16,4,16,128]{4,3,2,1,0:T(8,128)} %fields_ref.1, f32[3,4,16,128]{3,2,1,0:T(8,128)} %velocity_ref.1, f32[4,16,128]{2,1,0:T(8,128)} %diffusivity_ref.1), custom_call_target="tpu_custom_call" | custom-call | tf_op jit(solution)/shard_map/pack/pallas_call | solution.py:59
  1.8 10.7 %collective-permute-start = (f32[12,4,16,128]{3,2,1,0:T(8,128)S(1)}, f32[12,4,16,128]{3,2,1,0:T(8,128)S(1)}, u32[]{:S(2)}, u32[]{:S(2)}) collective-permute-start(f32[12,4,16,128]{3,2,1,0:T(8,128)S(1)} %get-tuple-element.10.own_ref), channel_id=1, source_target_pairs={{1,2},{2,1},{3,4},{4,3},{5,6},{6,5},{9,10},{10,9},{11,12},{12,11},... | collective-permute-start | bytes 1179656 | tf_op jit(solution)/shard_map/ppermute | solution.py:244
  12.5 1.9 %collective-permute-start.1 = (f32[12,4,16,128]{3,2,1,0:T(8,128)S(1)}, f32[12,4,16,128]{3,2,1,0:T(8,128)S(1)}, u32[]{:S(2)}, u32[]{:S(2)}) collective-permute-start(f32[12,4,16,128]{3,2,1,0:T(8,128)S(1)} %get-tuple-element.10.own_ref), channel_id=1, source_target_pairs={{0,1},{1,0},{2,3},{3,2},{4,5},{5,4},{6,7},{7,6},{8,9},{9,8},{10,11... | collective-permute-start | bytes 1179656 | tf_op jit(solution)/shard_map/ppermute | solution.py:245
  14.4 5.8 %collective-permute-done.first_ref = f32[12,4,16,128]{3,2,1,0:T(8,128)S(1)} collective-permute-done((f32[12,4,16,128]{3,2,1,0:T(8,128)S(1)}, f32[12,4,16,128]{3,2,1,0:T(8,128)S(1)}, u32[]{:S(2)}, u32[]{:S(2)}) %collective-permute-start) | collective-permute-done | bytes 393248 | tf_op jit(solution)/shard_map/ppermute | solution.py:244
  20.2 1.3 %collective-permute-start.2 = (f32[12,4,16,128]{3,2,1,0:T(8,128)S(1)}, f32[12,4,16,128]{3,2,1,0:T(8,128)S(1)}, u32[]{:S(2)}, u32[]{:S(2)}) collective-permute-start(f32[12,4,16,128]{3,2,1,0:T(8,128)S(1)} %collective-permute-done.first_ref), channel_id=1, source_target_pairs={{0,8},{15,7},{16,24},{31,23},{32,40},{47,39},{48,56},{63,55},{64,7... | collective-permute-start | bytes 1179656 | tf_op jit(solution)/shard_map/ppermute | solution.py:246
  21.5 1.9 %collective-permute-start.4 = (f32[8,4,16,128]{3,2,1,0:T(8,128)S(1)}, f32[8,4,16,128]{3,2,1,0:T(8,128)S(1)}, u32[]{:S(2)}, u32[]{:S(2)}) collective-permute-start(f32[8,4,16,128]{3,2,1,0:T(8,128)S(1)} %get-tuple-element.14.own_ref), channel_id=1, source_target_pairs={{0,1},{1,0},{2,3},{3,2},{4,5},{5,4},{6,7},{7,6},{8,9},{9,8},{10,11... | collective-permute-start | bytes 786440 | tf_op jit(solution)/shard_map/ppermute | solution.py:249
  23.4 0.8 copy.12
  24.2 6.0 %collective-permute-start.3 = (f32[8,4,16,128]{3,2,1,0:T(8,128)S(1)}, f32[8,4,16,128]{3,2,1,0:T(8,128)S(1)}, u32[]{:S(2)}, u32[]{:S(2)}) collective-permute-start(f32[8,4,16,128]{3,2,1,0:T(8,128)S(1)} %get-tuple-element.14.own_ref), channel_id=1, source_target_pairs={{1,2},{2,1},{3,4},{4,3},{5,6},{6,5},{7,8},{8,7},{9,10},{10,9},{11,... | collective-permute-start | bytes 786440 | tf_op jit(solution)/shard_map/ppermute | solution.py:248
  30.2 0.0 collective-permute-done.1.inner_ref
  30.2 7.0 %collective-permute-done.2.crossed_ref = f32[12,4,16,128]{3,2,1,0:T(8,128)S(1)} collective-permute-done((f32[12,4,16,128]{3,2,1,0:T(8,128)S(1)}, f32[12,4,16,128]{3,2,1,0:T(8,128)S(1)}, u32[]{:S(2)}, u32[]{:S(2)}) %collective-permute-start.2) | collective-permute-done | bytes 393248 | tf_op jit(solution)/shard_map/ppermute | solution.py:246
  37.2 2.0 %transport_sent.1 = (f32[8,4,16,128]{3,2,1,0:T(8,128)S(1)}, f32[28,7,16,128]{3,2,1,0:T(8,128)S(1)}) custom-call(s32[2]{0:T(128)S(1)} %pad_add_fusion.where_ref, f32[4,3]{1,0:T(4,128)S(1)} %bitcast.21, f32[12,4,16,128]{3,2,1,0:T(8,128)S(1)} %get-tuple-element.10.own_ref, f32[12,4,16,128]{3,2,1,0:T(8,128)S(1)} %collective-permute-done.first_ref, ...), custom_call_target="tpu_custom_call" | custom-call | tf_op jit(solution)/shard_map/transport_sent/pallas_call | solution.py:139
  39.2 4.5 %collective-permute-start.5 = (f32[8,4,16,128]{3,2,1,0:T(8,128)S(1)}, f32[8,4,16,128]{3,2,1,0:T(8,128)S(1)}, u32[]{:S(2)}, u32[]{:S(2)}) collective-permute-start(f32[8,4,16,128]{3,2,1,0:T(8,128)S(1)} %get-tuple-element.11), channel_id=1, source_target_pairs={{0,16},{16,0},{1,17},{17,1},{2,18},{18,2},{3,19},{19,3},{4,20},{20... | collective-permute-start | bytes 786440 | tf_op jit(solution)/shard_map/ppermute | solution.py:252
  43.7 0.0 collective-permute-done.4.inner_ref
  43.7 0.0 collective-permute-done.3.outer_ref
  43.7 1.8 %transport_kept.1 = f32[8,4,16,128]{3,2,1,0:T(8,128)S(1)} custom-call(s32[2]{0:T(128)S(1)} %pad_add_fusion.where_ref, f32[28,7,16,128]{3,2,1,0:T(8,128)S(1)} %get-tuple-element.12.coef_ref, f32[8,4,16,128]{3,2,1,0:T(8,128)S(1)} %get-tuple-element.14.own_ref, f32[8,4,16,128]{3,2,1,0:T(8,128)S(1)} %collective-permute-done.3.outer_ref, ...), custom_call_target="tpu_custom_call" | custom-call | tf_op jit(solution)/shard_map/transport_kept/pallas_call | solution.py:157
  45.5 0.0 copy-start.3
  45.5 0.0 copy-start.4
  45.5 0.0 copy-start
  45.5 0.0 copy-start.1
  45.6 0.0 copy-start.2
  45.6 0.0 collective-permute-done.5
  45.6 19.8 %all_to_all.10 = f32[16,2,16,128]{3,2,1,0:T(8,128)S(1)} all-to-all(f32[16,2,16,128]{3,2,1,0:T(8,128)S(1)} %bitcast.22), channel_id=1, replica_groups=mesh['field_0'=4,'field_1'=4,'field_2'=2,'slab'=16] {'field_0','field_1'}, dimensions={0} | all-to-all | bytes 524288 | tf_op jit(solution)/shard_map/all_to_all | solution.py:256
  65.5 13.1 %all_to_all.11 = f32[16,2,16,128]{3,2,1,0:T(8,128)S(1)} all-to-all(f32[16,2,16,128]{3,2,1,0:T(8,128)S(1)} %broadcast_in_dim.2), channel_id=1, replica_groups=mesh['field_0'=4,'field_1'=4,'field_2'=2,'slab'=16] {'field_0','field_1'}, dimensions={0} | all-to-all | bytes 524288 | tf_op jit(solution)/shard_map/all_to_all | solution.py:259
  78.6 3.8 %collective-permute-start.6 = (f32[16,2,16,128]{3,2,1,0:T(8,128)S(1)}, f32[16,2,16,128]{3,2,1,0:T(8,128)S(1)}, u32[]{:S(2)}, u32[]{:S(2)}) collective-permute-start(f32[16,2,16,128]{3,2,1,0:T(8,128)S(1)} %all_to_all.11), channel_id=1, source_target_pairs={{0,16},{16,0},{1,17},{17,1},{2,18},{18,2},{3,19},{19,3},{4,20},{20... | collective-permute-start | bytes 786440 | tf_op jit(solution)/shard_map/ppermute | solution.py:260
  82.4 0.0 copy-done.3
  82.4 0.1 copy.13
  82.5 0.0 copy-done.4
  82.5 0.1 multiply_bitcast_fusion.stoich_ref
  82.6 1.0 %collective-permute-done.6 = f32[16,2,16,128]{3,2,1,0:T(8,128)S(1)} collective-permute-done((f32[16,2,16,128]{3,2,1,0:T(8,128)S(1)}, f32[16,2,16,128]{3,2,1,0:T(8,128)S(1)}, u32[]{:S(2)}, u32[]{:S(2)}) %collective-permute-start.6) | collective-permute-done | bytes 262176 | tf_op jit(solution)/shard_map/ppermute | solution.py:260
  83.6 0.0 copy-done
  83.6 0.0 copy-done.1
  83.6 0.0 copy-done.2
  83.6 2.8 %react.1 = f32[1024,128]{1,0:T(8,128)} custom-call(s32[2]{0:T(128)S(1)} %pad_add_fusion.where_ref, f32[512,128]{1,0:T(8,128)S(1)} %bitcast.16, f32[512,128]{1,0:T(8,128)S(1)} %bitcast.14, f32[512,128]{1,0:T(8,128)S(1)} %bitcast.15, f32[512,128]{1,0:T(8,128)S(1)} %bitcast.17, f32[64,128]{1,0:T(8,128)S(1)} %bitcast.18, f32[64,128]{1,0:T(8,128)S(1)} %bitcast.19, ...), custom_call_target="tpu_custom_call" | custom-call | tf_op jit(solution)/shard_map/react/pallas_call | solution.py:220
  (4 shorter events, 0.1 us)
Async XLA Ops:
  1.8 18.4 %collective-permute-start = (f32[12,4,16,128]{3,2,1,0:T(8,128)S(1)}, f32[12,4,16,128]{3,2,1,0:T(8,128)S(1)}, u32[]{:S(2)}, u32[]{:S(2)}) collective-permute-start(f32[12,4,16,128]{3,2,1,0:T(8,128)S(1)} %get-tuple-element.10.own_ref), channel_id=1, source_target_pairs={{1,2},{2,1},{3,4},{4,3},{5,6},{6,5},{9,10},{10,9},{11,12},{12,11},... | collective-permute-start | bytes 1179656 | tf_op jit(solution)/shard_map/ppermute | solution.py:244
  12.5 17.7 %collective-permute-start.1 = (f32[12,4,16,128]{3,2,1,0:T(8,128)S(1)}, f32[12,4,16,128]{3,2,1,0:T(8,128)S(1)}, u32[]{:S(2)}, u32[]{:S(2)}) collective-permute-start(f32[12,4,16,128]{3,2,1,0:T(8,128)S(1)} %get-tuple-element.10.own_ref), channel_id=1, source_target_pairs={{0,1},{1,0},{2,3},{3,2},{4,5},{5,4},{6,7},{7,6},{8,9},{9,8},{10,11... | collective-permute-start | bytes 1179656 | tf_op jit(solution)/shard_map/ppermute | solution.py:245
  20.2 17.0 %collective-permute-start.2 = (f32[12,4,16,128]{3,2,1,0:T(8,128)S(1)}, f32[12,4,16,128]{3,2,1,0:T(8,128)S(1)}, u32[]{:S(2)}, u32[]{:S(2)}) collective-permute-start(f32[12,4,16,128]{3,2,1,0:T(8,128)S(1)} %collective-permute-done.first_ref), channel_id=1, source_target_pairs={{0,8},{15,7},{16,24},{31,23},{32,40},{47,39},{48,56},{63,55},{64,7... | collective-permute-start | bytes 1179656 | tf_op jit(solution)/shard_map/ppermute | solution.py:246
  21.5 22.2 %collective-permute-start.4 = (f32[8,4,16,128]{3,2,1,0:T(8,128)S(1)}, f32[8,4,16,128]{3,2,1,0:T(8,128)S(1)}, u32[]{:S(2)}, u32[]{:S(2)}) collective-permute-start(f32[8,4,16,128]{3,2,1,0:T(8,128)S(1)} %get-tuple-element.14.own_ref), channel_id=1, source_target_pairs={{0,1},{1,0},{2,3},{3,2},{4,5},{5,4},{6,7},{7,6},{8,9},{9,8},{10,11... | collective-permute-start | bytes 786440 | tf_op jit(solution)/shard_map/ppermute | solution.py:249
  24.2 19.5 %collective-permute-start.3 = (f32[8,4,16,128]{3,2,1,0:T(8,128)S(1)}, f32[8,4,16,128]{3,2,1,0:T(8,128)S(1)}, u32[]{:S(2)}, u32[]{:S(2)}) collective-permute-start(f32[8,4,16,128]{3,2,1,0:T(8,128)S(1)} %get-tuple-element.14.own_ref), channel_id=1, source_target_pairs={{1,2},{2,1},{3,4},{4,3},{5,6},{6,5},{7,8},{8,7},{9,10},{10,9},{11,... | collective-permute-start | bytes 786440 | tf_op jit(solution)/shard_map/ppermute | solution.py:248
  39.2 6.4 %collective-permute-start.5 = (f32[8,4,16,128]{3,2,1,0:T(8,128)S(1)}, f32[8,4,16,128]{3,2,1,0:T(8,128)S(1)}, u32[]{:S(2)}, u32[]{:S(2)}) collective-permute-start(f32[8,4,16,128]{3,2,1,0:T(8,128)S(1)} %get-tuple-element.11), channel_id=1, source_target_pairs={{0,16},{16,0},{1,17},{17,1},{2,18},{18,2},{3,19},{19,3},{4,20},{20... | collective-permute-start | bytes 786440 | tf_op jit(solution)/shard_map/ppermute | solution.py:252
  45.5 36.9 %copy-start.3 = (f32[16,32]{1,0:T(8,128)S(1)}, f32[16,32]{1,0:T(8,128)}, u32[]{:S(2)}) copy-start(f32[16,32]{1,0:T(8,128)} %param.16) | copy-start | bytes 6148
  45.5 37.0 %copy-start.4 = (f32[32]{0:T(128)S(1)}, f32[32]{0:T(128)}, u32[]{:S(2)}) copy-start(f32[32]{0:T(128)} %param.17) | copy-start | bytes 388
  45.5 38.0 %copy-start = (f32[4,16,128]{2,1,0:T(8,128)S(1)}, f32[4,16,128]{2,1,0:T(8,128)}, u32[]{:S(2)}) copy-start(f32[4,16,128]{2,1,0:T(8,128)} %param.13) | copy-start | bytes 98308
  45.5 38.0 %copy-start.1 = (f32[4,16,128]{2,1,0:T(8,128)S(1)}, f32[4,16,128]{2,1,0:T(8,128)}, u32[]{:S(2)}) copy-start(f32[4,16,128]{2,1,0:T(8,128)} %param.14) | copy-start | bytes 98308
  45.6 38.0 %copy-start.2 = (f32[32,16]{0,1:T(8,128)S(1)}, f32[32,16]{0,1:T(8,128)}, u32[]{:S(2)}) copy-start(f32[32,16]{0,1:T(8,128)} %param.15) | copy-start | bytes 6148
  78.6 4.9 %collective-permute-start.6 = (f32[16,2,16,128]{3,2,1,0:T(8,128)S(1)}, f32[16,2,16,128]{3,2,1,0:T(8,128)S(1)}, u32[]{:S(2)}, u32[]{:S(2)}) collective-permute-start(f32[16,2,16,128]{3,2,1,0:T(8,128)S(1)} %all_to_all.11), channel_id=1, source_target_pairs={{0,16},{16,0},{1,17},{17,1},{2,18},{18,2},{3,19},{19,3},{4,20},{20... | collective-permute-start | bytes 786440 | tf_op jit(solution)/shard_map/ppermute | solution.py:260

commit v7 on v3

--- a/solution.py
+++ b/solution.py
@@ -18,6 +18,7 @@
 HALF = S // 2
 CHIPS = ("field_0", "field_1")
 FIELD = ("field_0", "field_1", "field_2")
+ALIKE = ("field_0", "field_2")
 
 
 SLOT = {}
@@ -31,33 +32,43 @@
 LIMIT = pltpu.CompilerParams(vmem_limit_bytes=48 * 2**20)
 
 
-def pack_kernel(where_ref, fields_ref, velocity_ref, diffusivity_ref, sent_ref, kept_ref, sems):
-    core = where_ref[0]
+def pack_kernel(where_ref, fields_ref, velocity_ref, diffusivity_ref, part_ref, sent_ref, kept_ref, sems):
+    core, part = where_ref[0], where_ref[2]
+    layers = pl.ds(part % 2 * 2, 2)
     copies = [
-        pltpu.make_async_copy(fields_ref.at[0, pl.ds((1 - core) * HALF, HALF)], sent_ref.at[pl.ds(0, HALF)], sems.at[0]),
-        pltpu.make_async_copy(velocity_ref, sent_ref.at[pl.ds(HALF, 3)], sems.at[1]),
-        pltpu.make_async_copy(diffusivity_ref, sent_ref.at[HALF + 3], sems.at[2]),
-        pltpu.make_async_copy(fields_ref.at[0, pl.ds(core * HALF, HALF)], kept_ref, sems.at[3]),
+        pltpu.make_async_copy(fields_ref.at[0, pl.ds((1 - core) * HALF, HALF)], sent_ref, sems.at[1]),
+        pltpu.make_async_copy(fields_ref.at[0, pl.ds(core * HALF, HALF)], kept_ref, sems.at[2]),
     ]
     for c in copies:
         c.start()
+
+    @pl.when(part < 6)
+    def _():
+        copy = pltpu.make_async_copy(velocity_ref.at[part // 2, layers], part_ref, sems.at[0])
+        copy.start()
+        copy.wait()
+
+    @pl.when(part >= 6)
+    def _():
+        copy = pltpu.make_async_copy(diffusivity_ref.at[layers], part_ref, sems.at[0])
+        copy.start()
+        copy.wait()
+
     for c in copies:
         c.wait()
 
 
-def pack(where, fields, velocity, diffusivity):
+def pack(where, *arrays):
+    half = jax.ShapeDtypeStruct((HALF, X, NZ, NY), jnp.float32)
     return pl.pallas_call(
         pack_kernel,
-        out_shape=(
-            jax.ShapeDtypeStruct((HALF + 4, X, NZ, NY), jnp.float32),
-            jax.ShapeDtypeStruct((HALF, X, NZ, NY), jnp.float32),
-        ),
+        out_shape=(jax.ShapeDtypeStruct((2, NZ, NY), jnp.float32), half, half),
         in_specs=[SMEM] + [pl.BlockSpec(memory_space=pltpu.HBM)] * 3,
-        out_specs=(VMEM, VMEM),
-        scratch_shapes=[pltpu.SemaphoreType.DMA((4,))],
+        out_specs=(VMEM, VMEM, VMEM),
+        scratch_shapes=[pltpu.SemaphoreType.DMA((3,))],
         compiler_params=LIMIT,
         name="pack",
-    )(where, *(pltpu.with_memory_space_constraint(x, pltpu.HBM) for x in (fields, velocity, diffusivity)))
+    )(where, *(pltpu.with_memory_space_constraint(x, pltpu.HBM) for x in arrays))
 
 
 def extended(where_ref, own_ref, inner_ref, outer_ref):
@@ -72,10 +83,18 @@
     return layer
 
 
-def coefficients(noise_ref, layer, coef_ref):
+def coefficients_kernel(where_ref, noise_ref, parts_ref, velocity_ref, diffusivity_ref, coef_ref):
+    odd = where_ref[1] % 2 == 1
+
+    def layer(channel, i):
+        if X <= i < 2 * X:
+            return velocity_ref[channel, i - X] if channel < 3 else diffusivity_ref[i - X]
+        j = i % X
+        outer, inner = (parts_ref[2 * channel + j // 2, n, j % 2] for n in range(2))
+        return jnp.where(odd, inner, outer) if i < X else jnp.where(odd, outer, inner)
+
     for i in range(1, 3 * X - 1):
-        diff = layer(HALF + 3, i)
-        vx, vy, vz = layer(HALF, i), layer(HALF + 1, i), layer(HALF + 2, i)
+        vx, vy, vz, diff = (layer(n, i) for n in range(4))
         stir = jnp.sqrt(2.0 * diff)
         center = 1.0 - 6.0 * diff
         for k in range(SUBSTEPS):
@@ -86,6 +105,17 @@
             hz = 0.5 * (vz - stir * noise_ref[k, 2])
             for n, c in enumerate((center, diff - hx, diff + hx, diff - hy, diff + hy, diff - hz, diff + hz)):
                 coef_ref[SLOT[k, i], n] = c
+
+
+def coefficients(*args):
+    return pl.pallas_call(
+        coefficients_kernel,
+        out_shape=jax.ShapeDtypeStruct((len(SLOT), 7, NZ, NY), jnp.float32),
+        in_specs=[SMEM, SMEM, VMEM, VMEM, VMEM],
+        out_specs=VMEM,
+        compiler_params=LIMIT,
+        name="coefficients",
+    )(*args)
 
 
 def substeps(layer, coef_ref, out_ref):
@@ -110,39 +140,19 @@
     lax.fori_loop(0, HALF // TOGETHER, some, 0)
 
 
-def sent_kernel(where_ref, noise_ref, own_ref, outer_ref, inner_ref, out_ref, coef_ref):
-    layer = extended(where_ref, own_ref, inner_ref, outer_ref)
-    coefficients(noise_ref, layer, coef_ref)
-    substeps(layer, coef_ref, out_ref)
-
-
-def transport_sent(where, noise, own, outer, inner):
-    return pl.pallas_call(
-        sent_kernel,
-        out_shape=(
-            jax.ShapeDtypeStruct((HALF, X, NZ, NY), jnp.float32),
-            jax.ShapeDtypeStruct((len(SLOT), 7, NZ, NY), jnp.float32),
-        ),
-        in_specs=[SMEM, SMEM, VMEM, VMEM, VMEM],
-        out_specs=(VMEM, VMEM),
-        compiler_params=LIMIT,
-        name="transport_sent",
-    )(where, noise, own, outer, inner)
-
-
-def kept_kernel(where_ref, own_ref, inner_ref, outer_ref, coef_ref, out_ref):
+def transport_kernel(where_ref, coef_ref, own_ref, outer_ref, inner_ref, out_ref):
     substeps(extended(where_ref, own_ref, inner_ref, outer_ref), coef_ref, out_ref)
 
 
-def transport_kept(where, own, inner, outer, coef):
-    return pl.pallas_call(
-        kept_kernel,
+def transport(name, *args):
+    return pl.pallas_call(
+        transport_kernel,
         out_shape=jax.ShapeDtypeStruct((HALF, X, NZ, NY), jnp.float32),
-        in_specs=[SMEM, VMEM, VMEM, VMEM, VMEM],
+        in_specs=[SMEM] + [VMEM] * 4,
         out_specs=VMEM,
         compiler_params=LIMIT,
-        name="transport_kept",
-    )(where, own, inner, outer, coef)
+        name=name,
+    )(*args)
 
 
 def halves(x):
@@ -217,18 +227,23 @@
 
 def per_device(fields, velocity, diffusivity, noise, mix_rate, evaporation, rate_matrix, stoich, prefactor):
     slabs = lax.axis_size("slab")
-    where = jnp.stack([lax.axis_index("field_2"), lax.axis_index("slab")]).astype(jnp.int32)
+    where = jnp.stack([lax.axis_index("field_2"), lax.axis_index("slab"), lax.axis_index(ALIKE)]).astype(jnp.int32)
     inner = [(i, i ^ 1) for i in range(slabs)]
     outer = [(i, i + 1 if i % 2 else i - 1) for i in range(1, slabs - 1)]
-    send, keep = pack(where, fields, velocity, diffusivity)
+    part, send, keep = pack(where, fields, velocity, diffusivity)
+    part_outer = lax.ppermute(part, "slab", outer)
+    part_inner = lax.ppermute(part, "slab", inner)
     send_outer = lax.ppermute(send, "slab", outer)
     send_inner = lax.ppermute(send, "slab", inner)
+    keep_outer = lax.ppermute(keep, "slab", outer)
     keep_inner = lax.ppermute(keep, "slab", inner)
-    keep_outer = lax.ppermute(keep, "slab", outer)
+    parts = jnp.stack([part_outer, part_inner])
+    parts = lax.all_to_all(jnp.broadcast_to(parts, (lax.axis_size(ALIKE), *parts.shape)), ALIKE, 0, 0, tiled=True)
+    coef = coefficients(where, noise[0], parts, velocity, diffusivity)
     swap = functools.partial(lax.ppermute, axis_name="field_2", perm=[(0, 1), (1, 0)])
-    sent, coef = transport_sent(where, noise[0], send, send_outer, send_inner)
+    sent = transport("transport_sent", where, coef, send, send_outer, send_inner)
     other = swap(sent)
-    kept = transport_kept(where, keep, keep_inner, keep_outer, coef)
+    kept = transport("transport_kept", where, coef, keep, keep_outer, keep_inner)
     chips = lax.axis_size(CHIPS)
     pair = (kept + other).reshape(chips, -1, NZ, NY)
     parts = lax.all_to_all(pair, CHIPS, 0, 0, tiled=True)

time: 80.5 us -> 87.2 us (1.083)
  starting transfers between devices: 29.7 us -> 42 us
  blocking collectives: 35.1 us -> 30.2 us
  waiting for transfers between devices: 5.25 us -> 3.04 us
    ppermute x0 -> x2, starting transfers between devices: none -> 14.8 us  [the longest x1 12.9 us: per_device(): part_outer = lax.ppermute(part, 'slab', outer)]
    ppermute x1, starting transfers between devices: 12.9 us -> 2.44 us  [per_device(): send_outer = lax.ppermute(send, 'slab', outer)]
    all_to_all x0 -> x1, starting transfers between devices: none -> 5.81 us  [per_device(): lax.all_to_all(jnp.broadcast_to(parts, (lax.axis_size(ALIKE), *parts.shap...]
    ppermute x1, starting transfers between devices: 1.92 us -> 7.65 us  [per_device(): keep_outer = lax.ppermute(keep, 'slab', outer)]
    all_to_all x1, blocking collectives: 21.8 us -> 16.9 us  [per_device(): parts = lax.all_to_all(pair, CHIPS, 0, 0, tiled=True)]
    ppermute x1, starting transfers between devices: 5.24 us -> 2.19 us  [per_device(): other = swap(sent)]
    ppermute x1, waiting for transfers between devices: 2.73 us -> 0.01 us  [per_device(): send_inner = lax.ppermute(send, 'slab', inner)]
    ppermute x1, starting transfers between devices: 3.36 us -> 1.92 us  [per_device(): keep_inner = lax.ppermute(keep, 'slab', inner)]
  transfers between devices with their start and end apart: 6 -> 9, of which waited for: 4 -> 3; matrix products, arithmetic and copies ran while one was open for 1% -> 2% of each run, Pallas kernels for 5% -> 5%
where the time goes in v7:
time: 87.2 us; the launch traced here: 86.1 us
  starting transfers between devices  42 us (48%)
  blocking collectives  30.2 us (35%)
  Pallas kernels  8.73 us (10%)
  waiting for transfers between devices  3.04 us (3%)
  local copies, waits for them, and re-layouts  1.63 us (2%)
    all_to_all x1, blocking collectives, per_device(): parts = lax.all_to_all(pair, CHIPS, 0, 0, tiled=True)  16.9 us
    all_to_all x1, blocking collectives, per_device(): mine = lax.all_to_all(spread, CHIPS, 0, 0, tiled=True)  13.3 us
    ppermute x1, starting transfers between devices, per_device(): part_outer = lax.ppermute(part, 'slab', outer)  12.9 us
    ppermute x1, starting transfers between devices, per_device(): keep_outer = lax.ppermute(keep, 'slab', outer)  7.65 us
    all_to_all x1, starting transfers between devices, per_device(): lax.all_to_all(jnp.broadcast_to(parts, (lax.axis_size(ALIKE), *parts.shap...  5.81 us
    ppermute x1, starting transfers between devices, per_device(): swap(mine)  4.35 us
    pallas_call x2, Pallas kernels, transport(): pl.pallas_call(transport_kernel, out_shape=jax.ShapeDtypeStruct((HALF, X,...  3.56 us
    ppermute x1, starting transfers between devices, per_device(): send_inner = lax.ppermute(send, 'slab', inner)  2.84 us
  transfers between devices with their start and end apart: 9, of which 3 were waited for; matrix products, arithmetic and copies ran while one was open for 2% of the time, Pallas kernels for 5%

profile of v7, /device:TPU:57, one launch (start us, length us, event | category | flops | bytes accessed | tf_op | source)
XLA Modules:
  0.0 86.1 jit_solution(14881556902109896414)
XLA Ops:
  0.0 0.0 copy-start
  0.0 0.0 copy-start.1
  0.0 0.1 pad_add_fusion.where_ref
  0.1 1.6 %pack.1 = (f32[2,16,128]{2,1,0:T(8,128)S(1)}, f32[8,4,16,128]{3,2,1,0:T(8,128)S(1)}, f32[8,4,16,128]{3,2,1,0:T(8,128)S(1)}) custom-call(s32[3]{0:T(128)S(1)} %pad_add_fusion.where_ref, f32[1,16,4,16,128]{4,3,2,1,0:T(8,128)} %fields_ref.1, f32[3,4,16,128]{3,2,1,0:T(8,128)} %velocity_ref.3, f32[4,16,128]{2,1,0:T(8,128)} %diffusivity_ref.3), custom_call_target="tpu_custom_call" | custom-call | tf_op jit(solution)/shard_map/pack/pallas_call | solution.py:63
  1.7 12.9 %collective-permute-start = (f32[2,16,128]{2,1,0:T(8,128)S(1)}, f32[2,16,128]{2,1,0:T(8,128)S(1)}, u32[]{:S(2)}, u32[]{:S(2)}) collective-permute-start(f32[2,16,128]{2,1,0:T(8,128)S(1)} %get-tuple-element.8), channel_id=1, source_target_pairs={{1,2},{2,1},{3,4},{4,3},{5,6},{6,5},{7,8},{8,7},{9,10},{10,9},{11,... | collective-permute-start | bytes 49160 | tf_op jit(solution)/shard_map/ppermute | solution.py:234
  14.6 1.9 %collective-permute-start.1 = (f32[2,16,128]{2,1,0:T(8,128)S(1)}, f32[2,16,128]{2,1,0:T(8,128)S(1)}, u32[]{:S(2)}, u32[]{:S(2)}) collective-permute-start(f32[2,16,128]{2,1,0:T(8,128)S(1)} %get-tuple-element.8), channel_id=1, source_target_pairs={{0,1},{1,0},{2,3},{3,2},{4,5},{5,4},{6,7},{7,6},{8,9},{9,8},{10,11... | collective-permute-start | bytes 49160 | tf_op jit(solution)/shard_map/ppermute | solution.py:235
  16.5 2.4 %collective-permute-start.2 = (f32[8,4,16,128]{3,2,1,0:T(8,128)S(1)}, f32[8,4,16,128]{3,2,1,0:T(8,128)S(1)}, u32[]{:S(2)}, u32[]{:S(2)}) collective-permute-start(f32[8,4,16,128]{3,2,1,0:T(8,128)S(1)} %get-tuple-element.9.own_ref), channel_id=1, source_target_pairs={{1,2},{2,1},{3,4},{4,3},{5,6},{6,5},{7,8},{8,7},{9,10},{10,9},{11,... | collective-permute-start | bytes 786440 | tf_op jit(solution)/shard_map/ppermute | solution.py:236
  19.0 2.8 %collective-permute-start.3 = (f32[8,4,16,128]{3,2,1,0:T(8,128)S(1)}, f32[8,4,16,128]{3,2,1,0:T(8,128)S(1)}, u32[]{:S(2)}, u32[]{:S(2)}) collective-permute-start(f32[8,4,16,128]{3,2,1,0:T(8,128)S(1)} %get-tuple-element.9.own_ref), channel_id=1, source_target_pairs={{0,1},{1,0},{2,3},{3,2},{4,5},{5,4},{6,7},{7,6},{8,9},{9,8},{10,11... | collective-permute-start | bytes 786440 | tf_op jit(solution)/shard_map/ppermute | solution.py:237
  21.8 0.0 collective-permute-done
  21.8 0.0 collective-permute-done.1
  21.9 0.7 broadcast_in_dim.4
  22.6 5.8 %all-to-all-start = ((f32[8,2,2,16,128]{4,3,2,1,0:T(8,128)}), f32[8,2,2,16,128]{4,3,2,1,0:T(8,128)S(1)}, u32[]{:S(2)}, u32[]{:S(2)}) async-start(f32[8,2,2,16,128]{4,3,2,1,0:T(8,128)} %broadcast_in_dim.4), calls=%async_computation | async-start | bytes 524288 | tf_op jit(solution)/shard_map/all_to_all | solution.py:241
  28.4 7.6 %collective-permute-start.4 = (f32[8,4,16,128]{3,2,1,0:T(8,128)S(1)}, f32[8,4,16,128]{3,2,1,0:T(8,128)S(1)}, u32[]{:S(2)}, u32[]{:S(2)}) collective-permute-start(f32[8,4,16,128]{3,2,1,0:T(8,128)S(1)} %get-tuple-element.10.own_ref), channel_id=1, source_target_pairs={{1,2},{2,1},{3,4},{4,3},{5,6},{6,5},{7,8},{8,7},{9,10},{10,9},{11,... | collective-permute-start | bytes 786440 | tf_op jit(solution)/shard_map/ppermute | solution.py:238
  36.1 1.9 %collective-permute-start.5 = (f32[8,4,16,128]{3,2,1,0:T(8,128)S(1)}, f32[8,4,16,128]{3,2,1,0:T(8,128)S(1)}, u32[]{:S(2)}, u32[]{:S(2)}) collective-permute-start(f32[8,4,16,128]{3,2,1,0:T(8,128)S(1)} %get-tuple-element.10.own_ref), channel_id=1, source_target_pairs={{0,1},{1,0},{2,3},{3,2},{4,5},{5,4},{6,7},{7,6},{8,9},{9,8},{10,11... | collective-permute-start | bytes 786440 | tf_op jit(solution)/shard_map/ppermute | solution.py:239
  38.0 0.8 copy.12
  38.8 0.0 all-to-all-done.parts_ref
  38.8 0.0 copy-done
  38.8 0.0 copy-done.1
  38.8 0.7 coefficients.1.coef_ref
  39.5 0.0 collective-permute-done.2.outer_ref
  39.5 0.0 collective-permute-done.3.inner_ref
  39.5 1.8 %transport_sent.1 = f32[8,4,16,128]{3,2,1,0:T(8,128)S(1)} custom-call(s32[3]{0:T(128)S(1)} %pad_add_fusion.where_ref, f32[28,7,16,128]{3,2,1,0:T(8,128)S(1)} %coefficients.1.coef_ref, f32[8,4,16,128]{3,2,1,0:T(8,128)S(1)} %get-tuple-element.9.own_ref, f32[8,4,16,128]{3,2,1,0:T(8,128)S(1)} %collective-permute-done.2.outer_ref, ...), custom_call_target="tpu_custom_call" | custom-call | tf_op jit(solution)/shard_map/transport_sent/pallas_call | solution.py:148
  41.3 2.2 %collective-permute-start.6 = (f32[8,4,16,128]{3,2,1,0:T(8,128)S(1)}, f32[8,4,16,128]{3,2,1,0:T(8,128)S(1)}, u32[]{:S(2)}, u32[]{:S(2)}) collective-permute-start(f32[8,4,16,128]{3,2,1,0:T(8,128)S(1)} %transport_sent.1), channel_id=1, source_target_pairs={{0,16},{16,0},{1,17},{17,1},{2,18},{18,2},{3,19},{19,3},{4,20},{20... | collective-permute-start | bytes 786440 | tf_op jit(solution)/shard_map/ppermute | solution.py:245
  43.5 0.7 collective-permute-done.4.outer_ref
  44.2 1.3 %collective-permute-done.5.inner_ref = f32[8,4,16,128]{3,2,1,0:T(8,128)S(1)} collective-permute-done((f32[8,4,16,128]{3,2,1,0:T(8,128)S(1)}, f32[8,4,16,128]{3,2,1,0:T(8,128)S(1)}, u32[]{:S(2)}, u32[]{:S(2)}) %collective-permute-start.5) | collective-permute-done | bytes 262176 | tf_op jit(solution)/shard_map/ppermute | solution.py:239
  45.6 1.8 %transport_kept.1 = f32[8,4,16,128]{3,2,1,0:T(8,128)S(1)} custom-call(s32[3]{0:T(128)S(1)} %pad_add_fusion.where_ref, f32[28,7,16,128]{3,2,1,0:T(8,128)S(1)} %coefficients.1.coef_ref, f32[8,4,16,128]{3,2,1,0:T(8,128)S(1)} %get-tuple-element.10.own_ref, f32[8,4,16,128]{3,2,1,0:T(8,128)S(1)} %collective-permute-done.4.outer_ref, ...), custom_call_target="tpu_custom_call" | custom-call | tf_op jit(solution)/shard_map/transport_kept/pallas_call | solution.py:148
  47.4 0.0 copy-start.5
  47.4 0.0 copy-start.6
  47.4 0.0 copy-start.2
  47.4 0.0 copy-start.3
  47.4 0.0 copy-start.4
  47.4 0.0 collective-permute-done.6
  47.5 16.9 %all_to_all.15 = f32[16,2,16,128]{3,2,1,0:T(8,128)S(1)} all-to-all(f32[16,2,16,128]{3,2,1,0:T(8,128)S(1)} %bitcast.25), channel_id=1, replica_groups=mesh['field_0'=4,'field_1'=4,'field_2'=2,'slab'=16] {'field_0','field_1'}, dimensions={0} | all-to-all | bytes 524288 | tf_op jit(solution)/shard_map/all_to_all | solution.py:249
  64.4 13.3 %all_to_all.16 = f32[16,2,16,128]{3,2,1,0:T(8,128)S(1)} all-to-all(f32[16,2,16,128]{3,2,1,0:T(8,128)S(1)} %broadcast_in_dim.5), channel_id=1, replica_groups=mesh['field_0'=4,'field_1'=4,'field_2'=2,'slab'=16] {'field_0','field_1'}, dimensions={0} | all-to-all | bytes 524288 | tf_op jit(solution)/shard_map/all_to_all | solution.py:252
  77.8 4.3 %collective-permute-start.7 = (f32[16,2,16,128]{3,2,1,0:T(8,128)S(1)}, f32[16,2,16,128]{3,2,1,0:T(8,128)S(1)}, u32[]{:S(2)}, u32[]{:S(2)}) collective-permute-start(f32[16,2,16,128]{3,2,1,0:T(8,128)S(1)} %all_to_all.16), channel_id=1, source_target_pairs={{0,16},{16,0},{1,17},{17,1},{2,18},{18,2},{3,19},{19,3},{4,20},{20... | collective-permute-start | bytes 786440 | tf_op jit(solution)/shard_map/ppermute | solution.py:253
  82.1 0.0 copy-done.5
  82.1 0.1 copy.13
  82.2 0.0 copy-done.6
  82.2 0.1 multiply_bitcast_fusion.stoich_ref
  82.3 1.0 %collective-permute-done.7 = f32[16,2,16,128]{3,2,1,0:T(8,128)S(1)} collective-permute-done((f32[16,2,16,128]{3,2,1,0:T(8,128)S(1)}, f32[16,2,16,128]{3,2,1,0:T(8,128)S(1)}, u32[]{:S(2)}, u32[]{:S(2)}) %collective-permute-start.7) | collective-permute-done | bytes 262176 | tf_op jit(solution)/shard_map/ppermute | solution.py:253
  83.3 0.0 copy-done.2
  83.3 0.0 copy-done.3
  83.3 0.0 copy-done.4
  83.3 2.8 %react.1 = f32[1024,128]{1,0:T(8,128)} custom-call(s32[3]{0:T(128)S(1)} %pad_add_fusion.where_ref, f32[512,128]{1,0:T(8,128)S(1)} %bitcast.18, f32[512,128]{1,0:T(8,128)S(1)} %bitcast.17, f32[512,128]{1,0:T(8,128)S(1)} %bitcast.19, f32[512,128]{1,0:T(8,128)S(1)} %bitcast.20, f32[64,128]{1,0:T(8,128)S(1)} %bitcast.21, f32[64,128]{1,0:T(8,128)S(1)} %bitcast.22, ...), custom_call_target="tpu_custom_call" | custom-call | tf_op jit(solution)/shard_map/react/pallas_call | solution.py:211
  (5 shorter events, 0.1 us)
Async XLA Ops:
  0.0 38.8 %copy-start = (f32[3,4,16,128]{3,2,1,0:T(8,128)S(1)}, f32[3,4,16,128]{3,2,1,0:T(8,128)}, u32[]{:S(2)}) copy-start(f32[3,4,16,128]{3,2,1,0:T(8,128)} %velocity_ref.3) | copy-start | bytes 294916
  0.0 38.8 %copy-start.1 = (f32[4,16,128]{2,1,0:T(8,128)S(1)}, f32[4,16,128]{2,1,0:T(8,128)}, u32[]{:S(2)}) copy-start(f32[4,16,128]{2,1,0:T(8,128)} %diffusivity_ref.3) | copy-start | bytes 98308
  1.7 20.1 %collective-permute-start = (f32[2,16,128]{2,1,0:T(8,128)S(1)}, f32[2,16,128]{2,1,0:T(8,128)S(1)}, u32[]{:S(2)}, u32[]{:S(2)}) collective-permute-start(f32[2,16,128]{2,1,0:T(8,128)S(1)} %get-tuple-element.8), channel_id=1, source_target_pairs={{1,2},{2,1},{3,4},{4,3},{5,6},{6,5},{7,8},{8,7},{9,10},{10,9},{11,... | collective-permute-start | bytes 49160 | tf_op jit(solution)/shard_map/ppermute | solution.py:234
  14.6 7.2 %collective-permute-start.1 = (f32[2,16,128]{2,1,0:T(8,128)S(1)}, f32[2,16,128]{2,1,0:T(8,128)S(1)}, u32[]{:S(2)}, u32[]{:S(2)}) collective-permute-start(f32[2,16,128]{2,1,0:T(8,128)S(1)} %get-tuple-element.8), channel_id=1, source_target_pairs={{0,1},{1,0},{2,3},{3,2},{4,5},{5,4},{6,7},{7,6},{8,9},{9,8},{10,11... | collective-permute-start | bytes 49160 | tf_op jit(solution)/shard_map/ppermute | solution.py:235
  16.5 23.0 %collective-permute-start.2 = (f32[8,4,16,128]{3,2,1,0:T(8,128)S(1)}, f32[8,4,16,128]{3,2,1,0:T(8,128)S(1)}, u32[]{:S(2)}, u32[]{:S(2)}) collective-permute-start(f32[8,4,16,128]{3,2,1,0:T(8,128)S(1)} %get-tuple-element.9.own_ref), channel_id=1, source_target_pairs={{1,2},{2,1},{3,4},{4,3},{5,6},{6,5},{7,8},{8,7},{9,10},{10,9},{11,... | collective-permute-start | bytes 786440 | tf_op jit(solution)/shard_map/ppermute | solution.py:236
  19.0 20.5 %collective-permute-start.3 = (f32[8,4,16,128]{3,2,1,0:T(8,128)S(1)}, f32[8,4,16,128]{3,2,1,0:T(8,128)S(1)}, u32[]{:S(2)}, u32[]{:S(2)}) collective-permute-start(f32[8,4,16,128]{3,2,1,0:T(8,128)S(1)} %get-tuple-element.9.own_ref), channel_id=1, source_target_pairs={{0,1},{1,0},{2,3},{3,2},{4,5},{5,4},{6,7},{7,6},{8,9},{9,8},{10,11... | collective-permute-start | bytes 786440 | tf_op jit(solution)/shard_map/ppermute | solution.py:237
  22.6 16.2 %all-to-all-start = ((f32[8,2,2,16,128]{4,3,2,1,0:T(8,128)}), f32[8,2,2,16,128]{4,3,2,1,0:T(8,128)S(1)}, u32[]{:S(2)}, u32[]{:S(2)}) async-start(f32[8,2,2,16,128]{4,3,2,1,0:T(8,128)} %broadcast_in_dim.4), calls=%async_computation | async-start | bytes 524288 | tf_op jit(solution)/shard_map/all_to_all | solution.py:241
  28.4 15.8 %collective-permute-start.4 = (f32[8,4,16,128]{3,2,1,0:T(8,128)S(1)}, f32[8,4,16,128]{3,2,1,0:T(8,128)S(1)}, u32[]{:S(2)}, u32[]{:S(2)}) collective-permute-start(f32[8,4,16,128]{3,2,1,0:T(8,128)S(1)} %get-tuple-element.10.own_ref), channel_id=1, source_target_pairs={{1,2},{2,1},{3,4},{4,3},{5,6},{6,5},{7,8},{8,7},{9,10},{10,9},{11,... | collective-permute-start | bytes 786440 | tf_op jit(solution)/shard_map/ppermute | solution.py:238
  36.1 9.5 %collective-permute-start.5 = (f32[8,4,16,128]{3,2,1,0:T(8,128)S(1)}, f32[8,4,16,128]{3,2,1,0:T(8,128)S(1)}, u32[]{:S(2)}, u32[]{:S(2)}) collective-permute-start(f32[8,4,16,128]{3,2,1,0:T(8,128)S(1)} %get-tuple-element.10.own_ref), channel_id=1, source_target_pairs={{0,1},{1,0},{2,3},{3,2},{4,5},{5,4},{6,7},{7,6},{8,9},{9,8},{10,11... | collective-permute-start | bytes 786440 | tf_op jit(solution)/shard_map/ppermute | solution.py:239
  41.3 6.1 %collective-permute-start.6 = (f32[8,4,16,128]{3,2,1,0:T(8,128)S(1)}, f32[8,4,16,128]{3,2,1,0:T(8,128)S(1)}, u32[]{:S(2)}, u32[]{:S(2)}) collective-permute-start(f32[8,4,16,128]{3,2,1,0:T(8,128)S(1)} %transport_sent.1), channel_id=1, source_target_pairs={{0,16},{16,0},{1,17},{17,1},{2,18},{18,2},{3,19},{19,3},{4,20},{20... | collective-permute-start | bytes 786440 | tf_op jit(solution)/shard_map/ppermute | solution.py:245
  47.4 34.8 %copy-start.5 = (f32[16,32]{1,0:T(8,128)S(1)}, f32[16,32]{1,0:T(8,128)}, u32[]{:S(2)}) copy-start(f32[16,32]{1,0:T(8,128)} %param.16) | copy-start | bytes 6148
  47.4 34.8 %copy-start.6 = (f32[32]{0:T(128)S(1)}, f32[32]{0:T(128)}, u32[]{:S(2)}) copy-start(f32[32]{0:T(128)} %param.17) | copy-start | bytes 388
  47.4 35.9 %copy-start.2 = (f32[4,16,128]{2,1,0:T(8,128)S(1)}, f32[4,16,128]{2,1,0:T(8,128)}, u32[]{:S(2)}) copy-start(f32[4,16,128]{2,1,0:T(8,128)} %param.13) | copy-start | bytes 98308
  47.4 35.9 %copy-start.3 = (f32[4,16,128]{2,1,0:T(8,128)S(1)}, f32[4,16,128]{2,1,0:T(8,128)}, u32[]{:S(2)}) copy-start(f32[4,16,128]{2,1,0:T(8,128)} %param.14) | copy-start | bytes 98308
  47.4 35.9 %copy-start.4 = (f32[32,16]{0,1:T(8,128)S(1)}, f32[32,16]{0,1:T(8,128)}, u32[]{:S(2)}) copy-start(f32[32,16]{0,1:T(8,128)} %param.15) | copy-start | bytes 6148
  77.8 5.5 %collective-permute-start.7 = (f32[16,2,16,128]{3,2,1,0:T(8,128)S(1)}, f32[16,2,16,128]{3,2,1,0:T(8,128)S(1)}, u32[]{:S(2)}, u32[]{:S(2)}) collective-permute-start(f32[16,2,16,128]{3,2,1,0:T(8,128)S(1)} %all_to_all.16), channel_id=1, source_target_pairs={{0,16},{16,0},{1,17},{17,1},{2,18},{18,2},{3,19},{19,3},{4,20},{20... | collective-permute-start | bytes 786440 | tf_op jit(solution)/shard_map/ppermute | solution.py:253

commit v8 on v3

--- a/solution.py
+++ b/solution.py
@@ -31,51 +31,82 @@
 LIMIT = pltpu.CompilerParams(vmem_limit_bytes=48 * 2**20)
 
 
-def pack_kernel(where_ref, fields_ref, velocity_ref, diffusivity_ref, sent_ref, kept_ref, sems):
-    core = where_ref[0]
-    copies = [
-        pltpu.make_async_copy(fields_ref.at[0, pl.ds((1 - core) * HALF, HALF)], sent_ref.at[pl.ds(0, HALF)], sems.at[0]),
-        pltpu.make_async_copy(velocity_ref, sent_ref.at[pl.ds(HALF, 3)], sems.at[1]),
-        pltpu.make_async_copy(diffusivity_ref, sent_ref.at[HALF + 3], sems.at[2]),
-        pltpu.make_async_copy(fields_ref.at[0, pl.ds(core * HALF, HALF)], kept_ref, sems.at[3]),
-    ]
-    for c in copies:
-        c.start()
+USED = X - 1
+CELLS = X * HALF
+
+
+def pack_kernel(where_ref, fields_ref, velocity_ref, diffusivity_ref, outer_ref, inner_ref, kept_ref, sems):
+    core, odd = where_ref[0], where_ref[1] % 2
+    copies = []
+
+    def copy(source, target):
+        copies.append(pltpu.make_async_copy(source, target, sems.at[len(copies)]))
+        copies[-1].start()
+
+    for target, first, head in (
+        (outer_ref, (1 - core) * HALF, odd),
+        (inner_ref, (1 - core) * HALF, 1 - odd),
+        (kept_ref, core * HALF, None),
+    ):
+        for j in range(X):
+            copy(fields_ref.at[0, pl.ds(first, HALF), j], target.at[pl.ds(j * HALF, HALF)])
+        if head is None:
+            continue
+        for n in range(4):
+            source = velocity_ref.at[n] if n < 3 else diffusivity_ref
+            copy(source.at[pl.ds(head, USED)], target.at[pl.ds(CELLS + n * USED, USED)])
     for c in copies:
         c.wait()
 
 
-def pack(where, fields, velocity, diffusivity):
+def pack(where, *arrays):
+    planes = (CELLS + 4 * USED, CELLS + 4 * USED, CELLS)
     return pl.pallas_call(
         pack_kernel,
-        out_shape=(
-            jax.ShapeDtypeStruct((HALF + 4, X, NZ, NY), jnp.float32),
-            jax.ShapeDtypeStruct((HALF, X, NZ, NY), jnp.float32),
-        ),
+        out_shape=tuple(jax.ShapeDtypeStruct((n, NZ, NY), jnp.float32) for n in planes),
         in_specs=[SMEM] + [pl.BlockSpec(memory_space=pltpu.HBM)] * 3,
-        out_specs=(VMEM, VMEM),
-        scratch_shapes=[pltpu.SemaphoreType.DMA((4,))],
+        out_specs=(VMEM,) * 3,
+        scratch_shapes=[pltpu.SemaphoreType.DMA((3 * X + 8,))],
         compiler_params=LIMIT,
         name="pack",
-    )(where, *(pltpu.with_memory_space_constraint(x, pltpu.HBM) for x in (fields, velocity, diffusivity)))
+    )(where, *(pltpu.with_memory_space_constraint(x, pltpu.HBM) for x in arrays))
 
 
 def extended(where_ref, own_ref, inner_ref, outer_ref):
     odd = where_ref[1] % 2 == 1
 
+    def layer(some, i):
+        at = pl.ds(i % X * HALF + some * TOGETHER, TOGETHER)
+        if X <= i < 2 * X:
+            return own_ref[at]
+        inner, outer = inner_ref[at], outer_ref[at]
+        return jnp.where(odd, inner, outer) if i < X else jnp.where(odd, outer, inner)
+
+    return layer
+
+
+def flow(where_ref, own_inner_ref, own_outer_ref, inner_ref, outer_ref):
+    odd = where_ref[1] % 2 == 1
+
     def layer(channel, i):
-        if X <= i < 2 * X:
-            return own_ref[channel, i - X]
-        inner, outer = inner_ref[channel, i % X], outer_ref[channel, i % X]
-        return jnp.where(odd, inner, outer) if i < X else jnp.where(odd, outer, inner)
+        def pick(if_odd, if_even, j):
+            at = CELLS + channel * USED + j
+            return jnp.where(odd, if_odd[at], if_even[at])
+
+        if i < X:
+            return pick(inner_ref, outer_ref, i - 1)
+        if i >= 2 * X:
+            return pick(outer_ref, inner_ref, i - 2 * X)
+        if i == X:
+            return pick(own_inner_ref, own_outer_ref, 0)
+        return pick(own_outer_ref, own_inner_ref, i - X - 1)
 
     return layer
 
 
 def coefficients(noise_ref, layer, coef_ref):
     for i in range(1, 3 * X - 1):
-        diff = layer(HALF + 3, i)
-        vx, vy, vz = layer(HALF, i), layer(HALF + 1, i), layer(HALF + 2, i)
+        vx, vy, vz, diff = (layer(n, i) for n in range(4))
         stir = jnp.sqrt(2.0 * diff)
         center = 1.0 - 6.0 * diff
         for k in range(SUBSTEPS):
@@ -91,7 +122,7 @@
 def substeps(layer, coef_ref, out_ref):
     def some(g, carry):
         scalars = pl.ds(g * TOGETHER, TOGETHER)
-        state = [layer(scalars, i) for i in range(3 * X)]
+        state = [layer(g, i) for i in range(3 * X)]
         for k in range(SUBSTEPS):
             new = [None] * (3 * X)
             for i in range(k + 1, 3 * X - 1 - k):
@@ -110,24 +141,23 @@
     lax.fori_loop(0, HALF // TOGETHER, some, 0)
 
 
-def sent_kernel(where_ref, noise_ref, own_ref, outer_ref, inner_ref, out_ref, coef_ref):
-    layer = extended(where_ref, own_ref, inner_ref, outer_ref)
-    coefficients(noise_ref, layer, coef_ref)
-    substeps(layer, coef_ref, out_ref)
-
-
-def transport_sent(where, noise, own, outer, inner):
+def sent_kernel(where_ref, noise_ref, own_outer_ref, own_inner_ref, outer_ref, inner_ref, out_ref, coef_ref):
+    coefficients(noise_ref, flow(where_ref, own_inner_ref, own_outer_ref, inner_ref, outer_ref), coef_ref)
+    substeps(extended(where_ref, own_outer_ref, inner_ref, outer_ref), coef_ref, out_ref)
+
+
+def transport_sent(*args):
     return pl.pallas_call(
         sent_kernel,
         out_shape=(
             jax.ShapeDtypeStruct((HALF, X, NZ, NY), jnp.float32),
             jax.ShapeDtypeStruct((len(SLOT), 7, NZ, NY), jnp.float32),
         ),
-        in_specs=[SMEM, SMEM, VMEM, VMEM, VMEM],
+        in_specs=[SMEM, SMEM] + [VMEM] * 4,
         out_specs=(VMEM, VMEM),
         compiler_params=LIMIT,
         name="transport_sent",
-    )(where, noise, own, outer, inner)
+    )(*args)
 
 
 def kept_kernel(where_ref, own_ref, inner_ref, outer_ref, coef_ref, out_ref):
@@ -220,13 +250,13 @@
     where = jnp.stack([lax.axis_index("field_2"), lax.axis_index("slab")]).astype(jnp.int32)
     inner = [(i, i ^ 1) for i in range(slabs)]
     outer = [(i, i + 1 if i % 2 else i - 1) for i in range(1, slabs - 1)]
-    send, keep = pack(where, fields, velocity, diffusivity)
-    send_outer = lax.ppermute(send, "slab", outer)
-    send_inner = lax.ppermute(send, "slab", inner)
+    to_outer, to_inner, keep = pack(where, fields, velocity, diffusivity)
+    from_outer = lax.ppermute(to_outer, "slab", outer)
+    from_inner = lax.ppermute(to_inner, "slab", inner)
     keep_inner = lax.ppermute(keep, "slab", inner)
     keep_outer = lax.ppermute(keep, "slab", outer)
     swap = functools.partial(lax.ppermute, axis_name="field_2", perm=[(0, 1), (1, 0)])
-    sent, coef = transport_sent(where, noise[0], send, send_outer, send_inner)
+    sent, coef = transport_sent(where, noise[0], to_outer, to_inner, from_outer, from_inner)
     other = swap(sent)
     kept = transport_kept(where, keep, keep_inner, keep_outer, coef)
     chips = lax.axis_size(CHIPS)

time: 80.5 us -> 79.5 us (0.988)
  blocking collectives: 35.1 us -> 33.7 us
    all_to_all x1, blocking collectives: 21.8 us -> 20.4 us  [per_device(): parts = lax.all_to_all(pair, CHIPS, 0, 0, tiled=True)]
where the time goes in v8:
time: 79.5 us; the launch traced here: 78.5 us
  blocking collectives  33.7 us (42%)
  starting transfers between devices  29.7 us (37%)
  Pallas kernels  8.55 us (11%)
  waiting for transfers between devices  5.23 us (7%)
  local copies, waits for them, and re-layouts  0.89 us (1%)
    all_to_all x1, blocking collectives, per_device(): parts = lax.all_to_all(pair, CHIPS, 0, 0, tiled=True)  20.4 us
    all_to_all x1, blocking collectives, per_device(): mine = lax.all_to_all(spread, CHIPS, 0, 0, tiled=True)  13.3 us
    ppermute x1, starting transfers between devices, per_device(): from_outer = lax.ppermute(to_outer, 'slab', outer)  12.9 us
    ppermute x1, starting transfers between devices, per_device(): other = swap(sent)  5.24 us
    ppermute x1, starting transfers between devices, per_device(): swap(mine)  4.37 us
    ppermute x1, starting transfers between devices, per_device(): keep_inner = lax.ppermute(keep, 'slab', inner)  3.36 us
    pallas_call x1, Pallas kernels, react(): pl.pallas_call(react_kernel, out_shape=jax.ShapeDtypeStruct((S * rows, NY...  2.83 us
    ppermute x1, waiting for transfers between devices, per_device(): from_inner = lax.ppermute(to_inner, 'slab', inner)  2.73 us
  transfers between devices with their start and end apart: 6, of which 4 were waited for; matrix products, arithmetic and copies ran while one was open for 1% of the time, Pallas kernels for 5%

profile of v8, /device:TPU:57, one launch (start us, length us, event | category | flops | bytes accessed | tf_op | source)
XLA Modules:
  0.0 78.5 jit_solution(7086264643589629852)
XLA Ops:
  0.0 0.1 pad_add_fusion.where_ref
  0.1 2.0 %pack.1 = (f32[44,16,128]{2,1,0:T(8,128)S(1)}, f32[44,16,128]{2,1,0:T(8,128)S(1)}, f32[32,16,128]{2,1,0:T(8,128)S(1)}) custom-call(s32[2]{0:T(128)S(1)} %pad_add_fusion.where_ref, f32[1,16,4,16,128]{4,3,2,1,0:T(8,128)} %fields_ref.1, f32[3,4,16,128]{3,2,1,0:T(8,128)} %velocity_ref.1, f32[4,16,128]{2,1,0:T(8,128)} %diffusivity_ref.1), custom_call_target="tpu_custom_call" | custom-call | tf_op jit(solution)/shard_map/pack/pallas_call | solution.py:64
  2.0 12.9 %collective-permute-start = (f32[44,16,128]{2,1,0:T(8,128)S(1)}, f32[44,16,128]{2,1,0:T(8,128)S(1)}, u32[]{:S(2)}, u32[]{:S(2)}) collective-permute-start(f32[44,16,128]{2,1,0:T(8,128)S(1)} %get-tuple-element.10.own_outer_ref), channel_id=1, source_target_pairs={{1,2},{2,1},{3,4},{4,3},{5,6},{6,5},{7,8},{8,7},{9,10},{10,9},{11,... | collective-permute-start | bytes 1081352 | tf_op jit(solution)/shard_map/ppermute | solution.py:254
  15.0 1.9 %collective-permute-start.1 = (f32[44,16,128]{2,1,0:T(8,128)S(1)}, f32[44,16,128]{2,1,0:T(8,128)S(1)}, u32[]{:S(2)}, u32[]{:S(2)}) collective-permute-start(f32[44,16,128]{2,1,0:T(8,128)S(1)} %get-tuple-element.11.own_inner_ref), channel_id=1, source_target_pairs={{0,1},{1,0},{2,3},{3,2},{4,5},{5,4},{6,7},{7,6},{8,9},{9,8},{10,11... | collective-permute-start | bytes 1081352 | tf_op jit(solution)/shard_map/ppermute | solution.py:255
  16.9 3.4 %collective-permute-start.2 = (f32[32,16,128]{2,1,0:T(8,128)S(1)}, f32[32,16,128]{2,1,0:T(8,128)S(1)}, u32[]{:S(2)}, u32[]{:S(2)}) collective-permute-start(f32[32,16,128]{2,1,0:T(8,128)S(1)} %get-tuple-element.13.own_ref), channel_id=1, source_target_pairs={{0,1},{1,0},{2,3},{3,2},{4,5},{5,4},{6,7},{7,6},{8,9},{9,8},{10,11... | collective-permute-start | bytes 786440 | tf_op jit(solution)/shard_map/ppermute | solution.py:256
  20.3 1.9 %collective-permute-start.3 = (f32[32,16,128]{2,1,0:T(8,128)S(1)}, f32[32,16,128]{2,1,0:T(8,128)S(1)}, u32[]{:S(2)}, u32[]{:S(2)}) collective-permute-start(f32[32,16,128]{2,1,0:T(8,128)S(1)} %get-tuple-element.13.own_ref), channel_id=1, source_target_pairs={{1,2},{2,1},{3,4},{4,3},{5,6},{6,5},{7,8},{8,7},{9,10},{10,9},{11,... | collective-permute-start | bytes 786440 | tf_op jit(solution)/shard_map/ppermute | solution.py:257
  22.2 0.8 copy.12
  23.0 0.1 collective-permute-done.outer_ref
  23.1 2.7 %collective-permute-done.1.inner_ref = f32[44,16,128]{2,1,0:T(8,128)S(1)} collective-permute-done((f32[44,16,128]{2,1,0:T(8,128)S(1)}, f32[44,16,128]{2,1,0:T(8,128)S(1)}, u32[]{:S(2)}, u32[]{:S(2)}) %collective-permute-start.1) | collective-permute-done | bytes 360480 | tf_op jit(solution)/shard_map/ppermute | solution.py:255
  25.8 2.0 %transport_sent.1 = (f32[8,4,16,128]{3,2,1,0:T(8,128)S(1)}, f32[28,7,16,128]{3,2,1,0:T(8,128)S(1)}) custom-call(s32[2]{0:T(128)S(1)} %pad_add_fusion.where_ref, f32[4,3]{1,0:T(4,128)S(1)} %bitcast.21, f32[44,16,128]{2,1,0:T(8,128)S(1)} %get-tuple-element.10.own_outer_ref, f32[44,16,128]{2,1,0:T(8,128)S(1)} %get-tuple-element.11.own_inner_ref, ...), custom_call_target="tpu_custom_call" | custom-call | tf_op jit(solution)/shard_map/transport_sent/pallas_call | solution.py:150
  27.8 5.2 %collective-permute-start.4 = (f32[8,4,16,128]{3,2,1,0:T(8,128)S(1)}, f32[8,4,16,128]{3,2,1,0:T(8,128)S(1)}, u32[]{:S(2)}, u32[]{:S(2)}) collective-permute-start(f32[8,4,16,128]{3,2,1,0:T(8,128)S(1)} %get-tuple-element.12), channel_id=1, source_target_pairs={{0,16},{16,0},{1,17},{17,1},{2,18},{18,2},{3,19},{19,3},{4,20},{20... | collective-permute-start | bytes 786440 | tf_op jit(solution)/shard_map/ppermute | solution.py:260
  33.1 0.0 collective-permute-done.2.inner_ref
  33.1 1.4 %collective-permute-done.3.outer_ref = f32[32,16,128]{2,1,0:T(8,128)S(1)} collective-permute-done((f32[32,16,128]{2,1,0:T(8,128)S(1)}, f32[32,16,128]{2,1,0:T(8,128)S(1)}, u32[]{:S(2)}, u32[]{:S(2)}) %collective-permute-start.3) | collective-permute-done | bytes 262176 | tf_op jit(solution)/shard_map/ppermute | solution.py:257
  34.5 1.8 %transport_kept.1 = f32[8,4,16,128]{3,2,1,0:T(8,128)S(1)} custom-call(s32[2]{0:T(128)S(1)} %pad_add_fusion.where_ref, f32[32,16,128]{2,1,0:T(8,128)S(1)} %get-tuple-element.13.own_ref, f32[32,16,128]{2,1,0:T(8,128)S(1)} %collective-permute-done.2.inner_ref, f32[32,16,128]{2,1,0:T(8,128)S(1)} %collective-permute-done.3.outer_ref, ...), custom_call_target="tpu_custom_call" | custom-call | tf_op jit(solution)/shard_map/transport_kept/pallas_call | solution.py:168
  36.2 0.0 copy-start.3
  36.3 0.0 copy-start.4
  36.3 0.0 copy-start
  36.3 0.0 copy-start.1
  36.3 0.0 copy-start.2
  36.3 0.0 collective-permute-done.4
  36.4 20.4 %all_to_all.10 = f32[16,2,16,128]{3,2,1,0:T(8,128)S(1)} all-to-all(f32[16,2,16,128]{3,2,1,0:T(8,128)S(1)} %bitcast.22), channel_id=1, replica_groups=mesh['field_0'=4,'field_1'=4,'field_2'=2,'slab'=16] {'field_0','field_1'}, dimensions={0} | all-to-all | bytes 524288 | tf_op jit(solution)/shard_map/all_to_all | solution.py:264
  56.8 13.3 %all_to_all.11 = f32[16,2,16,128]{3,2,1,0:T(8,128)S(1)} all-to-all(f32[16,2,16,128]{3,2,1,0:T(8,128)S(1)} %broadcast_in_dim.2), channel_id=1, replica_groups=mesh['field_0'=4,'field_1'=4,'field_2'=2,'slab'=16] {'field_0','field_1'}, dimensions={0} | all-to-all | bytes 524288 | tf_op jit(solution)/shard_map/all_to_all | solution.py:267
  70.1 4.4 %collective-permute-start.5 = (f32[16,2,16,128]{3,2,1,0:T(8,128)S(1)}, f32[16,2,16,128]{3,2,1,0:T(8,128)S(1)}, u32[]{:S(2)}, u32[]{:S(2)}) collective-permute-start(f32[16,2,16,128]{3,2,1,0:T(8,128)S(1)} %all_to_all.11), channel_id=1, source_target_pairs={{0,16},{16,0},{1,17},{17,1},{2,18},{18,2},{3,19},{19,3},{4,20},{20... | collective-permute-start | bytes 786440 | tf_op jit(solution)/shard_map/ppermute | solution.py:268
  74.5 0.0 copy-done.3
  74.5 0.1 copy.13
  74.6 0.0 copy-done.4
  74.6 0.1 multiply_bitcast_fusion.stoich_ref
  74.7 1.0 %collective-permute-done.5 = f32[16,2,16,128]{3,2,1,0:T(8,128)S(1)} collective-permute-done((f32[16,2,16,128]{3,2,1,0:T(8,128)S(1)}, f32[16,2,16,128]{3,2,1,0:T(8,128)S(1)}, u32[]{:S(2)}, u32[]{:S(2)}) %collective-permute-start.5) | collective-permute-done | bytes 262176 | tf_op jit(solution)/shard_map/ppermute | solution.py:268
  75.7 0.0 copy-done
  75.7 0.0 copy-done.1
  75.7 0.0 copy-done.2
  75.7 2.8 %react.1 = f32[1024,128]{1,0:T(8,128)} custom-call(s32[2]{0:T(128)S(1)} %pad_add_fusion.where_ref, f32[512,128]{1,0:T(8,128)S(1)} %bitcast.16, f32[512,128]{1,0:T(8,128)S(1)} %bitcast.14, f32[512,128]{1,0:T(8,128)S(1)} %bitcast.15, f32[512,128]{1,0:T(8,128)S(1)} %bitcast.17, f32[64,128]{1,0:T(8,128)S(1)} %bitcast.18, f32[64,128]{1,0:T(8,128)S(1)} %bitcast.19, ...), custom_call_target="tpu_custom_call" | custom-call | tf_op jit(solution)/shard_map/react/pallas_call | solution.py:231
  (4 shorter events, 0.1 us)
Async XLA Ops:
  2.0 21.0 %collective-permute-start = (f32[44,16,128]{2,1,0:T(8,128)S(1)}, f32[44,16,128]{2,1,0:T(8,128)S(1)}, u32[]{:S(2)}, u32[]{:S(2)}) collective-permute-start(f32[44,16,128]{2,1,0:T(8,128)S(1)} %get-tuple-element.10.own_outer_ref), channel_id=1, source_target_pairs={{1,2},{2,1},{3,4},{4,3},{5,6},{6,5},{7,8},{8,7},{9,10},{10,9},{11,... | collective-permute-start | bytes 1081352 | tf_op jit(solution)/shard_map/ppermute | solution.py:254
  15.0 10.9 %collective-permute-start.1 = (f32[44,16,128]{2,1,0:T(8,128)S(1)}, f32[44,16,128]{2,1,0:T(8,128)S(1)}, u32[]{:S(2)}, u32[]{:S(2)}) collective-permute-start(f32[44,16,128]{2,1,0:T(8,128)S(1)} %get-tuple-element.11.own_inner_ref), channel_id=1, source_target_pairs={{0,1},{1,0},{2,3},{3,2},{4,5},{5,4},{6,7},{7,6},{8,9},{9,8},{10,11... | collective-permute-start | bytes 1081352 | tf_op jit(solution)/shard_map/ppermute | solution.py:255
  16.9 16.2 %collective-permute-start.2 = (f32[32,16,128]{2,1,0:T(8,128)S(1)}, f32[32,16,128]{2,1,0:T(8,128)S(1)}, u32[]{:S(2)}, u32[]{:S(2)}) collective-permute-start(f32[32,16,128]{2,1,0:T(8,128)S(1)} %get-tuple-element.13.own_ref), channel_id=1, source_target_pairs={{0,1},{1,0},{2,3},{3,2},{4,5},{5,4},{6,7},{7,6},{8,9},{9,8},{10,11... | collective-permute-start | bytes 786440 | tf_op jit(solution)/shard_map/ppermute | solution.py:256
  20.3 14.2 %collective-permute-start.3 = (f32[32,16,128]{2,1,0:T(8,128)S(1)}, f32[32,16,128]{2,1,0:T(8,128)S(1)}, u32[]{:S(2)}, u32[]{:S(2)}) collective-permute-start(f32[32,16,128]{2,1,0:T(8,128)S(1)} %get-tuple-element.13.own_ref), channel_id=1, source_target_pairs={{1,2},{2,1},{3,4},{4,3},{5,6},{6,5},{7,8},{8,7},{9,10},{10,9},{11,... | collective-permute-start | bytes 786440 | tf_op jit(solution)/shard_map/ppermute | solution.py:257
  27.8 8.5 %collective-permute-start.4 = (f32[8,4,16,128]{3,2,1,0:T(8,128)S(1)}, f32[8,4,16,128]{3,2,1,0:T(8,128)S(1)}, u32[]{:S(2)}, u32[]{:S(2)}) collective-permute-start(f32[8,4,16,128]{3,2,1,0:T(8,128)S(1)} %get-tuple-element.12), channel_id=1, source_target_pairs={{0,16},{16,0},{1,17},{17,1},{2,18},{18,2},{3,19},{19,3},{4,20},{20... | collective-permute-start | bytes 786440 | tf_op jit(solution)/shard_map/ppermute | solution.py:260
  36.2 38.3 %copy-start.3 = (f32[16,32]{1,0:T(8,128)S(1)}, f32[16,32]{1,0:T(8,128)}, u32[]{:S(2)}) copy-start(f32[16,32]{1,0:T(8,128)} %param.16) | copy-start | bytes 6148
  36.3 38.4 %copy-start.4 = (f32[32]{0:T(128)S(1)}, f32[32]{0:T(128)}, u32[]{:S(2)}) copy-start(f32[32]{0:T(128)} %param.17) | copy-start | bytes 388
  36.3 39.4 %copy-start = (f32[4,16,128]{2,1,0:T(8,128)S(1)}, f32[4,16,128]{2,1,0:T(8,128)}, u32[]{:S(2)}) copy-start(f32[4,16,128]{2,1,0:T(8,128)} %param.13) | copy-start | bytes 98308
  36.3 39.4 %copy-start.1 = (f32[4,16,128]{2,1,0:T(8,128)S(1)}, f32[4,16,128]{2,1,0:T(8,128)}, u32[]{:S(2)}) copy-start(f32[4,16,128]{2,1,0:T(8,128)} %param.14) | copy-start | bytes 98308
  36.3 39.4 %copy-start.2 = (f32[32,16]{0,1:T(8,128)S(1)}, f32[32,16]{0,1:T(8,128)}, u32[]{:S(2)}) copy-start(f32[32,16]{0,1:T(8,128)} %param.15) | copy-start | bytes 6148
  70.1 5.5 %collective-permute-start.5 = (f32[16,2,16,128]{3,2,1,0:T(8,128)S(1)}, f32[16,2,16,128]{3,2,1,0:T(8,128)S(1)}, u32[]{:S(2)}, u32[]{:S(2)}) collective-permute-start(f32[16,2,16,128]{3,2,1,0:T(8,128)S(1)} %all_to_all.11), channel_id=1, source_target_pairs={{0,16},{16,0},{1,17},{17,1},{2,18},{18,2},{3,19},{19,3},{4,20},{20... | collective-permute-start | bytes 786440 | tf_op jit(solution)/shard_map/ppermute | solution.py:268

commit v9 on v8

--- a/solution.py
+++ b/solution.py
@@ -25,7 +25,7 @@
     for _k in range(SUBSTEPS):
         if _k < _i < 3 * X - 1 - _k:
             SLOT[_k, _i] = len(SLOT)
-TOGETHER = 4
+TOGETHER = 8
 VMEM = pl.BlockSpec(memory_space=pltpu.VMEM)
 SMEM = pl.BlockSpec(memory_space=pltpu.SMEM)
 LIMIT = pltpu.CompilerParams(vmem_limit_bytes=48 * 2**20)
@@ -191,22 +191,32 @@
     )
 
 
-ROWS = 16
+ROWS = 32
 
 
 def react_kernel(
-    where_ref, sent_ref, kept_ref, mine_ref, other_ref, rate_ref, vapour_ref, rate_matrix_ref, stoich_ref, out_ref
+    where_ref,
+    sent_ref,
+    kept_ref,
+    mine_ref,
+    other_ref,
+    rate_ref,
+    vapour_ref,
+    rate_matrix_ref,
+    stoich_ref,
+    out_ref,
+    done_ref,
+    sems,
 ):
     cells = X * NZ
     drive_weights = halves(rate_matrix_ref[...])
     source_weights = halves(stoich_ref[...])
     first = where_ref[0] == 0
     fuel = lax.broadcasted_iota(jnp.int32, (S, NY), 0) == 0
-
-    def some(step, carry):
+    copies = []
+    for block in range(cells // ROWS):
         mixed = []
-        for j in range(ROWS):
-            r = step * ROWS + j
+        for r in range(block * ROWS, (block + 1) * ROWS):
             sent, kept, mine, other = (
                 ref[pl.ds(r, HALF, stride=cells), :] for ref in (sent_ref, kept_ref, mine_ref, other_ref)
             )
@@ -220,10 +230,18 @@
         speed = jnp.exp(2.0 * jnp.tanh(product(drive_weights, mixed)))
         updated = mixed + product(source_weights, speed)
         for j in range(ROWS):
-            out_ref[pl.ds(step * ROWS + j, S, stride=cells), :] = updated[:, j * NY : (j + 1) * NY]
-        return carry
-
-    lax.fori_loop(0, cells // ROWS, some, 0, unroll=4)
+            done_ref.at[block][pl.ds(j, S, stride=ROWS), :] = updated[:, j * NY : (j + 1) * NY]
+        for s in range(S):
+            copies.append(
+                pltpu.make_async_copy(
+                    done_ref.at[block, pl.ds(s * ROWS, ROWS)],
+                    out_ref.at[pl.ds(s * cells + block * ROWS, ROWS)],
+                    sems.at[len(copies)],
+                )
+            )
+            copies[-1].start()
+    for c in copies:
+        c.wait()
 
 
 def react(where, sent, kept, mine, other, rates, vapour, rate_matrix, stoich, prefactor):
@@ -232,7 +250,11 @@
         react_kernel,
         out_shape=jax.ShapeDtypeStruct((S * rows, NY), jnp.float32),
         in_specs=[SMEM] + [VMEM] * 8,
-        out_specs=VMEM,
+        out_specs=pl.BlockSpec(memory_space=pltpu.HBM),
+        scratch_shapes=[
+            pltpu.VMEM((rows // ROWS, S * ROWS, NY), jnp.float32),
+            pltpu.SemaphoreType.DMA((S * rows // ROWS,)),
+        ],
         compiler_params=LIMIT,
         name="react",
     )(

time: 79.5 us -> 79.4 us (level)
  transfers between devices with their start and end apart: 6 -> 6, of which waited for: 4 -> 4; matrix products, arithmetic and copies ran while one was open for 1% -> 1% of each run, Pallas kernels for 5% -> 4%
where the time goes in v9:
time: 79.4 us; the launch traced here: 78.4 us
  blocking collectives  33.7 us (42%)
  starting transfers between devices  29.7 us (37%)
  Pallas kernels  8.36 us (11%)
  waiting for transfers between devices  5.37 us (7%)
  local copies, waits for them, and re-layouts  0.89 us (1%)
    all_to_all x1, blocking collectives, per_device(): parts = lax.all_to_all(pair, CHIPS, 0, 0, tiled=True)  20.4 us
    all_to_all x1, blocking collectives, per_device(): mine = lax.all_to_all(spread, CHIPS, 0, 0, tiled=True)  13.3 us
    ppermute x1, starting transfers between devices, per_device(): from_outer = lax.ppermute(to_outer, 'slab', outer)  12.9 us
    ppermute x1, starting transfers between devices, per_device(): other = swap(sent)  5.24 us
    ppermute x1, starting transfers between devices, per_device(): swap(mine)  4.37 us
    ppermute x1, starting transfers between devices, per_device(): keep_inner = lax.ppermute(keep, 'slab', inner)  3.36 us
    pallas_call x1, Pallas kernels, react(): pl.pallas_call(react_kernel, out_shape=jax.ShapeDtypeStruct((S * rows, NY...  2.88 us
    ppermute x1, waiting for transfers between devices, per_device(): from_inner = lax.ppermute(to_inner, 'slab', inner)  2.73 us
  transfers between devices with their start and end apart: 6, of which 4 were waited for; matrix products, arithmetic and copies ran while one was open for 1% of the time, Pallas kernels for 4%

profile of v9, /device:TPU:57, one launch (start us, length us, event | category | flops | bytes accessed | tf_op | source)
XLA Modules:
  0.0 78.4 jit_solution(13985102602215391940)
XLA Ops:
  0.0 0.1 pad_add_fusion.where_ref
  0.1 2.0 %pack.1 = (f32[44,16,128]{2,1,0:T(8,128)S(1)}, f32[44,16,128]{2,1,0:T(8,128)S(1)}, f32[32,16,128]{2,1,0:T(8,128)S(1)}) custom-call(s32[2]{0:T(128)S(1)} %pad_add_fusion.where_ref, f32[1,16,4,16,128]{4,3,2,1,0:T(8,128)} %fields_ref.1, f32[3,4,16,128]{3,2,1,0:T(8,128)} %velocity_ref.1, f32[4,16,128]{2,1,0:T(8,128)} %diffusivity_ref.1), custom_call_target="tpu_custom_call" | custom-call | tf_op jit(solution)/shard_map/pack/pallas_call | solution.py:64
  2.0 12.9 %collective-permute-start = (f32[44,16,128]{2,1,0:T(8,128)S(1)}, f32[44,16,128]{2,1,0:T(8,128)S(1)}, u32[]{:S(2)}, u32[]{:S(2)}) collective-permute-start(f32[44,16,128]{2,1,0:T(8,128)S(1)} %get-tuple-element.10.own_outer_ref), channel_id=1, source_target_pairs={{1,2},{2,1},{3,4},{4,3},{5,6},{6,5},{7,8},{8,7},{9,10},{10,9},{11,... | collective-permute-start | bytes 1081352 | tf_op jit(solution)/shard_map/ppermute | solution.py:276
  15.0 1.9 %collective-permute-start.1 = (f32[44,16,128]{2,1,0:T(8,128)S(1)}, f32[44,16,128]{2,1,0:T(8,128)S(1)}, u32[]{:S(2)}, u32[]{:S(2)}) collective-permute-start(f32[44,16,128]{2,1,0:T(8,128)S(1)} %get-tuple-element.11.own_inner_ref), channel_id=1, source_target_pairs={{0,1},{1,0},{2,3},{3,2},{4,5},{5,4},{6,7},{7,6},{8,9},{9,8},{10,11... | collective-permute-start | bytes 1081352 | tf_op jit(solution)/shard_map/ppermute | solution.py:277
  16.9 3.4 %collective-permute-start.2 = (f32[32,16,128]{2,1,0:T(8,128)S(1)}, f32[32,16,128]{2,1,0:T(8,128)S(1)}, u32[]{:S(2)}, u32[]{:S(2)}) collective-permute-start(f32[32,16,128]{2,1,0:T(8,128)S(1)} %get-tuple-element.13.own_ref), channel_id=1, source_target_pairs={{0,1},{1,0},{2,3},{3,2},{4,5},{5,4},{6,7},{7,6},{8,9},{9,8},{10,11... | collective-permute-start | bytes 786440 | tf_op jit(solution)/shard_map/ppermute | solution.py:278
  20.3 1.9 %collective-permute-start.3 = (f32[32,16,128]{2,1,0:T(8,128)S(1)}, f32[32,16,128]{2,1,0:T(8,128)S(1)}, u32[]{:S(2)}, u32[]{:S(2)}) collective-permute-start(f32[32,16,128]{2,1,0:T(8,128)S(1)} %get-tuple-element.13.own_ref), channel_id=1, source_target_pairs={{1,2},{2,1},{3,4},{4,3},{5,6},{6,5},{7,8},{8,7},{9,10},{10,9},{11,... | collective-permute-start | bytes 786440 | tf_op jit(solution)/shard_map/ppermute | solution.py:279
  22.2 0.8 copy.12
  23.0 0.1 collective-permute-done.outer_ref
  23.1 2.7 %collective-permute-done.1.inner_ref = f32[44,16,128]{2,1,0:T(8,128)S(1)} collective-permute-done((f32[44,16,128]{2,1,0:T(8,128)S(1)}, f32[44,16,128]{2,1,0:T(8,128)S(1)}, u32[]{:S(2)}, u32[]{:S(2)}) %collective-permute-start.1) | collective-permute-done | bytes 360480 | tf_op jit(solution)/shard_map/ppermute | solution.py:277
  25.8 1.8 %transport_sent.1 = (f32[8,4,16,128]{3,2,1,0:T(8,128)S(1)}, f32[28,7,16,128]{3,2,1,0:T(8,128)S(1)}) custom-call(s32[2]{0:T(128)S(1)} %pad_add_fusion.where_ref, f32[4,3]{1,0:T(4,128)S(1)} %bitcast.21, f32[44,16,128]{2,1,0:T(8,128)S(1)} %get-tuple-element.10.own_outer_ref, f32[44,16,128]{2,1,0:T(8,128)S(1)} %get-tuple-element.11.own_inner_ref, ...), custom_call_target="tpu_custom_call" | custom-call | tf_op jit(solution)/shard_map/transport_sent/pallas_call | solution.py:150
  27.7 5.2 %collective-permute-start.4 = (f32[8,4,16,128]{3,2,1,0:T(8,128)S(1)}, f32[8,4,16,128]{3,2,1,0:T(8,128)S(1)}, u32[]{:S(2)}, u32[]{:S(2)}) collective-permute-start(f32[8,4,16,128]{3,2,1,0:T(8,128)S(1)} %get-tuple-element.12), channel_id=1, source_target_pairs={{0,16},{16,0},{1,17},{17,1},{2,18},{18,2},{3,19},{19,3},{4,20},{20... | collective-permute-start | bytes 786440 | tf_op jit(solution)/shard_map/ppermute | solution.py:282
  32.9 0.0 collective-permute-done.2.inner_ref
  32.9 1.5 %collective-permute-done.3.outer_ref = f32[32,16,128]{2,1,0:T(8,128)S(1)} collective-permute-done((f32[32,16,128]{2,1,0:T(8,128)S(1)}, f32[32,16,128]{2,1,0:T(8,128)S(1)}, u32[]{:S(2)}, u32[]{:S(2)}) %collective-permute-start.3) | collective-permute-done | bytes 262176 | tf_op jit(solution)/shard_map/ppermute | solution.py:279
  34.5 1.7 %transport_kept.1 = f32[8,4,16,128]{3,2,1,0:T(8,128)S(1)} custom-call(s32[2]{0:T(128)S(1)} %pad_add_fusion.where_ref, f32[32,16,128]{2,1,0:T(8,128)S(1)} %get-tuple-element.13.own_ref, f32[32,16,128]{2,1,0:T(8,128)S(1)} %collective-permute-done.2.inner_ref, f32[32,16,128]{2,1,0:T(8,128)S(1)} %collective-permute-done.3.outer_ref, ...), custom_call_target="tpu_custom_call" | custom-call | tf_op jit(solution)/shard_map/transport_kept/pallas_call | solution.py:168
  36.1 0.0 copy-start.3
  36.2 0.0 copy-start.4
  36.2 0.0 copy-start
  36.2 0.0 copy-start.1
  36.2 0.0 copy-start.2
  36.2 0.0 collective-permute-done.4
  36.3 20.4 %all_to_all.10 = f32[16,2,16,128]{3,2,1,0:T(8,128)S(1)} all-to-all(f32[16,2,16,128]{3,2,1,0:T(8,128)S(1)} %bitcast.22), channel_id=1, replica_groups=mesh['field_0'=4,'field_1'=4,'field_2'=2,'slab'=16] {'field_0','field_1'}, dimensions={0} | all-to-all | bytes 524288 | tf_op jit(solution)/shard_map/all_to_all | solution.py:286
  56.7 13.3 %all_to_all.11 = f32[16,2,16,128]{3,2,1,0:T(8,128)S(1)} all-to-all(f32[16,2,16,128]{3,2,1,0:T(8,128)S(1)} %broadcast_in_dim.2), channel_id=1, replica_groups=mesh['field_0'=4,'field_1'=4,'field_2'=2,'slab'=16] {'field_0','field_1'}, dimensions={0} | all-to-all | bytes 524288 | tf_op jit(solution)/shard_map/all_to_all | solution.py:289
  70.0 4.4 %collective-permute-start.5 = (f32[16,2,16,128]{3,2,1,0:T(8,128)S(1)}, f32[16,2,16,128]{3,2,1,0:T(8,128)S(1)}, u32[]{:S(2)}, u32[]{:S(2)}) collective-permute-start(f32[16,2,16,128]{3,2,1,0:T(8,128)S(1)} %all_to_all.11), channel_id=1, source_target_pairs={{0,16},{16,0},{1,17},{17,1},{2,18},{18,2},{3,19},{19,3},{4,20},{20... | collective-permute-start | bytes 786440 | tf_op jit(solution)/shard_map/ppermute | solution.py:290
  74.4 0.0 copy-done.3
  74.4 0.1 copy.13
  74.5 0.0 copy-done.4
  74.5 0.1 multiply_bitcast_fusion.stoich_ref
  74.6 1.0 %collective-permute-done.5 = f32[16,2,16,128]{3,2,1,0:T(8,128)S(1)} collective-permute-done((f32[16,2,16,128]{3,2,1,0:T(8,128)S(1)}, f32[16,2,16,128]{3,2,1,0:T(8,128)S(1)}, u32[]{:S(2)}, u32[]{:S(2)}) %collective-permute-start.5) | collective-permute-done | bytes 262176 | tf_op jit(solution)/shard_map/ppermute | solution.py:290
  75.6 0.0 copy-done
  75.6 0.0 copy-done.1
  75.6 0.0 copy-done.2
  75.6 2.9 %react.1 = f32[1024,128]{1,0:T(8,128)} custom-call(s32[2]{0:T(128)S(1)} %pad_add_fusion.where_ref, f32[512,128]{1,0:T(8,128)S(1)} %bitcast.16, f32[512,128]{1,0:T(8,128)S(1)} %bitcast.14, f32[512,128]{1,0:T(8,128)S(1)} %bitcast.15, f32[512,128]{1,0:T(8,128)S(1)} %bitcast.17, f32[64,128]{1,0:T(8,128)S(1)} %bitcast.18, f32[64,128]{1,0:T(8,128)S(1)} %bitcast.19, ...), custom_call_target="tpu_custom_call" | custom-call | tf_op jit(solution)/shard_map/react/pallas_call | solution.py:249
  (4 shorter events, 0.1 us)
Async XLA Ops:
  2.0 21.0 %collective-permute-start = (f32[44,16,128]{2,1,0:T(8,128)S(1)}, f32[44,16,128]{2,1,0:T(8,128)S(1)}, u32[]{:S(2)}, u32[]{:S(2)}) collective-permute-start(f32[44,16,128]{2,1,0:T(8,128)S(1)} %get-tuple-element.10.own_outer_ref), channel_id=1, source_target_pairs={{1,2},{2,1},{3,4},{4,3},{5,6},{6,5},{7,8},{8,7},{9,10},{10,9},{11,... | collective-permute-start | bytes 1081352 | tf_op jit(solution)/shard_map/ppermute | solution.py:276
  15.0 10.9 %collective-permute-start.1 = (f32[44,16,128]{2,1,0:T(8,128)S(1)}, f32[44,16,128]{2,1,0:T(8,128)S(1)}, u32[]{:S(2)}, u32[]{:S(2)}) collective-permute-start(f32[44,16,128]{2,1,0:T(8,128)S(1)} %get-tuple-element.11.own_inner_ref), channel_id=1, source_target_pairs={{0,1},{1,0},{2,3},{3,2},{4,5},{5,4},{6,7},{7,6},{8,9},{9,8},{10,11... | collective-permute-start | bytes 1081352 | tf_op jit(solution)/shard_map/ppermute | solution.py:277
  16.9 16.0 %collective-permute-start.2 = (f32[32,16,128]{2,1,0:T(8,128)S(1)}, f32[32,16,128]{2,1,0:T(8,128)S(1)}, u32[]{:S(2)}, u32[]{:S(2)}) collective-permute-start(f32[32,16,128]{2,1,0:T(8,128)S(1)} %get-tuple-element.13.own_ref), channel_id=1, source_target_pairs={{0,1},{1,0},{2,3},{3,2},{4,5},{5,4},{6,7},{7,6},{8,9},{9,8},{10,11... | collective-permute-start | bytes 786440 | tf_op jit(solution)/shard_map/ppermute | solution.py:278
  20.3 14.2 %collective-permute-start.3 = (f32[32,16,128]{2,1,0:T(8,128)S(1)}, f32[32,16,128]{2,1,0:T(8,128)S(1)}, u32[]{:S(2)}, u32[]{:S(2)}) collective-permute-start(f32[32,16,128]{2,1,0:T(8,128)S(1)} %get-tuple-element.13.own_ref), channel_id=1, source_target_pairs={{1,2},{2,1},{3,4},{4,3},{5,6},{6,5},{7,8},{8,7},{9,10},{10,9},{11,... | collective-permute-start | bytes 786440 | tf_op jit(solution)/shard_map/ppermute | solution.py:279
  27.7 8.5 %collective-permute-start.4 = (f32[8,4,16,128]{3,2,1,0:T(8,128)S(1)}, f32[8,4,16,128]{3,2,1,0:T(8,128)S(1)}, u32[]{:S(2)}, u32[]{:S(2)}) collective-permute-start(f32[8,4,16,128]{3,2,1,0:T(8,128)S(1)} %get-tuple-element.12), channel_id=1, source_target_pairs={{0,16},{16,0},{1,17},{17,1},{2,18},{18,2},{3,19},{19,3},{4,20},{20... | collective-permute-start | bytes 786440 | tf_op jit(solution)/shard_map/ppermute | solution.py:282
  36.1 38.3 %copy-start.3 = (f32[16,32]{1,0:T(8,128)S(1)}, f32[16,32]{1,0:T(8,128)}, u32[]{:S(2)}) copy-start(f32[16,32]{1,0:T(8,128)} %param.16) | copy-start | bytes 6148
  36.2 38.4 %copy-start.4 = (f32[32]{0:T(128)S(1)}, f32[32]{0:T(128)}, u32[]{:S(2)}) copy-start(f32[32]{0:T(128)} %param.17) | copy-start | bytes 388
  36.2 39.4 %copy-start = (f32[4,16,128]{2,1,0:T(8,128)S(1)}, f32[4,16,128]{2,1,0:T(8,128)}, u32[]{:S(2)}) copy-start(f32[4,16,128]{2,1,0:T(8,128)} %param.13) | copy-start | bytes 98308
  36.2 39.4 %copy-start.1 = (f32[4,16,128]{2,1,0:T(8,128)S(1)}, f32[4,16,128]{2,1,0:T(8,128)}, u32[]{:S(2)}) copy-start(f32[4,16,128]{2,1,0:T(8,128)} %param.14) | copy-start | bytes 98308
  36.2 39.4 %copy-start.2 = (f32[32,16]{0,1:T(8,128)S(1)}, f32[32,16]{0,1:T(8,128)}, u32[]{:S(2)}) copy-start(f32[32,16]{0,1:T(8,128)} %param.15) | copy-start | bytes 6148
  70.0 5.5 %collective-permute-start.5 = (f32[16,2,16,128]{3,2,1,0:T(8,128)S(1)}, f32[16,2,16,128]{3,2,1,0:T(8,128)S(1)}, u32[]{:S(2)}, u32[]{:S(2)}) collective-permute-start(f32[16,2,16,128]{3,2,1,0:T(8,128)S(1)} %all_to_all.11), channel_id=1, source_target_pairs={{0,16},{16,0},{1,17},{17,1},{2,18},{18,2},{3,19},{19,3},{4,20},{20... | collective-permute-start | bytes 786440 | tf_op jit(solution)/shard_map/ppermute | solution.py:290

commit v10 on v9

--- a/solution.py
+++ b/solution.py
@@ -16,7 +16,7 @@
 NZ = 16
 NY = 128
 HALF = S // 2
-CHIPS = ("field_0", "field_1")
+CHIPS = ("field_1", "field_0")
 FIELD = ("field_0", "field_1", "field_2")
 
 
@@ -160,11 +160,11 @@
     )(*args)
 
 
-def kept_kernel(where_ref, own_ref, inner_ref, outer_ref, coef_ref, out_ref):
+def kept_kernel(where_ref, own_ref, outer_ref, inner_ref, coef_ref, out_ref):
     substeps(extended(where_ref, own_ref, inner_ref, outer_ref), coef_ref, out_ref)
 
 
-def transport_kept(where, own, inner, outer, coef):
+def transport_kept(where, own, outer, inner, coef):
     return pl.pallas_call(
         kept_kernel,
         out_shape=jax.ShapeDtypeStruct((HALF, X, NZ, NY), jnp.float32),
@@ -172,7 +172,7 @@
         out_specs=VMEM,
         compiler_params=LIMIT,
         name="transport_kept",
-    )(where, own, inner, outer, coef)
+    )(where, own, outer, inner, coef)
 
 
 def halves(x):
@@ -275,12 +275,12 @@
     to_outer, to_inner, keep = pack(where, fields, velocity, diffusivity)
     from_outer = lax.ppermute(to_outer, "slab", outer)
     from_inner = lax.ppermute(to_inner, "slab", inner)
+    keep_outer = lax.ppermute(keep, "slab", outer)
     keep_inner = lax.ppermute(keep, "slab", inner)
-    keep_outer = lax.ppermute(keep, "slab", outer)
     swap = functools.partial(lax.ppermute, axis_name="field_2", perm=[(0, 1), (1, 0)])
     sent, coef = transport_sent(where, noise[0], to_outer, to_inner, from_outer, from_inner)
     other = swap(sent)
-    kept = transport_kept(where, keep, keep_inner, keep_outer, coef)
+    kept = transport_kept(where, keep, keep_outer, keep_inner, coef)
     chips = lax.axis_size(CHIPS)
     pair = (kept + other).reshape(chips, -1, NZ, NY)
     parts = lax.all_to_all(pair, CHIPS, 0, 0, tiled=True)

time: 79.4 us -> 79.6 us (level)
  blocking collectives: 33.7 us -> 36 us
  waiting for transfers between devices: 5.37 us -> 3.85 us
    all_to_all x1, blocking collectives: 20.4 us -> 23.6 us  [per_device(): parts = lax.all_to_all(pair, CHIPS, 0, 0, tiled=True)]
    ppermute x1, waiting for transfers between devices: 1.53 us -> 0.01 us  [per_device(): keep_outer = lax.ppermute(keep, 'slab', outer)]
    all_to_all x1, blocking collectives: 13.3 us -> 12.4 us  [per_device(): mine = lax.all_to_all(spread, CHIPS, 0, 0, tiled=True)]
  transfers between devices with their start and end apart: 6 -> 6, of which waited for: 4 -> 3; matrix products, arithmetic and copies ran while one was open for 1% -> 1% of each run, Pallas kernels for 4% -> 4%
where the time goes in v10:
time: 79.6 us; the launch traced here: 79.2 us
  blocking collectives  36 us (45%)
  starting transfers between devices  29.7 us (37%)
  Pallas kernels  8.37 us (11%)
  waiting for transfers between devices  3.85 us (5%)
  local copies, waits for them, and re-layouts  0.89 us (1%)
    all_to_all x1, blocking collectives, per_device(): parts = lax.all_to_all(pair, CHIPS, 0, 0, tiled=True)  23.6 us
    ppermute x1, starting transfers between devices, per_device(): from_outer = lax.ppermute(to_outer, 'slab', outer)  12.9 us
    all_to_all x1, blocking collectives, per_device(): mine = lax.all_to_all(spread, CHIPS, 0, 0, tiled=True)  12.4 us
    ppermute x1, starting transfers between devices, per_device(): other = swap(sent)  5.24 us
    ppermute x1, starting transfers between devices, per_device(): swap(mine)  4.35 us
    pallas_call x1, Pallas kernels, react(): pl.pallas_call(react_kernel, out_shape=jax.ShapeDtypeStruct((S * rows, NY...  2.88 us
    ppermute x1, starting transfers between devices, per_device(): keep_inner = lax.ppermute(keep, 'slab', inner)  2.84 us
    ppermute x1, waiting for transfers between devices, per_device(): from_inner = lax.ppermute(to_inner, 'slab', inner)  2.73 us
  transfers between devices with their start and end apart: 6, of which 3 were waited for; matrix products, arithmetic and copies ran while one was open for 1% of the time, Pallas kernels for 4%

profile of v10, /device:TPU:57, one launch (start us, length us, event | category | flops | bytes accessed | tf_op | source)
XLA Modules:
  0.0 79.2 jit_solution(4526300158295420280)
XLA Ops:
  0.0 0.1 pad_add_fusion.where_ref
  0.1 2.0 %pack.1 = (f32[44,16,128]{2,1,0:T(8,128)S(1)}, f32[44,16,128]{2,1,0:T(8,128)S(1)}, f32[32,16,128]{2,1,0:T(8,128)S(1)}) custom-call(s32[2]{0:T(128)S(1)} %pad_add_fusion.where_ref, f32[1,16,4,16,128]{4,3,2,1,0:T(8,128)} %fields_ref.1, f32[3,4,16,128]{3,2,1,0:T(8,128)} %velocity_ref.1, f32[4,16,128]{2,1,0:T(8,128)} %diffusivity_ref.1), custom_call_target="tpu_custom_call" | custom-call | tf_op jit(solution)/shard_map/pack/pallas_call | solution.py:64
  2.0 12.9 %collective-permute-start = (f32[44,16,128]{2,1,0:T(8,128)S(1)}, f32[44,16,128]{2,1,0:T(8,128)S(1)}, u32[]{:S(2)}, u32[]{:S(2)}) collective-permute-start(f32[44,16,128]{2,1,0:T(8,128)S(1)} %get-tuple-element.10.own_outer_ref), channel_id=1, source_target_pairs={{1,2},{2,1},{3,4},{4,3},{5,6},{6,5},{7,8},{8,7},{9,10},{10,9},{11,... | collective-permute-start | bytes 1081352 | tf_op jit(solution)/shard_map/ppermute | solution.py:276
  15.0 1.9 %collective-permute-start.1 = (f32[44,16,128]{2,1,0:T(8,128)S(1)}, f32[44,16,128]{2,1,0:T(8,128)S(1)}, u32[]{:S(2)}, u32[]{:S(2)}) collective-permute-start(f32[44,16,128]{2,1,0:T(8,128)S(1)} %get-tuple-element.11.own_inner_ref), channel_id=1, source_target_pairs={{0,1},{1,0},{2,3},{3,2},{4,5},{5,4},{6,7},{7,6},{8,9},{9,8},{10,11... | collective-permute-start | bytes 1081352 | tf_op jit(solution)/shard_map/ppermute | solution.py:277
  16.9 2.4 %collective-permute-start.2 = (f32[32,16,128]{2,1,0:T(8,128)S(1)}, f32[32,16,128]{2,1,0:T(8,128)S(1)}, u32[]{:S(2)}, u32[]{:S(2)}) collective-permute-start(f32[32,16,128]{2,1,0:T(8,128)S(1)} %get-tuple-element.13.own_ref), channel_id=1, source_target_pairs={{1,2},{2,1},{3,4},{4,3},{5,6},{6,5},{7,8},{8,7},{9,10},{10,9},{11,... | collective-permute-start | bytes 786440 | tf_op jit(solution)/shard_map/ppermute | solution.py:278
  19.3 2.8 %collective-permute-start.3 = (f32[32,16,128]{2,1,0:T(8,128)S(1)}, f32[32,16,128]{2,1,0:T(8,128)S(1)}, u32[]{:S(2)}, u32[]{:S(2)}) collective-permute-start(f32[32,16,128]{2,1,0:T(8,128)S(1)} %get-tuple-element.13.own_ref), channel_id=1, source_target_pairs={{0,1},{1,0},{2,3},{3,2},{4,5},{5,4},{6,7},{7,6},{8,9},{9,8},{10,11... | collective-permute-start | bytes 786440 | tf_op jit(solution)/shard_map/ppermute | solution.py:279
  22.2 0.8 copy.12
  23.0 0.1 collective-permute-done.outer_ref
  23.1 2.7 %collective-permute-done.1.inner_ref = f32[44,16,128]{2,1,0:T(8,128)S(1)} collective-permute-done((f32[44,16,128]{2,1,0:T(8,128)S(1)}, f32[44,16,128]{2,1,0:T(8,128)S(1)}, u32[]{:S(2)}, u32[]{:S(2)}) %collective-permute-start.1) | collective-permute-done | bytes 360480 | tf_op jit(solution)/shard_map/ppermute | solution.py:277
  25.8 1.8 %transport_sent.1 = (f32[8,4,16,128]{3,2,1,0:T(8,128)S(1)}, f32[28,7,16,128]{3,2,1,0:T(8,128)S(1)}) custom-call(s32[2]{0:T(128)S(1)} %pad_add_fusion.where_ref, f32[4,3]{1,0:T(4,128)S(1)} %bitcast.21, f32[44,16,128]{2,1,0:T(8,128)S(1)} %get-tuple-element.10.own_outer_ref, f32[44,16,128]{2,1,0:T(8,128)S(1)} %get-tuple-element.11.own_inner_ref, ...), custom_call_target="tpu_custom_call" | custom-call | tf_op jit(solution)/shard_map/transport_sent/pallas_call | solution.py:150
  27.7 5.2 %collective-permute-start.4 = (f32[8,4,16,128]{3,2,1,0:T(8,128)S(1)}, f32[8,4,16,128]{3,2,1,0:T(8,128)S(1)}, u32[]{:S(2)}, u32[]{:S(2)}) collective-permute-start(f32[8,4,16,128]{3,2,1,0:T(8,128)S(1)} %get-tuple-element.12), channel_id=1, source_target_pairs={{0,16},{16,0},{1,17},{17,1},{2,18},{18,2},{3,19},{19,3},{4,20},{20... | collective-permute-start | bytes 786440 | tf_op jit(solution)/shard_map/ppermute | solution.py:282
  32.9 0.0 collective-permute-done.2.outer_ref
  32.9 0.0 collective-permute-done.3.inner_ref
  32.9 1.7 %transport_kept.1 = f32[8,4,16,128]{3,2,1,0:T(8,128)S(1)} custom-call(s32[2]{0:T(128)S(1)} %pad_add_fusion.where_ref, f32[32,16,128]{2,1,0:T(8,128)S(1)} %get-tuple-element.13.own_ref, f32[32,16,128]{2,1,0:T(8,128)S(1)} %collective-permute-done.2.outer_ref, f32[32,16,128]{2,1,0:T(8,128)S(1)} %collective-permute-done.3.inner_ref, ...), custom_call_target="tpu_custom_call" | custom-call | tf_op jit(solution)/shard_map/transport_kept/pallas_call | solution.py:168
  34.6 0.0 copy-start.3
  34.6 0.0 copy-start.4
  34.6 0.0 copy-start
  34.7 0.0 copy-start.1
  34.7 0.0 copy-start.2
  34.7 0.0 collective-permute-done.4
  34.7 23.6 %all_to_all.10 = f32[16,2,16,128]{3,2,1,0:T(8,128)S(1)} all-to-all(f32[16,2,16,128]{3,2,1,0:T(8,128)S(1)} %bitcast.22), channel_id=1, replica_groups=mesh['field_0'=4,'field_1'=4,'field_2'=2,'slab'=16] {'field_1','field_0'}, dimensions={0} | all-to-all | bytes 524288 | tf_op jit(solution)/shard_map/all_to_all | solution.py:286
  58.4 12.4 %all_to_all.11 = f32[16,2,16,128]{3,2,1,0:T(8,128)S(1)} all-to-all(f32[16,2,16,128]{3,2,1,0:T(8,128)S(1)} %broadcast_in_dim.2), channel_id=1, replica_groups=mesh['field_0'=4,'field_1'=4,'field_2'=2,'slab'=16] {'field_1','field_0'}, dimensions={0} | all-to-all | bytes 524288 | tf_op jit(solution)/shard_map/all_to_all | solution.py:289
  70.8 4.3 %collective-permute-start.5 = (f32[16,2,16,128]{3,2,1,0:T(8,128)S(1)}, f32[16,2,16,128]{3,2,1,0:T(8,128)S(1)}, u32[]{:S(2)}, u32[]{:S(2)}) collective-permute-start(f32[16,2,16,128]{3,2,1,0:T(8,128)S(1)} %all_to_all.11), channel_id=1, source_target_pairs={{0,16},{16,0},{1,17},{17,1},{2,18},{18,2},{3,19},{19,3},{4,20},{20... | collective-permute-start | bytes 786440 | tf_op jit(solution)/shard_map/ppermute | solution.py:290
  75.1 0.0 copy-done.3
  75.1 0.1 copy.13
  75.2 0.0 copy-done.4
  75.2 0.1 multiply_bitcast_fusion.stoich_ref
  75.3 1.0 %collective-permute-done.5 = f32[16,2,16,128]{3,2,1,0:T(8,128)S(1)} collective-permute-done((f32[16,2,16,128]{3,2,1,0:T(8,128)S(1)}, f32[16,2,16,128]{3,2,1,0:T(8,128)S(1)}, u32[]{:S(2)}, u32[]{:S(2)}) %collective-permute-start.5) | collective-permute-done | bytes 262176 | tf_op jit(solution)/shard_map/ppermute | solution.py:290
  76.3 0.0 copy-done
  76.3 0.0 copy-done.1
  76.3 0.0 copy-done.2
  76.3 2.9 %react.1 = f32[1024,128]{1,0:T(8,128)} custom-call(s32[2]{0:T(128)S(1)} %pad_add_fusion.where_ref, f32[512,128]{1,0:T(8,128)S(1)} %bitcast.16, f32[512,128]{1,0:T(8,128)S(1)} %bitcast.14, f32[512,128]{1,0:T(8,128)S(1)} %bitcast.15, f32[512,128]{1,0:T(8,128)S(1)} %bitcast.17, f32[64,128]{1,0:T(8,128)S(1)} %bitcast.18, f32[64,128]{1,0:T(8,128)S(1)} %bitcast.19, ...), custom_call_target="tpu_custom_call" | custom-call | tf_op jit(solution)/shard_map/react/pallas_call | solution.py:249
  (4 shorter events, 0.1 us)
Async XLA Ops:
  2.0 21.0 %collective-permute-start = (f32[44,16,128]{2,1,0:T(8,128)S(1)}, f32[44,16,128]{2,1,0:T(8,128)S(1)}, u32[]{:S(2)}, u32[]{:S(2)}) collective-permute-start(f32[44,16,128]{2,1,0:T(8,128)S(1)} %get-tuple-element.10.own_outer_ref), channel_id=1, source_target_pairs={{1,2},{2,1},{3,4},{4,3},{5,6},{6,5},{7,8},{8,7},{9,10},{10,9},{11,... | collective-permute-start | bytes 1081352 | tf_op jit(solution)/shard_map/ppermute | solution.py:276
  15.0 10.9 %collective-permute-start.1 = (f32[44,16,128]{2,1,0:T(8,128)S(1)}, f32[44,16,128]{2,1,0:T(8,128)S(1)}, u32[]{:S(2)}, u32[]{:S(2)}) collective-permute-start(f32[44,16,128]{2,1,0:T(8,128)S(1)} %get-tuple-element.11.own_inner_ref), channel_id=1, source_target_pairs={{0,1},{1,0},{2,3},{3,2},{4,5},{5,4},{6,7},{7,6},{8,9},{9,8},{10,11... | collective-permute-start | bytes 1081352 | tf_op jit(solution)/shard_map/ppermute | solution.py:277
  16.9 16.0 %collective-permute-start.2 = (f32[32,16,128]{2,1,0:T(8,128)S(1)}, f32[32,16,128]{2,1,0:T(8,128)S(1)}, u32[]{:S(2)}, u32[]{:S(2)}) collective-permute-start(f32[32,16,128]{2,1,0:T(8,128)S(1)} %get-tuple-element.13.own_ref), channel_id=1, source_target_pairs={{1,2},{2,1},{3,4},{4,3},{5,6},{6,5},{7,8},{8,7},{9,10},{10,9},{11,... | collective-permute-start | bytes 786440 | tf_op jit(solution)/shard_map/ppermute | solution.py:278
  19.3 13.6 %collective-permute-start.3 = (f32[32,16,128]{2,1,0:T(8,128)S(1)}, f32[32,16,128]{2,1,0:T(8,128)S(1)}, u32[]{:S(2)}, u32[]{:S(2)}) collective-permute-start(f32[32,16,128]{2,1,0:T(8,128)S(1)} %get-tuple-element.13.own_ref), channel_id=1, source_target_pairs={{0,1},{1,0},{2,3},{3,2},{4,5},{5,4},{6,7},{7,6},{8,9},{9,8},{10,11... | collective-permute-start | bytes 786440 | tf_op jit(solution)/shard_map/ppermute | solution.py:279
  27.7 7.0 %collective-permute-start.4 = (f32[8,4,16,128]{3,2,1,0:T(8,128)S(1)}, f32[8,4,16,128]{3,2,1,0:T(8,128)S(1)}, u32[]{:S(2)}, u32[]{:S(2)}) collective-permute-start(f32[8,4,16,128]{3,2,1,0:T(8,128)S(1)} %get-tuple-element.12), channel_id=1, source_target_pairs={{0,16},{16,0},{1,17},{17,1},{2,18},{18,2},{3,19},{19,3},{4,20},{20... | collective-permute-start | bytes 786440 | tf_op jit(solution)/shard_map/ppermute | solution.py:282
  34.6 40.5 %copy-start.3 = (f32[16,32]{1,0:T(8,128)S(1)}, f32[16,32]{1,0:T(8,128)}, u32[]{:S(2)}) copy-start(f32[16,32]{1,0:T(8,128)} %param.16) | copy-start | bytes 6148
  34.6 40.6 %copy-start.4 = (f32[32]{0:T(128)S(1)}, f32[32]{0:T(128)}, u32[]{:S(2)}) copy-start(f32[32]{0:T(128)} %param.17) | copy-start | bytes 388
  34.6 41.6 %copy-start = (f32[4,16,128]{2,1,0:T(8,128)S(1)}, f32[4,16,128]{2,1,0:T(8,128)}, u32[]{:S(2)}) copy-start(f32[4,16,128]{2,1,0:T(8,128)} %param.13) | copy-start | bytes 98308
  34.7 41.6 %copy-start.1 = (f32[4,16,128]{2,1,0:T(8,128)S(1)}, f32[4,16,128]{2,1,0:T(8,128)}, u32[]{:S(2)}) copy-start(f32[4,16,128]{2,1,0:T(8,128)} %param.14) | copy-start | bytes 98308
  34.7 41.6 %copy-start.2 = (f32[32,16]{0,1:T(8,128)S(1)}, f32[32,16]{0,1:T(8,128)}, u32[]{:S(2)}) copy-start(f32[32,16]{0,1:T(8,128)} %param.15) | copy-start | bytes 6148
  70.8 5.5 %collective-permute-start.5 = (f32[16,2,16,128]{3,2,1,0:T(8,128)S(1)}, f32[16,2,16,128]{3,2,1,0:T(8,128)S(1)}, u32[]{:S(2)}, u32[]{:S(2)}) collective-permute-start(f32[16,2,16,128]{3,2,1,0:T(8,128)S(1)} %all_to_all.11), channel_id=1, source_target_pairs={{0,16},{16,0},{1,17},{17,1},{2,18},{18,2},{3,19},{19,3},{4,20},{20... | collective-permute-start | bytes 786440 | tf_op jit(solution)/shard_map/ppermute | solution.py:290

commit v11 on v8

--- a/solution.py
+++ b/solution.py
@@ -25,7 +25,7 @@
     for _k in range(SUBSTEPS):
         if _k < _i < 3 * X - 1 - _k:
             SLOT[_k, _i] = len(SLOT)
-TOGETHER = 4
+TOGETHER = 8
 VMEM = pl.BlockSpec(memory_space=pltpu.VMEM)
 SMEM = pl.BlockSpec(memory_space=pltpu.SMEM)
 LIMIT = pltpu.CompilerParams(vmem_limit_bytes=48 * 2**20)
@@ -191,7 +191,8 @@
     )
 
 
-ROWS = 16
+ROWS = 32
+TILE = 8
 
 
 def react_kernel(
@@ -203,27 +204,30 @@
     first = where_ref[0] == 0
     fuel = lax.broadcasted_iota(jnp.int32, (S, NY), 0) == 0
 
-    def some(step, carry):
+    def by_row(ref, row):
+        return jnp.swapaxes(jnp.stack([ref[pl.ds(s * cells + row, TILE), :] for s in range(HALF)]), 0, 1)
+
+    for block in range(0, cells, ROWS):
         mixed = []
-        for j in range(ROWS):
-            r = step * ROWS + j
-            sent, kept, mine, other = (
-                ref[pl.ds(r, HALF, stride=cells), :] for ref in (sent_ref, kept_ref, mine_ref, other_ref)
-            )
-            rate = 0.5 * rate_ref[pl.ds(r, 1), :]
-            vapour = vapour_ref[pl.ds(r, 1), :]
-            kept = kept - rate * (kept - mine)
-            sent = sent - rate * (sent - other)
-            both = jnp.concatenate([jnp.where(first, kept, sent), jnp.where(first, sent, kept)], 0)
-            mixed.append(both + jnp.where(fuel, vapour, 0.0))
+        for row in range(block, block + ROWS, TILE):
+            tiles = [by_row(ref, row) for ref in (sent_ref, kept_ref, mine_ref, other_ref)]
+            for j in range(TILE):
+                sent, kept, mine, other = (tile[j] for tile in tiles)
+                rate = 0.5 * rate_ref[pl.ds(row + j, 1), :]
+                vapour = vapour_ref[pl.ds(row + j, 1), :]
+                kept = kept - rate * (kept - mine)
+                sent = sent - rate * (sent - other)
+                both = jnp.concatenate([jnp.where(first, kept, sent), jnp.where(first, sent, kept)], 0)
+                mixed.append(both + jnp.where(fuel, vapour, 0.0))
         mixed = jnp.concatenate(mixed, 1)
         speed = jnp.exp(2.0 * jnp.tanh(product(drive_weights, mixed)))
         updated = mixed + product(source_weights, speed)
-        for j in range(ROWS):
-            out_ref[pl.ds(step * ROWS + j, S, stride=cells), :] = updated[:, j * NY : (j + 1) * NY]
-        return carry
-
-    lax.fori_loop(0, cells // ROWS, some, 0, unroll=4)
+        for half in range(0, S, HALF):
+            for row in range(0, ROWS, TILE):
+                tile = [updated[half : half + HALF, (row + j) * NY : (row + j + 1) * NY] for j in range(TILE)]
+                tile = jnp.swapaxes(jnp.stack(tile), 0, 1)
+                for s in range(HALF):
+                    out_ref[pl.ds((half + s) * cells + block + row, TILE), :] = tile[s]
 
 
 def react(where, sent, kept, mine, other, rates, vapour, rate_matrix, stoich, prefactor):

time: 79.5 us -> 78.7 us (0.990)
  Pallas kernels: 8.55 us -> 7.7 us
where the time goes in v11:
time: 78.7 us; the launch traced here: 77.8 us
  blocking collectives  33.7 us (43%)
  starting transfers between devices  29.7 us (38%)
  Pallas kernels  7.7 us (10%)
  waiting for transfers between devices  5.37 us (7%)
  local copies, waits for them, and re-layouts  0.89 us (1%)
    all_to_all x1, blocking collectives, per_device(): parts = lax.all_to_all(pair, CHIPS, 0, 0, tiled=True)  20.4 us
    all_to_all x1, blocking collectives, per_device(): mine = lax.all_to_all(spread, CHIPS, 0, 0, tiled=True)  13.3 us
    ppermute x1, starting transfers between devices, per_device(): from_outer = lax.ppermute(to_outer, 'slab', outer)  12.9 us
    ppermute x1, starting transfers between devices, per_device(): other = swap(sent)  5.24 us
    ppermute x1, starting transfers between devices, per_device(): swap(mine)  4.37 us
    ppermute x1, starting transfers between devices, per_device(): keep_inner = lax.ppermute(keep, 'slab', inner)  3.36 us
    ppermute x1, waiting for transfers between devices, per_device(): from_inner = lax.ppermute(to_inner, 'slab', inner)  2.73 us
    pallas_call x1, Pallas kernels, react(): pl.pallas_call(react_kernel, out_shape=jax.ShapeDtypeStruct((S * rows, NY...  2.22 us
  transfers between devices with their start and end apart: 6, of which 4 were waited for; matrix products, arithmetic and copies ran while one was open for 1% of the time, Pallas kernels for 5%

profile of v11, /device:TPU:57, one launch (start us, length us, event | category | flops | bytes accessed | tf_op | source)
XLA Modules:
  0.0 77.8 jit_solution(5991510150577436602)
XLA Ops:
  0.0 0.1 pad_add_fusion.where_ref
  0.1 2.0 %pack.1 = (f32[44,16,128]{2,1,0:T(8,128)S(1)}, f32[44,16,128]{2,1,0:T(8,128)S(1)}, f32[32,16,128]{2,1,0:T(8,128)S(1)}) custom-call(s32[2]{0:T(128)S(1)} %pad_add_fusion.where_ref, f32[1,16,4,16,128]{4,3,2,1,0:T(8,128)} %fields_ref.1, f32[3,4,16,128]{3,2,1,0:T(8,128)} %velocity_ref.1, f32[4,16,128]{2,1,0:T(8,128)} %diffusivity_ref.1), custom_call_target="tpu_custom_call" | custom-call | tf_op jit(solution)/shard_map/pack/pallas_call | solution.py:64
  2.0 12.9 %collective-permute-start = (f32[44,16,128]{2,1,0:T(8,128)S(1)}, f32[44,16,128]{2,1,0:T(8,128)S(1)}, u32[]{:S(2)}, u32[]{:S(2)}) collective-permute-start(f32[44,16,128]{2,1,0:T(8,128)S(1)} %get-tuple-element.10.own_outer_ref), channel_id=1, source_target_pairs={{1,2},{2,1},{3,4},{4,3},{5,6},{6,5},{7,8},{8,7},{9,10},{10,9},{11,... | collective-permute-start | bytes 1081352 | tf_op jit(solution)/shard_map/ppermute | solution.py:258
  15.0 1.9 %collective-permute-start.1 = (f32[44,16,128]{2,1,0:T(8,128)S(1)}, f32[44,16,128]{2,1,0:T(8,128)S(1)}, u32[]{:S(2)}, u32[]{:S(2)}) collective-permute-start(f32[44,16,128]{2,1,0:T(8,128)S(1)} %get-tuple-element.11.own_inner_ref), channel_id=1, source_target_pairs={{0,1},{1,0},{2,3},{3,2},{4,5},{5,4},{6,7},{7,6},{8,9},{9,8},{10,11... | collective-permute-start | bytes 1081352 | tf_op jit(solution)/shard_map/ppermute | solution.py:259
  16.9 3.4 %collective-permute-start.2 = (f32[32,16,128]{2,1,0:T(8,128)S(1)}, f32[32,16,128]{2,1,0:T(8,128)S(1)}, u32[]{:S(2)}, u32[]{:S(2)}) collective-permute-start(f32[32,16,128]{2,1,0:T(8,128)S(1)} %get-tuple-element.13.own_ref), channel_id=1, source_target_pairs={{0,1},{1,0},{2,3},{3,2},{4,5},{5,4},{6,7},{7,6},{8,9},{9,8},{10,11... | collective-permute-start | bytes 786440 | tf_op jit(solution)/shard_map/ppermute | solution.py:260
  20.3 1.9 %collective-permute-start.3 = (f32[32,16,128]{2,1,0:T(8,128)S(1)}, f32[32,16,128]{2,1,0:T(8,128)S(1)}, u32[]{:S(2)}, u32[]{:S(2)}) collective-permute-start(f32[32,16,128]{2,1,0:T(8,128)S(1)} %get-tuple-element.13.own_ref), channel_id=1, source_target_pairs={{1,2},{2,1},{3,4},{4,3},{5,6},{6,5},{7,8},{8,7},{9,10},{10,9},{11,... | collective-permute-start | bytes 786440 | tf_op jit(solution)/shard_map/ppermute | solution.py:261
  22.2 0.8 copy.12
  23.0 0.1 collective-permute-done.outer_ref
  23.1 2.7 %collective-permute-done.1.inner_ref = f32[44,16,128]{2,1,0:T(8,128)S(1)} collective-permute-done((f32[44,16,128]{2,1,0:T(8,128)S(1)}, f32[44,16,128]{2,1,0:T(8,128)S(1)}, u32[]{:S(2)}, u32[]{:S(2)}) %collective-permute-start.1) | collective-permute-done | bytes 360480 | tf_op jit(solution)/shard_map/ppermute | solution.py:259
  25.8 1.8 %transport_sent.1 = (f32[8,4,16,128]{3,2,1,0:T(8,128)S(1)}, f32[28,7,16,128]{3,2,1,0:T(8,128)S(1)}) custom-call(s32[2]{0:T(128)S(1)} %pad_add_fusion.where_ref, f32[4,3]{1,0:T(4,128)S(1)} %bitcast.21, f32[44,16,128]{2,1,0:T(8,128)S(1)} %get-tuple-element.10.own_outer_ref, f32[44,16,128]{2,1,0:T(8,128)S(1)} %get-tuple-element.11.own_inner_ref, ...), custom_call_target="tpu_custom_call" | custom-call | tf_op jit(solution)/shard_map/transport_sent/pallas_call | solution.py:150
  27.7 5.2 %collective-permute-start.4 = (f32[8,4,16,128]{3,2,1,0:T(8,128)S(1)}, f32[8,4,16,128]{3,2,1,0:T(8,128)S(1)}, u32[]{:S(2)}, u32[]{:S(2)}) collective-permute-start(f32[8,4,16,128]{3,2,1,0:T(8,128)S(1)} %get-tuple-element.12), channel_id=1, source_target_pairs={{0,16},{16,0},{1,17},{17,1},{2,18},{18,2},{3,19},{19,3},{4,20},{20... | collective-permute-start | bytes 786440 | tf_op jit(solution)/shard_map/ppermute | solution.py:264
  32.9 0.0 collective-permute-done.2.inner_ref
  32.9 1.5 %collective-permute-done.3.outer_ref = f32[32,16,128]{2,1,0:T(8,128)S(1)} collective-permute-done((f32[32,16,128]{2,1,0:T(8,128)S(1)}, f32[32,16,128]{2,1,0:T(8,128)S(1)}, u32[]{:S(2)}, u32[]{:S(2)}) %collective-permute-start.3) | collective-permute-done | bytes 262176 | tf_op jit(solution)/shard_map/ppermute | solution.py:261
  34.5 1.7 %transport_kept.1 = f32[8,4,16,128]{3,2,1,0:T(8,128)S(1)} custom-call(s32[2]{0:T(128)S(1)} %pad_add_fusion.where_ref, f32[32,16,128]{2,1,0:T(8,128)S(1)} %get-tuple-element.13.own_ref, f32[32,16,128]{2,1,0:T(8,128)S(1)} %collective-permute-done.2.inner_ref, f32[32,16,128]{2,1,0:T(8,128)S(1)} %collective-permute-done.3.outer_ref, ...), custom_call_target="tpu_custom_call" | custom-call | tf_op jit(solution)/shard_map/transport_kept/pallas_call | solution.py:168
  36.1 0.0 copy-start.3
  36.2 0.0 copy-start.4
  36.2 0.0 copy-start
  36.2 0.0 copy-start.1
  36.2 0.0 copy-start.2
  36.2 0.0 collective-permute-done.4
  36.3 20.4 %all_to_all.10 = f32[16,2,16,128]{3,2,1,0:T(8,128)S(1)} all-to-all(f32[16,2,16,128]{3,2,1,0:T(8,128)S(1)} %bitcast.22), channel_id=1, replica_groups=mesh['field_0'=4,'field_1'=4,'field_2'=2,'slab'=16] {'field_0','field_1'}, dimensions={0} | all-to-all | bytes 524288 | tf_op jit(solution)/shard_map/all_to_all | solution.py:268
  56.7 13.3 %all_to_all.11 = f32[16,2,16,128]{3,2,1,0:T(8,128)S(1)} all-to-all(f32[16,2,16,128]{3,2,1,0:T(8,128)S(1)} %broadcast_in_dim.2), channel_id=1, replica_groups=mesh['field_0'=4,'field_1'=4,'field_2'=2,'slab'=16] {'field_0','field_1'}, dimensions={0} | all-to-all | bytes 524288 | tf_op jit(solution)/shard_map/all_to_all | solution.py:271
  70.0 4.4 %collective-permute-start.5 = (f32[16,2,16,128]{3,2,1,0:T(8,128)S(1)}, f32[16,2,16,128]{3,2,1,0:T(8,128)S(1)}, u32[]{:S(2)}, u32[]{:S(2)}) collective-permute-start(f32[16,2,16,128]{3,2,1,0:T(8,128)S(1)} %all_to_all.11), channel_id=1, source_target_pairs={{0,16},{16,0},{1,17},{17,1},{2,18},{18,2},{3,19},{19,3},{4,20},{20... | collective-permute-start | bytes 786440 | tf_op jit(solution)/shard_map/ppermute | solution.py:272
  74.4 0.0 copy-done.3
  74.4 0.1 copy.13
  74.5 0.0 copy-done.4
  74.5 0.1 multiply_bitcast_fusion.stoich_ref
  74.6 1.0 %collective-permute-done.5 = f32[16,2,16,128]{3,2,1,0:T(8,128)S(1)} collective-permute-done((f32[16,2,16,128]{3,2,1,0:T(8,128)S(1)}, f32[16,2,16,128]{3,2,1,0:T(8,128)S(1)}, u32[]{:S(2)}, u32[]{:S(2)}) %collective-permute-start.5) | collective-permute-done | bytes 262176 | tf_op jit(solution)/shard_map/ppermute | solution.py:272
  75.6 0.0 copy-done
  75.6 0.0 copy-done.1
  75.6 0.0 copy-done.2
  75.6 2.2 %react.1 = f32[1024,128]{1,0:T(8,128)} custom-call(s32[2]{0:T(128)S(1)} %pad_add_fusion.where_ref, f32[512,128]{1,0:T(8,128)S(1)} %bitcast.16, f32[512,128]{1,0:T(8,128)S(1)} %bitcast.14, f32[512,128]{1,0:T(8,128)S(1)} %bitcast.15, f32[512,128]{1,0:T(8,128)S(1)} %bitcast.17, f32[64,128]{1,0:T(8,128)S(1)} %bitcast.18, f32[64,128]{1,0:T(8,128)S(1)} %bitcast.19, ...), custom_call_target="tpu_custom_call" | custom-call | tf_op jit(solution)/shard_map/react/pallas_call | solution.py:235
  (4 shorter events, 0.1 us)
Async XLA Ops:
  2.0 21.0 %collective-permute-start = (f32[44,16,128]{2,1,0:T(8,128)S(1)}, f32[44,16,128]{2,1,0:T(8,128)S(1)}, u32[]{:S(2)}, u32[]{:S(2)}) collective-permute-start(f32[44,16,128]{2,1,0:T(8,128)S(1)} %get-tuple-element.10.own_outer_ref), channel_id=1, source_target_pairs={{1,2},{2,1},{3,4},{4,3},{5,6},{6,5},{7,8},{8,7},{9,10},{10,9},{11,... | collective-permute-start | bytes 1081352 | tf_op jit(solution)/shard_map/ppermute | solution.py:258
  15.0 10.9 %collective-permute-start.1 = (f32[44,16,128]{2,1,0:T(8,128)S(1)}, f32[44,16,128]{2,1,0:T(8,128)S(1)}, u32[]{:S(2)}, u32[]{:S(2)}) collective-permute-start(f32[44,16,128]{2,1,0:T(8,128)S(1)} %get-tuple-element.11.own_inner_ref), channel_id=1, source_target_pairs={{0,1},{1,0},{2,3},{3,2},{4,5},{5,4},{6,7},{7,6},{8,9},{9,8},{10,11... | collective-permute-start | bytes 1081352 | tf_op jit(solution)/shard_map/ppermute | solution.py:259
  16.9 16.0 %collective-permute-start.2 = (f32[32,16,128]{2,1,0:T(8,128)S(1)}, f32[32,16,128]{2,1,0:T(8,128)S(1)}, u32[]{:S(2)}, u32[]{:S(2)}) collective-permute-start(f32[32,16,128]{2,1,0:T(8,128)S(1)} %get-tuple-element.13.own_ref), channel_id=1, source_target_pairs={{0,1},{1,0},{2,3},{3,2},{4,5},{5,4},{6,7},{7,6},{8,9},{9,8},{10,11... | collective-permute-start | bytes 786440 | tf_op jit(solution)/shard_map/ppermute | solution.py:260
  20.3 14.2 %collective-permute-start.3 = (f32[32,16,128]{2,1,0:T(8,128)S(1)}, f32[32,16,128]{2,1,0:T(8,128)S(1)}, u32[]{:S(2)}, u32[]{:S(2)}) collective-permute-start(f32[32,16,128]{2,1,0:T(8,128)S(1)} %get-tuple-element.13.own_ref), channel_id=1, source_target_pairs={{1,2},{2,1},{3,4},{4,3},{5,6},{6,5},{7,8},{8,7},{9,10},{10,9},{11,... | collective-permute-start | bytes 786440 | tf_op jit(solution)/shard_map/ppermute | solution.py:261
  27.7 8.5 %collective-permute-start.4 = (f32[8,4,16,128]{3,2,1,0:T(8,128)S(1)}, f32[8,4,16,128]{3,2,1,0:T(8,128)S(1)}, u32[]{:S(2)}, u32[]{:S(2)}) collective-permute-start(f32[8,4,16,128]{3,2,1,0:T(8,128)S(1)} %get-tuple-element.12), channel_id=1, source_target_pairs={{0,16},{16,0},{1,17},{17,1},{2,18},{18,2},{3,19},{19,3},{4,20},{20... | collective-permute-start | bytes 786440 | tf_op jit(solution)/shard_map/ppermute | solution.py:264
  36.1 38.3 %copy-start.3 = (f32[16,32]{1,0:T(8,128)S(1)}, f32[16,32]{1,0:T(8,128)}, u32[]{:S(2)}) copy-start(f32[16,32]{1,0:T(8,128)} %param.16) | copy-start | bytes 6148
  36.2 38.4 %copy-start.4 = (f32[32]{0:T(128)S(1)}, f32[32]{0:T(128)}, u32[]{:S(2)}) copy-start(f32[32]{0:T(128)} %param.17) | copy-start | bytes 388
  36.2 39.4 %copy-start = (f32[4,16,128]{2,1,0:T(8,128)S(1)}, f32[4,16,128]{2,1,0:T(8,128)}, u32[]{:S(2)}) copy-start(f32[4,16,128]{2,1,0:T(8,128)} %param.13) | copy-start | bytes 98308
  36.2 39.4 %copy-start.1 = (f32[4,16,128]{2,1,0:T(8,128)S(1)}, f32[4,16,128]{2,1,0:T(8,128)}, u32[]{:S(2)}) copy-start(f32[4,16,128]{2,1,0:T(8,128)} %param.14) | copy-start | bytes 98308
  36.2 39.4 %copy-start.2 = (f32[32,16]{0,1:T(8,128)S(1)}, f32[32,16]{0,1:T(8,128)}, u32[]{:S(2)}) copy-start(f32[32,16]{0,1:T(8,128)} %param.15) | copy-start | bytes 6148
  70.0 5.5 %collective-permute-start.5 = (f32[16,2,16,128]{3,2,1,0:T(8,128)S(1)}, f32[16,2,16,128]{3,2,1,0:T(8,128)S(1)}, u32[]{:S(2)}, u32[]{:S(2)}) collective-permute-start(f32[16,2,16,128]{3,2,1,0:T(8,128)S(1)} %all_to_all.11), channel_id=1, source_target_pairs={{0,16},{16,0},{1,17},{17,1},{2,18},{18,2},{3,19},{19,3},{4,20},{20... | collective-permute-start | bytes 786440 | tf_op jit(solution)/shard_map/ppermute | solution.py:272

commit v12 on v11

--- a/solution.py
+++ b/solution.py
@@ -195,27 +195,33 @@
 TILE = 8
 
 
-def react_kernel(
-    where_ref, sent_ref, kept_ref, mine_ref, other_ref, rate_ref, vapour_ref, rate_matrix_ref, stoich_ref, out_ref
-):
+def by_row(ref, row):
+    return jnp.swapaxes(jnp.stack([ref[pl.ds(s * X * NZ + row, TILE), :] for s in range(HALF)]), 0, 1)
+
+
+def mix_kernel(sent_ref, kept_ref, mine_ref, rate_ref, rows_ref, mixed_ref):
+    for row in range(0, X * NZ, TILE):
+        rows_ref[pl.ds(row, TILE)] = by_row(sent_ref, row)
+        kept, mine = by_row(kept_ref, row), by_row(mine_ref, row)
+        rate = 0.5 * rate_ref[pl.ds(row, TILE), :]
+        mixed_ref[pl.ds(row, TILE)] = kept - rate[:, None] * (kept - mine)
+
+
+def react_kernel(where_ref, sent_ref, kept_ref, other_ref, rate_ref, vapour_ref, rate_matrix_ref, stoich_ref, out_ref):
     cells = X * NZ
     drive_weights = halves(rate_matrix_ref[...])
     source_weights = halves(stoich_ref[...])
     first = where_ref[0] == 0
     fuel = lax.broadcasted_iota(jnp.int32, (S, NY), 0) == 0
 
-    def by_row(ref, row):
-        return jnp.swapaxes(jnp.stack([ref[pl.ds(s * cells + row, TILE), :] for s in range(HALF)]), 0, 1)
-
     for block in range(0, cells, ROWS):
         mixed = []
         for row in range(block, block + ROWS, TILE):
-            tiles = [by_row(ref, row) for ref in (sent_ref, kept_ref, mine_ref, other_ref)]
+            others = by_row(other_ref, row)
             for j in range(TILE):
-                sent, kept, mine, other = (tile[j] for tile in tiles)
+                sent, kept, other = sent_ref[row + j], kept_ref[row + j], others[j]
                 rate = 0.5 * rate_ref[pl.ds(row + j, 1), :]
                 vapour = vapour_ref[pl.ds(row + j, 1), :]
-                kept = kept - rate * (kept - mine)
                 sent = sent - rate * (sent - other)
                 both = jnp.concatenate([jnp.where(first, kept, sent), jnp.where(first, sent, kept)], 0)
                 mixed.append(both + jnp.where(fuel, vapour, 0.0))
@@ -230,19 +236,32 @@
                     out_ref[pl.ds((half + s) * cells + block + row, TILE), :] = tile[s]
 
 
-def react(where, sent, kept, mine, other, rates, vapour, rate_matrix, stoich, prefactor):
+def react(where, sent, kept, mine, swap, rates, vapour, rate_matrix, stoich, prefactor):
     rows = X * NZ
+    rates = rates.reshape(rows, NY)
+    by_rows = jax.ShapeDtypeStruct((rows, HALF, NY), jnp.float32)
+    other = swap(mine)
+    sent, mixed = pl.pallas_call(
+        mix_kernel,
+        out_shape=(by_rows, by_rows),
+        in_specs=[VMEM] * 4,
+        out_specs=(VMEM, VMEM),
+        compiler_params=LIMIT,
+        name="mix",
+    )(*(x.reshape(HALF * rows, NY) for x in (sent, kept, mine)), rates)
     return pl.pallas_call(
         react_kernel,
         out_shape=jax.ShapeDtypeStruct((S * rows, NY), jnp.float32),
-        in_specs=[SMEM] + [VMEM] * 8,
+        in_specs=[SMEM] + [VMEM] * 7,
         out_specs=VMEM,
         compiler_params=LIMIT,
         name="react",
     )(
         where,
-        *(x.reshape(HALF * rows, NY) for x in (sent, kept, mine, other)),
-        rates.reshape(rows, NY),
+        sent,
+        mixed,
+        other.reshape(HALF * rows, NY),
+        rates,
         vapour.reshape(rows, NY),
         rate_matrix.T,
         (stoich * prefactor[None]).T,
@@ -269,7 +288,7 @@
     average = jnp.sum(parts, 0) / F
     spread = jnp.broadcast_to(average[None], pair.shape)
     mine = lax.all_to_all(spread, CHIPS, 0, 0, tiled=True)
-    updated = react(where, sent, kept, mine, swap(mine), mix_rate, evaporation, rate_matrix, stoich, prefactor)
+    updated = react(where, sent, kept, mine, swap, mix_rate, evaporation, rate_matrix, stoich, prefactor)
     return updated.reshape(fields.shape)
 
 

time: 78.7 us -> 78.6 us (level)
  no operation moved by 1% of the time
where the time goes in v12:
time: 78.6 us; the launch traced here: 77.7 us
  blocking collectives  33.7 us (43%)
  starting transfers between devices  29.7 us (38%)
  Pallas kernels  7.79 us (10%)
  waiting for transfers between devices  5.18 us (7%)
  local copies, waits for them, and re-layouts  0.89 us (1%)
    all_to_all x1, blocking collectives, per_device(): parts = lax.all_to_all(pair, CHIPS, 0, 0, tiled=True)  20.4 us
    all_to_all x1, blocking collectives, per_device(): mine = lax.all_to_all(spread, CHIPS, 0, 0, tiled=True)  13.3 us
    ppermute x1, starting transfers between devices, per_device(): from_outer = lax.ppermute(to_outer, 'slab', outer)  12.9 us
    ppermute x1, starting transfers between devices, per_device(): other = swap(sent)  5.24 us
    ppermute x1, starting transfers between devices, react(): other = swap(mine)  4.37 us
    ppermute x1, starting transfers between devices, per_device(): keep_inner = lax.ppermute(keep, 'slab', inner)  3.36 us
    ppermute x1, waiting for transfers between devices, per_device(): from_inner = lax.ppermute(to_inner, 'slab', inner)  2.73 us
    pallas_call x1, Pallas kernels, react(): pl.pallas_call(react_kernel, out_shape=jax.ShapeDtypeStruct((S * rows, NY...  2.11 us
  transfers between devices with their start and end apart: 6, of which 4 were waited for; matrix products, arithmetic and copies ran while one was open for 1% of the time, Pallas kernels for 5%

profile of v12, /device:TPU:57, one launch (start us, length us, event | category | flops | bytes accessed | tf_op | source)
XLA Modules:
  0.0 77.7 jit_solution(12963692914415605523)
XLA Ops:
  0.0 0.1 pad_add_fusion.where_ref
  0.1 2.0 %pack.1 = (f32[44,16,128]{2,1,0:T(8,128)S(1)}, f32[44,16,128]{2,1,0:T(8,128)S(1)}, f32[32,16,128]{2,1,0:T(8,128)S(1)}) custom-call(s32[2]{0:T(128)S(1)} %pad_add_fusion.where_ref, f32[1,16,4,16,128]{4,3,2,1,0:T(8,128)} %fields_ref.1, f32[3,4,16,128]{3,2,1,0:T(8,128)} %velocity_ref.1, f32[4,16,128]{2,1,0:T(8,128)} %diffusivity_ref.1), custom_call_target="tpu_custom_call" | custom-call | tf_op jit(solution)/shard_map/pack/pallas_call | solution.py:64
  2.0 12.9 %collective-permute-start = (f32[44,16,128]{2,1,0:T(8,128)S(1)}, f32[44,16,128]{2,1,0:T(8,128)S(1)}, u32[]{:S(2)}, u32[]{:S(2)}) collective-permute-start(f32[44,16,128]{2,1,0:T(8,128)S(1)} %get-tuple-element.12.own_outer_ref), channel_id=1, source_target_pairs={{1,2},{2,1},{3,4},{4,3},{5,6},{6,5},{7,8},{8,7},{9,10},{10,9},{11,... | collective-permute-start | bytes 1081352 | tf_op jit(solution)/shard_map/ppermute | solution.py:277
  15.0 1.9 %collective-permute-start.1 = (f32[44,16,128]{2,1,0:T(8,128)S(1)}, f32[44,16,128]{2,1,0:T(8,128)S(1)}, u32[]{:S(2)}, u32[]{:S(2)}) collective-permute-start(f32[44,16,128]{2,1,0:T(8,128)S(1)} %get-tuple-element.13.own_inner_ref), channel_id=1, source_target_pairs={{0,1},{1,0},{2,3},{3,2},{4,5},{5,4},{6,7},{7,6},{8,9},{9,8},{10,11... | collective-permute-start | bytes 1081352 | tf_op jit(solution)/shard_map/ppermute | solution.py:278
  16.9 3.4 %collective-permute-start.2 = (f32[32,16,128]{2,1,0:T(8,128)S(1)}, f32[32,16,128]{2,1,0:T(8,128)S(1)}, u32[]{:S(2)}, u32[]{:S(2)}) collective-permute-start(f32[32,16,128]{2,1,0:T(8,128)S(1)} %get-tuple-element.15.own_ref), channel_id=1, source_target_pairs={{0,1},{1,0},{2,3},{3,2},{4,5},{5,4},{6,7},{7,6},{8,9},{9,8},{10,11... | collective-permute-start | bytes 786440 | tf_op jit(solution)/shard_map/ppermute | solution.py:279
  20.3 1.9 %collective-permute-start.3 = (f32[32,16,128]{2,1,0:T(8,128)S(1)}, f32[32,16,128]{2,1,0:T(8,128)S(1)}, u32[]{:S(2)}, u32[]{:S(2)}) collective-permute-start(f32[32,16,128]{2,1,0:T(8,128)S(1)} %get-tuple-element.15.own_ref), channel_id=1, source_target_pairs={{1,2},{2,1},{3,4},{4,3},{5,6},{6,5},{7,8},{8,7},{9,10},{10,9},{11,... | collective-permute-start | bytes 786440 | tf_op jit(solution)/shard_map/ppermute | solution.py:280
  22.2 0.8 copy.12
  23.0 0.1 collective-permute-done.outer_ref
  23.1 2.7 %collective-permute-done.1.inner_ref = f32[44,16,128]{2,1,0:T(8,128)S(1)} collective-permute-done((f32[44,16,128]{2,1,0:T(8,128)S(1)}, f32[44,16,128]{2,1,0:T(8,128)S(1)}, u32[]{:S(2)}, u32[]{:S(2)}) %collective-permute-start.1) | collective-permute-done | bytes 360480 | tf_op jit(solution)/shard_map/ppermute | solution.py:278
  25.8 1.8 %transport_sent.1 = (f32[8,4,16,128]{3,2,1,0:T(8,128)S(1)}, f32[28,7,16,128]{3,2,1,0:T(8,128)S(1)}) custom-call(s32[2]{0:T(128)S(1)} %pad_add_fusion.where_ref, f32[4,3]{1,0:T(4,128)S(1)} %bitcast.22, f32[44,16,128]{2,1,0:T(8,128)S(1)} %get-tuple-element.12.own_outer_ref, f32[44,16,128]{2,1,0:T(8,128)S(1)} %get-tuple-element.13.own_inner_ref, ...), custom_call_target="tpu_custom_call" | custom-call | tf_op jit(solution)/shard_map/transport_sent/pallas_call | solution.py:150
  27.7 5.2 %collective-permute-start.4 = (f32[8,4,16,128]{3,2,1,0:T(8,128)S(1)}, f32[8,4,16,128]{3,2,1,0:T(8,128)S(1)}, u32[]{:S(2)}, u32[]{:S(2)}) collective-permute-start(f32[8,4,16,128]{3,2,1,0:T(8,128)S(1)} %get-tuple-element.14), channel_id=1, source_target_pairs={{0,16},{16,0},{1,17},{17,1},{2,18},{18,2},{3,19},{19,3},{4,20},{20... | collective-permute-start | bytes 786440 | tf_op jit(solution)/shard_map/ppermute | solution.py:283
  32.9 0.0 collective-permute-done.2.inner_ref
  32.9 1.5 %collective-permute-done.3.outer_ref = f32[32,16,128]{2,1,0:T(8,128)S(1)} collective-permute-done((f32[32,16,128]{2,1,0:T(8,128)S(1)}, f32[32,16,128]{2,1,0:T(8,128)S(1)}, u32[]{:S(2)}, u32[]{:S(2)}) %collective-permute-start.3) | collective-permute-done | bytes 262176 | tf_op jit(solution)/shard_map/ppermute | solution.py:280
  34.5 1.7 %transport_kept.1 = f32[8,4,16,128]{3,2,1,0:T(8,128)S(1)} custom-call(s32[2]{0:T(128)S(1)} %pad_add_fusion.where_ref, f32[32,16,128]{2,1,0:T(8,128)S(1)} %get-tuple-element.15.own_ref, f32[32,16,128]{2,1,0:T(8,128)S(1)} %collective-permute-done.2.inner_ref, f32[32,16,128]{2,1,0:T(8,128)S(1)} %collective-permute-done.3.outer_ref, ...), custom_call_target="tpu_custom_call" | custom-call | tf_op jit(solution)/shard_map/transport_kept/pallas_call | solution.py:168
  36.1 0.0 copy-start.3
  36.2 0.0 copy-start.4
  36.2 0.0 copy-start
  36.2 0.0 copy-start.1
  36.2 0.0 copy-start.2
  36.2 0.0 collective-permute-done.4
  36.3 20.4 %all_to_all.10 = f32[16,2,16,128]{3,2,1,0:T(8,128)S(1)} all-to-all(f32[16,2,16,128]{3,2,1,0:T(8,128)S(1)} %bitcast.23), channel_id=1, replica_groups=mesh['field_0'=4,'field_1'=4,'field_2'=2,'slab'=16] {'field_0','field_1'}, dimensions={0} | all-to-all | bytes 524288 | tf_op jit(solution)/shard_map/all_to_all | solution.py:287
  56.7 13.3 %all_to_all.11 = f32[16,2,16,128]{3,2,1,0:T(8,128)S(1)} all-to-all(f32[16,2,16,128]{3,2,1,0:T(8,128)S(1)} %broadcast_in_dim.2), channel_id=1, replica_groups=mesh['field_0'=4,'field_1'=4,'field_2'=2,'slab'=16] {'field_0','field_1'}, dimensions={0} | all-to-all | bytes 524288 | tf_op jit(solution)/shard_map/all_to_all | solution.py:290
  70.0 4.4 %collective-permute-start.5 = (f32[16,2,16,128]{3,2,1,0:T(8,128)S(1)}, f32[16,2,16,128]{3,2,1,0:T(8,128)S(1)}, u32[]{:S(2)}, u32[]{:S(2)}) collective-permute-start(f32[16,2,16,128]{3,2,1,0:T(8,128)S(1)} %all_to_all.11), channel_id=1, source_target_pairs={{0,16},{16,0},{1,17},{17,1},{2,18},{18,2},{3,19},{19,3},{4,20},{20... | collective-permute-start | bytes 786440 | tf_op jit(solution)/shard_map/ppermute | solution.py:243
  74.4 0.0 copy-done.3
  74.4 0.1 copy.13
  74.5 0.0 copy-done.4
  74.5 0.1 multiply_bitcast_fusion.stoich_ref
  74.6 0.0 copy-done
  74.6 0.2 mix.1
  74.8 0.8 %collective-permute-done.5 = f32[16,2,16,128]{3,2,1,0:T(8,128)S(1)} collective-permute-done((f32[16,2,16,128]{3,2,1,0:T(8,128)S(1)}, f32[16,2,16,128]{3,2,1,0:T(8,128)S(1)}, u32[]{:S(2)}, u32[]{:S(2)}) %collective-permute-start.5) | collective-permute-done | bytes 262176 | tf_op jit(solution)/shard_map/ppermute | solution.py:243
  75.6 0.0 copy-done.1
  75.6 0.0 copy-done.2
  75.6 2.1 %react.1 = f32[1024,128]{1,0:T(8,128)} custom-call(s32[2]{0:T(128)S(1)} %pad_add_fusion.where_ref, f32[64,8,128]{2,1,0:T(8,128)S(1)} %get-tuple-element.17.sent_ref, f32[64,8,128]{2,1,0:T(8,128)S(1)} %get-tuple-element.18.kept_ref, f32[512,128]{1,0:T(8,128)S(1)} %bitcast.17, f32[64,128]{1,0:T(8,128)S(1)} %bitcast.19, f32[64,128]{1,0:T(8,128)S(1)} %bitcast.20, ...), custom_call_target="tpu_custom_call" | custom-call | tf_op jit(solution)/shard_map/react/pallas_call | solution.py:252
  (4 shorter events, 0.1 us)
Async XLA Ops:
  2.0 21.0 %collective-permute-start = (f32[44,16,128]{2,1,0:T(8,128)S(1)}, f32[44,16,128]{2,1,0:T(8,128)S(1)}, u32[]{:S(2)}, u32[]{:S(2)}) collective-permute-start(f32[44,16,128]{2,1,0:T(8,128)S(1)} %get-tuple-element.12.own_outer_ref), channel_id=1, source_target_pairs={{1,2},{2,1},{3,4},{4,3},{5,6},{6,5},{7,8},{8,7},{9,10},{10,9},{11,... | collective-permute-start | bytes 1081352 | tf_op jit(solution)/shard_map/ppermute | solution.py:277
  15.0 10.9 %collective-permute-start.1 = (f32[44,16,128]{2,1,0:T(8,128)S(1)}, f32[44,16,128]{2,1,0:T(8,128)S(1)}, u32[]{:S(2)}, u32[]{:S(2)}) collective-permute-start(f32[44,16,128]{2,1,0:T(8,128)S(1)} %get-tuple-element.13.own_inner_ref), channel_id=1, source_target_pairs={{0,1},{1,0},{2,3},{3,2},{4,5},{5,4},{6,7},{7,6},{8,9},{9,8},{10,11... | collective-permute-start | bytes 1081352 | tf_op jit(solution)/shard_map/ppermute | solution.py:278
  16.9 16.0 %collective-permute-start.2 = (f32[32,16,128]{2,1,0:T(8,128)S(1)}, f32[32,16,128]{2,1,0:T(8,128)S(1)}, u32[]{:S(2)}, u32[]{:S(2)}) collective-permute-start(f32[32,16,128]{2,1,0:T(8,128)S(1)} %get-tuple-element.15.own_ref), channel_id=1, source_target_pairs={{0,1},{1,0},{2,3},{3,2},{4,5},{5,4},{6,7},{7,6},{8,9},{9,8},{10,11... | collective-permute-start | bytes 786440 | tf_op jit(solution)/shard_map/ppermute | solution.py:279
  20.3 14.2 %collective-permute-start.3 = (f32[32,16,128]{2,1,0:T(8,128)S(1)}, f32[32,16,128]{2,1,0:T(8,128)S(1)}, u32[]{:S(2)}, u32[]{:S(2)}) collective-permute-start(f32[32,16,128]{2,1,0:T(8,128)S(1)} %get-tuple-element.15.own_ref), channel_id=1, source_target_pairs={{1,2},{2,1},{3,4},{4,3},{5,6},{6,5},{7,8},{8,7},{9,10},{10,9},{11,... | collective-permute-start | bytes 786440 | tf_op jit(solution)/shard_map/ppermute | solution.py:280
  27.7 8.5 %collective-permute-start.4 = (f32[8,4,16,128]{3,2,1,0:T(8,128)S(1)}, f32[8,4,16,128]{3,2,1,0:T(8,128)S(1)}, u32[]{:S(2)}, u32[]{:S(2)}) collective-permute-start(f32[8,4,16,128]{3,2,1,0:T(8,128)S(1)} %get-tuple-element.14), channel_id=1, source_target_pairs={{0,16},{16,0},{1,17},{17,1},{2,18},{18,2},{3,19},{19,3},{4,20},{20... | collective-permute-start | bytes 786440 | tf_op jit(solution)/shard_map/ppermute | solution.py:283
  36.1 38.3 %copy-start.3 = (f32[16,32]{1,0:T(8,128)S(1)}, f32[16,32]{1,0:T(8,128)}, u32[]{:S(2)}) copy-start(f32[16,32]{1,0:T(8,128)} %param.16) | copy-start | bytes 6148
  36.2 38.4 %copy-start.4 = (f32[32]{0:T(128)S(1)}, f32[32]{0:T(128)}, u32[]{:S(2)}) copy-start(f32[32]{0:T(128)} %param.17) | copy-start | bytes 388
  36.2 38.4 %copy-start = (f32[4,16,128]{2,1,0:T(8,128)S(1)}, f32[4,16,128]{2,1,0:T(8,128)}, u32[]{:S(2)}) copy-start(f32[4,16,128]{2,1,0:T(8,128)} %param.13) | copy-start | bytes 98308
  36.2 39.4 %copy-start.1 = (f32[4,16,128]{2,1,0:T(8,128)S(1)}, f32[4,16,128]{2,1,0:T(8,128)}, u32[]{:S(2)}) copy-start(f32[4,16,128]{2,1,0:T(8,128)} %param.14) | copy-start | bytes 98308
  36.2 39.4 %copy-start.2 = (f32[32,16]{0,1:T(8,128)S(1)}, f32[32,16]{0,1:T(8,128)}, u32[]{:S(2)}) copy-start(f32[32,16]{0,1:T(8,128)} %param.15) | copy-start | bytes 6148
  70.0 5.5 %collective-permute-start.5 = (f32[16,2,16,128]{3,2,1,0:T(8,128)S(1)}, f32[16,2,16,128]{3,2,1,0:T(8,128)S(1)}, u32[]{:S(2)}, u32[]{:S(2)}) collective-permute-start(f32[16,2,16,128]{3,2,1,0:T(8,128)S(1)} %all_to_all.11), channel_id=1, source_target_pairs={{0,16},{16,0},{1,17},{17,1},{2,18},{18,2},{3,19},{19,3},{4,20},{20... | collective-permute-start | bytes 786440 | tf_op jit(solution)/shard_map/ppermute | solution.py:243

commit v13 on v12

--- a/solution.py
+++ b/solution.py
@@ -191,7 +191,7 @@
     )
 
 
-ROWS = 32
+ROWS = 64
 TILE = 8
 
 

time: 78.6 us -> 78.5 us (level)
  no operation moved by 1% of the time
where the time goes in v13:
time: 78.5 us; the launch traced here: 77.6 us
  blocking collectives  33.7 us (43%)
  starting transfers between devices  29.7 us (38%)
  Pallas kernels  7.66 us (10%)
  waiting for transfers between devices  5.18 us (7%)
  local copies, waits for them, and re-layouts  0.89 us (1%)
    all_to_all x1, blocking collectives, per_device(): parts = lax.all_to_all(pair, CHIPS, 0, 0, tiled=True)  20.4 us
    all_to_all x1, blocking collectives, per_device(): mine = lax.all_to_all(spread, CHIPS, 0, 0, tiled=True)  13.3 us
    ppermute x1, starting transfers between devices, per_device(): from_outer = lax.ppermute(to_outer, 'slab', outer)  12.9 us
    ppermute x1, starting transfers between devices, per_device(): other = swap(sent)  5.24 us
    ppermute x1, starting transfers between devices, react(): other = swap(mine)  4.37 us
    ppermute x1, starting transfers between devices, per_device(): keep_inner = lax.ppermute(keep, 'slab', inner)  3.36 us
    ppermute x1, waiting for transfers between devices, per_device(): from_inner = lax.ppermute(to_inner, 'slab', inner)  2.73 us
    pallas_call x1, Pallas kernels, react(): pl.pallas_call(react_kernel, out_shape=jax.ShapeDtypeStruct((S * rows, NY...  1.99 us
  transfers between devices with their start and end apart: 6, of which 4 were waited for; matrix products, arithmetic and copies ran while one was open for 1% of the time, Pallas kernels for 5%

profile of v13, /device:TPU:57, one launch (start us, length us, event | category | flops | bytes accessed | tf_op | source)
XLA Modules:
  0.0 77.6 jit_solution(6278164753280542667)
XLA Ops:
  0.0 0.1 pad_add_fusion.where_ref
  0.1 2.0 %pack.1 = (f32[44,16,128]{2,1,0:T(8,128)S(1)}, f32[44,16,128]{2,1,0:T(8,128)S(1)}, f32[32,16,128]{2,1,0:T(8,128)S(1)}) custom-call(s32[2]{0:T(128)S(1)} %pad_add_fusion.where_ref, f32[1,16,4,16,128]{4,3,2,1,0:T(8,128)} %fields_ref.1, f32[3,4,16,128]{3,2,1,0:T(8,128)} %velocity_ref.1, f32[4,16,128]{2,1,0:T(8,128)} %diffusivity_ref.1), custom_call_target="tpu_custom_call" | custom-call | tf_op jit(solution)/shard_map/pack/pallas_call | solution.py:64
  2.0 12.9 %collective-permute-start = (f32[44,16,128]{2,1,0:T(8,128)S(1)}, f32[44,16,128]{2,1,0:T(8,128)S(1)}, u32[]{:S(2)}, u32[]{:S(2)}) collective-permute-start(f32[44,16,128]{2,1,0:T(8,128)S(1)} %get-tuple-element.12.own_outer_ref), channel_id=1, source_target_pairs={{1,2},{2,1},{3,4},{4,3},{5,6},{6,5},{7,8},{8,7},{9,10},{10,9},{11,... | collective-permute-start | bytes 1081352 | tf_op jit(solution)/shard_map/ppermute | solution.py:277
  15.0 1.9 %collective-permute-start.1 = (f32[44,16,128]{2,1,0:T(8,128)S(1)}, f32[44,16,128]{2,1,0:T(8,128)S(1)}, u32[]{:S(2)}, u32[]{:S(2)}) collective-permute-start(f32[44,16,128]{2,1,0:T(8,128)S(1)} %get-tuple-element.13.own_inner_ref), channel_id=1, source_target_pairs={{0,1},{1,0},{2,3},{3,2},{4,5},{5,4},{6,7},{7,6},{8,9},{9,8},{10,11... | collective-permute-start | bytes 1081352 | tf_op jit(solution)/shard_map/ppermute | solution.py:278
  16.9 3.4 %collective-permute-start.2 = (f32[32,16,128]{2,1,0:T(8,128)S(1)}, f32[32,16,128]{2,1,0:T(8,128)S(1)}, u32[]{:S(2)}, u32[]{:S(2)}) collective-permute-start(f32[32,16,128]{2,1,0:T(8,128)S(1)} %get-tuple-element.15.own_ref), channel_id=1, source_target_pairs={{0,1},{1,0},{2,3},{3,2},{4,5},{5,4},{6,7},{7,6},{8,9},{9,8},{10,11... | collective-permute-start | bytes 786440 | tf_op jit(solution)/shard_map/ppermute | solution.py:279
  20.3 1.9 %collective-permute-start.3 = (f32[32,16,128]{2,1,0:T(8,128)S(1)}, f32[32,16,128]{2,1,0:T(8,128)S(1)}, u32[]{:S(2)}, u32[]{:S(2)}) collective-permute-start(f32[32,16,128]{2,1,0:T(8,128)S(1)} %get-tuple-element.15.own_ref), channel_id=1, source_target_pairs={{1,2},{2,1},{3,4},{4,3},{5,6},{6,5},{7,8},{8,7},{9,10},{10,9},{11,... | collective-permute-start | bytes 786440 | tf_op jit(solution)/shard_map/ppermute | solution.py:280
  22.2 0.8 copy.12
  23.0 0.1 collective-permute-done.outer_ref
  23.1 2.7 %collective-permute-done.1.inner_ref = f32[44,16,128]{2,1,0:T(8,128)S(1)} collective-permute-done((f32[44,16,128]{2,1,0:T(8,128)S(1)}, f32[44,16,128]{2,1,0:T(8,128)S(1)}, u32[]{:S(2)}, u32[]{:S(2)}) %collective-permute-start.1) | collective-permute-done | bytes 360480 | tf_op jit(solution)/shard_map/ppermute | solution.py:278
  25.8 1.8 %transport_sent.1 = (f32[8,4,16,128]{3,2,1,0:T(8,128)S(1)}, f32[28,7,16,128]{3,2,1,0:T(8,128)S(1)}) custom-call(s32[2]{0:T(128)S(1)} %pad_add_fusion.where_ref, f32[4,3]{1,0:T(4,128)S(1)} %bitcast.22, f32[44,16,128]{2,1,0:T(8,128)S(1)} %get-tuple-element.12.own_outer_ref, f32[44,16,128]{2,1,0:T(8,128)S(1)} %get-tuple-element.13.own_inner_ref, ...), custom_call_target="tpu_custom_call" | custom-call | tf_op jit(solution)/shard_map/transport_sent/pallas_call | solution.py:150
  27.7 5.2 %collective-permute-start.4 = (f32[8,4,16,128]{3,2,1,0:T(8,128)S(1)}, f32[8,4,16,128]{3,2,1,0:T(8,128)S(1)}, u32[]{:S(2)}, u32[]{:S(2)}) collective-permute-start(f32[8,4,16,128]{3,2,1,0:T(8,128)S(1)} %get-tuple-element.14), channel_id=1, source_target_pairs={{0,16},{16,0},{1,17},{17,1},{2,18},{18,2},{3,19},{19,3},{4,20},{20... | collective-permute-start | bytes 786440 | tf_op jit(solution)/shard_map/ppermute | solution.py:283
  32.9 0.0 collective-permute-done.2.inner_ref
  32.9 1.5 %collective-permute-done.3.outer_ref = f32[32,16,128]{2,1,0:T(8,128)S(1)} collective-permute-done((f32[32,16,128]{2,1,0:T(8,128)S(1)}, f32[32,16,128]{2,1,0:T(8,128)S(1)}, u32[]{:S(2)}, u32[]{:S(2)}) %collective-permute-start.3) | collective-permute-done | bytes 262176 | tf_op jit(solution)/shard_map/ppermute | solution.py:280
  34.5 1.7 %transport_kept.1 = f32[8,4,16,128]{3,2,1,0:T(8,128)S(1)} custom-call(s32[2]{0:T(128)S(1)} %pad_add_fusion.where_ref, f32[32,16,128]{2,1,0:T(8,128)S(1)} %get-tuple-element.15.own_ref, f32[32,16,128]{2,1,0:T(8,128)S(1)} %collective-permute-done.2.inner_ref, f32[32,16,128]{2,1,0:T(8,128)S(1)} %collective-permute-done.3.outer_ref, ...), custom_call_target="tpu_custom_call" | custom-call | tf_op jit(solution)/shard_map/transport_kept/pallas_call | solution.py:168
  36.1 0.0 copy-start.3
  36.2 0.0 copy-start.4
  36.2 0.0 copy-start
  36.2 0.0 copy-start.1
  36.2 0.0 copy-start.2
  36.2 0.0 collective-permute-done.4
  36.3 20.4 %all_to_all.10 = f32[16,2,16,128]{3,2,1,0:T(8,128)S(1)} all-to-all(f32[16,2,16,128]{3,2,1,0:T(8,128)S(1)} %bitcast.23), channel_id=1, replica_groups=mesh['field_0'=4,'field_1'=4,'field_2'=2,'slab'=16] {'field_0','field_1'}, dimensions={0} | all-to-all | bytes 524288 | tf_op jit(solution)/shard_map/all_to_all | solution.py:287
  56.7 13.3 %all_to_all.11 = f32[16,2,16,128]{3,2,1,0:T(8,128)S(1)} all-to-all(f32[16,2,16,128]{3,2,1,0:T(8,128)S(1)} %broadcast_in_dim.2), channel_id=1, replica_groups=mesh['field_0'=4,'field_1'=4,'field_2'=2,'slab'=16] {'field_0','field_1'}, dimensions={0} | all-to-all | bytes 524288 | tf_op jit(solution)/shard_map/all_to_all | solution.py:290
  70.0 4.4 %collective-permute-start.5 = (f32[16,2,16,128]{3,2,1,0:T(8,128)S(1)}, f32[16,2,16,128]{3,2,1,0:T(8,128)S(1)}, u32[]{:S(2)}, u32[]{:S(2)}) collective-permute-start(f32[16,2,16,128]{3,2,1,0:T(8,128)S(1)} %all_to_all.11), channel_id=1, source_target_pairs={{0,16},{16,0},{1,17},{17,1},{2,18},{18,2},{3,19},{19,3},{4,20},{20... | collective-permute-start | bytes 786440 | tf_op jit(solution)/shard_map/ppermute | solution.py:243
  74.4 0.0 copy-done.3
  74.4 0.1 copy.13
  74.5 0.0 copy-done.4
  74.5 0.1 multiply_bitcast_fusion.stoich_ref
  74.6 0.0 copy-done
  74.6 0.2 mix.1
  74.8 0.8 %collective-permute-done.5 = f32[16,2,16,128]{3,2,1,0:T(8,128)S(1)} collective-permute-done((f32[16,2,16,128]{3,2,1,0:T(8,128)S(1)}, f32[16,2,16,128]{3,2,1,0:T(8,128)S(1)}, u32[]{:S(2)}, u32[]{:S(2)}) %collective-permute-start.5) | collective-permute-done | bytes 262176 | tf_op jit(solution)/shard_map/ppermute | solution.py:243
  75.6 0.0 copy-done.1
  75.6 0.0 copy-done.2
  75.6 2.0 %react.1 = f32[1024,128]{1,0:T(8,128)} custom-call(s32[2]{0:T(128)S(1)} %pad_add_fusion.where_ref, f32[64,8,128]{2,1,0:T(8,128)S(1)} %get-tuple-element.17.sent_ref, f32[64,8,128]{2,1,0:T(8,128)S(1)} %get-tuple-element.18.kept_ref, f32[512,128]{1,0:T(8,128)S(1)} %bitcast.17, f32[64,128]{1,0:T(8,128)S(1)} %bitcast.19, f32[64,128]{1,0:T(8,128)S(1)} %bitcast.20, ...), custom_call_target="tpu_custom_call" | custom-call | tf_op jit(solution)/shard_map/react/pallas_call | solution.py:252
  (4 shorter events, 0.1 us)
Async XLA Ops:
  2.0 21.0 %collective-permute-start = (f32[44,16,128]{2,1,0:T(8,128)S(1)}, f32[44,16,128]{2,1,0:T(8,128)S(1)}, u32[]{:S(2)}, u32[]{:S(2)}) collective-permute-start(f32[44,16,128]{2,1,0:T(8,128)S(1)} %get-tuple-element.12.own_outer_ref), channel_id=1, source_target_pairs={{1,2},{2,1},{3,4},{4,3},{5,6},{6,5},{7,8},{8,7},{9,10},{10,9},{11,... | collective-permute-start | bytes 1081352 | tf_op jit(solution)/shard_map/ppermute | solution.py:277
  15.0 10.9 %collective-permute-start.1 = (f32[44,16,128]{2,1,0:T(8,128)S(1)}, f32[44,16,128]{2,1,0:T(8,128)S(1)}, u32[]{:S(2)}, u32[]{:S(2)}) collective-permute-start(f32[44,16,128]{2,1,0:T(8,128)S(1)} %get-tuple-element.13.own_inner_ref), channel_id=1, source_target_pairs={{0,1},{1,0},{2,3},{3,2},{4,5},{5,4},{6,7},{7,6},{8,9},{9,8},{10,11... | collective-permute-start | bytes 1081352 | tf_op jit(solution)/shard_map/ppermute | solution.py:278
  16.9 16.0 %collective-permute-start.2 = (f32[32,16,128]{2,1,0:T(8,128)S(1)}, f32[32,16,128]{2,1,0:T(8,128)S(1)}, u32[]{:S(2)}, u32[]{:S(2)}) collective-permute-start(f32[32,16,128]{2,1,0:T(8,128)S(1)} %get-tuple-element.15.own_ref), channel_id=1, source_target_pairs={{0,1},{1,0},{2,3},{3,2},{4,5},{5,4},{6,7},{7,6},{8,9},{9,8},{10,11... | collective-permute-start | bytes 786440 | tf_op jit(solution)/shard_map/ppermute | solution.py:279
  20.3 14.2 %collective-permute-start.3 = (f32[32,16,128]{2,1,0:T(8,128)S(1)}, f32[32,16,128]{2,1,0:T(8,128)S(1)}, u32[]{:S(2)}, u32[]{:S(2)}) collective-permute-start(f32[32,16,128]{2,1,0:T(8,128)S(1)} %get-tuple-element.15.own_ref), channel_id=1, source_target_pairs={{1,2},{2,1},{3,4},{4,3},{5,6},{6,5},{7,8},{8,7},{9,10},{10,9},{11,... | collective-permute-start | bytes 786440 | tf_op jit(solution)/shard_map/ppermute | solution.py:280
  27.7 8.5 %collective-permute-start.4 = (f32[8,4,16,128]{3,2,1,0:T(8,128)S(1)}, f32[8,4,16,128]{3,2,1,0:T(8,128)S(1)}, u32[]{:S(2)}, u32[]{:S(2)}) collective-permute-start(f32[8,4,16,128]{3,2,1,0:T(8,128)S(1)} %get-tuple-element.14), channel_id=1, source_target_pairs={{0,16},{16,0},{1,17},{17,1},{2,18},{18,2},{3,19},{19,3},{4,20},{20... | collective-permute-start | bytes 786440 | tf_op jit(solution)/shard_map/ppermute | solution.py:283
  36.1 38.3 %copy-start.3 = (f32[16,32]{1,0:T(8,128)S(1)}, f32[16,32]{1,0:T(8,128)}, u32[]{:S(2)}) copy-start(f32[16,32]{1,0:T(8,128)} %param.16) | copy-start | bytes 6148
  36.2 38.4 %copy-start.4 = (f32[32]{0:T(128)S(1)}, f32[32]{0:T(128)}, u32[]{:S(2)}) copy-start(f32[32]{0:T(128)} %param.17) | copy-start | bytes 388
  36.2 38.4 %copy-start = (f32[4,16,128]{2,1,0:T(8,128)S(1)}, f32[4,16,128]{2,1,0:T(8,128)}, u32[]{:S(2)}) copy-start(f32[4,16,128]{2,1,0:T(8,128)} %param.13) | copy-start | bytes 98308
  36.2 39.4 %copy-start.1 = (f32[4,16,128]{2,1,0:T(8,128)S(1)}, f32[4,16,128]{2,1,0:T(8,128)}, u32[]{:S(2)}) copy-start(f32[4,16,128]{2,1,0:T(8,128)} %param.14) | copy-start | bytes 98308
  36.2 39.4 %copy-start.2 = (f32[32,16]{0,1:T(8,128)S(1)}, f32[32,16]{0,1:T(8,128)}, u32[]{:S(2)}) copy-start(f32[32,16]{0,1:T(8,128)} %param.15) | copy-start | bytes 6148
  70.0 5.5 %collective-permute-start.5 = (f32[16,2,16,128]{3,2,1,0:T(8,128)S(1)}, f32[16,2,16,128]{3,2,1,0:T(8,128)S(1)}, u32[]{:S(2)}, u32[]{:S(2)}) collective-permute-start(f32[16,2,16,128]{3,2,1,0:T(8,128)S(1)} %all_to_all.11), channel_id=1, source_target_pairs={{0,16},{16,0},{1,17},{17,1},{2,18},{18,2},{3,19},{19,3},{4,20},{20... | collective-permute-start | bytes 786440 | tf_op jit(solution)/shard_map/ppermute | solution.py:243
